TPU v7x, 256 devices: a whole 4x4x8 slice. The times are simulated.
256 devices in a mesh: section: 2 (over y_hi), seq: 32 (over x, z), chan: 4 (over y_lo, core).
Axes of the slice: x: 4, y: 4 (y_hi: 2, y_lo: 2; y = y_hi * 2 + y_lo), z: 8, core: 2. Of those that a mesh axis runs over, the one named last changes fastest.
Arguments:
- bases: int32 [2, 2097152], P('section', 'seq'), may hold values from 0 to 3
- stem_embedding_weight: bfloat16 [512, 1536], P(None, 'chan'), may hold values from -1.64443437 to 1.64443437
- gains: float32 [3, 1536], replicated, may hold values from 0.1 to 1.9
- conv_weight: bfloat16 [3, 3, 1536, 1536], P(None, None, None, 'chan'), may hold values from -0.09375 to 0.09375
- dec_weight: bfloat16 [1536, 384], P('chan'), may hold values from -0.3125 to 0.3125
- upstream: bfloat16 [2, 16384, 1536], P('section', 'seq', 'chan'), may hold values from -0.032958984 to 0.032958984
Outputs:
- decoded: bfloat16 [2, 16384, 1536], P('section', 'seq', 'chan')
- weight_grad: float32 [1536, 384], P('chan')
All inputs are finite; a program needn't handle non-finite values.
Results may differ from a plain program's by a relative error of at most 0.0076.
Values may be sent and summed in bfloat16 or wider, within the bound.
No kernel may reach another device: no remote copies, remote signals or barrier semaphores. Data moves between devices by JAX's collectives and lax.ppermute only.
A program may use at most 128 MiB of HBM per device.

v0:
```python
import jax
import jax.numpy as jnp
from jax import lax
from jax.sharding import PartitionSpec as P

PATCH = 128
FIRST_DILATION0 = 2


EPSILON = 1e-06


def with_halo(shard, sides, width):
    for axis, dim in sides:
        size, length = (lax.axis_size(axis), shard.shape[dim])
        up = [(i, (i + 1) % size) for i in range(size - 1)]
        down = [(j, i) for i, j in up]
        last = lax.slice_in_dim(shard, length - width, length, axis=dim)
        initial = lax.slice_in_dim(shard, 0, width, axis=dim)
        before = lax.ppermute(last, axis, up)
        after = lax.ppermute(initial, axis, down)
        shard = jnp.concatenate([before, shard, after], axis=dim)
    return shard


def activate(rows, gain_row):
    widened = rows.astype(jnp.float32)
    inverse_rms = lax.rsqrt(jnp.mean(widened * widened, axis=-1, keepdims=True) + EPSILON)
    return jax.nn.gelu(widened * inverse_rms * gain_row).astype(jnp.bfloat16)


def apply_convolution(padded, kernel_taps, dilation_step, row_count):
    update = jnp.dot(padded[0:row_count], kernel_taps[0], preferred_element_type=jnp.float32)
    for offset in range(1, kernel_taps.shape[0]):
        start = offset * dilation_step
        update = update + jnp.dot(
            padded[start : start + row_count],
            kernel_taps[offset],
            preferred_element_type=jnp.float32,
        )
    return update


def body(bases, stem_embedding_weight, gains, conv_weight, dec_weight, upstream):
    row_count = upstream.shape[1]
    letters = bases.reshape(row_count, PATCH)
    onehot = letters[:, :, None] == jnp.arange(4, dtype=jnp.int32)[None, None, :]
    onehot = onehot.astype(jnp.bfloat16).reshape(row_count, PATCH * 4)
    stream = jnp.dot(onehot, stem_embedding_weight, preferred_element_type=jnp.float32).astype(
        jnp.bfloat16
    )
    for tower_layer_index in range(conv_weight.shape[0]):
        dilation_step = FIRST_DILATION0 * 2**tower_layer_index
        full_rows = lax.all_gather(stream, "chan", axis=1, tiled=True)
        padded = with_halo(
            activate(full_rows, gains[tower_layer_index]), (("seq", 0),), dilation_step
        )
        update = apply_convolution(padded, conv_weight[tower_layer_index], dilation_step, row_count)
        stream = (stream.astype(jnp.float32) + update).astype(jnp.bfloat16)
    decoded = jnp.dot(stream, dec_weight, preferred_element_type=jnp.float32).astype(jnp.bfloat16)
    upstream_rows = upstream[0]
    contract_row_pairs = (((0,), (0,)), ((), ()))
    partial_grad = lax.dot_general(
        stream, upstream_rows, contract_row_pairs, preferred_element_type=jnp.float32
    )
    weight_grad = lax.psum(partial_grad, ("section", "seq"))
    return (decoded[None], weight_grad)


def solution(mesh):
    placed = (
        P("section", "seq"),
        P(None, "chan"),
        P(),
        P(None, None, None, "chan"),
        P("chan", None),
        P("section", "seq", "chan"),
    )
    return jax.shard_map(
        body,
        mesh=mesh,
        in_specs=placed,
        out_specs=(P("section", "seq", "chan"), P("chan", None)),
        check_vma=False,
    )
```

profile of v0, /device:TPU:32, one launch (start us, length us, event | category | flops | bytes accessed | tf_op | source)
XLA Modules:
  0.0 812.0 jit_solution(4729358638135030658)
XLA Ops:
  7.2 0.0 copy-start
  7.2 0.0 all-gather.4.cloned.1.call-start
  7.2 0.1 eq.26
  7.4 1.1 copy.8
  8.4 0.2 eq.23
  8.6 0.4 eq.24
  9.0 1.3 convolution_convert_fusion.1
  10.3 0.0 all-gather.4.cloned.1.call-update
  10.4 0.0 all-gather.6.cloned.1.call-start
  10.4 0.1 slice_reduce_fusion
  10.5 29.9 %all-gather.4.cloned.1.call-done = bf16[512,1536]{1,0:T(8,128)(2,1)} async-done(((bf16[512,384]{1,0:T(8,128)(2,1)}), bf16[512,1536]{1,0:T(8,128)(2,1)}) %all-gather.4.cloned.1.call-update) | async-done | bytes 1572880 | tf_op jit(solution)/shard_map/all_gather | solution.py:54
  40.4 1.8 fusion
  42.2 2.8 fusion.4
  45.0 3.5 collective-permute-start
  48.5 2.4 collective-permute-start.1
  50.9 2.2 fusion.60
  53.1 0.0 copy-start.1
  53.1 0.9 collective-permute-done.1
  54.0 2.2 fusion.38
  56.3 3.0 fusion.49
  59.3 0.0 all-gather.6.cloned.1.call-update
  59.3 0.0 all-gather.8.cloned.1.call-start
  59.4 28.8 %all-gather.6.cloned.1.call-done = bf16[512,1536]{1,0:T(8,128)(2,1)} async-done(((bf16[512,384]{1,0:T(8,128)(2,1)}), bf16[512,1536]{1,0:T(8,128)(2,1)}) %all-gather.6.cloned.1.call-update) | async-done | bytes 1572880 | tf_op jit(solution)/shard_map/all_gather | solution.py:54
  88.2 1.8 fusion.9
  90.0 2.8 fusion.13
  92.8 2.4 collective-permute-start.3
  95.2 2.2 fusion.56
  97.4 0.0 copy-start.3
  97.5 3.6 collective-permute-start.2
  101.1 2.3 fusion.34
  103.3 3.0 add_convert_fusion.1
  106.4 0.0 all-gather.8.cloned.1.call-update
  106.4 0.0 all-reduce.2.cloned.1.call-start
  106.5 29.4 %all-gather.8.cloned.1.call-done = bf16[512,1536]{1,0:T(8,128)(2,1)} async-done(((bf16[512,384]{1,0:T(8,128)(2,1)}), bf16[512,1536]{1,0:T(8,128)(2,1)}) %all-gather.8.cloned.1.call-update) | async-done | bytes 1572880 | tf_op jit(solution)/shard_map/all_gather | solution.py:54
  135.9 1.8 fusion.18
  137.7 2.8 fusion.22
  140.5 2.6 collective-permute-start.5
  143.1 2.2 fusion.52
  145.3 0.0 copy-start.2
  145.3 3.6 collective-permute-start.4
  148.9 2.2 fusion.30
  151.2 0.0 copy-start.4
  151.2 2.3 add_convert_fusion
  153.6 1.2 fusion.74
  154.8 0.0 all-reduce.2.cloned.1.call-update
  154.9 1.1 fusion.50
  156.0 647.5 %all-reduce.2.cloned.1.call-done = f32[384,384]{1,0:T(8,128)} async-done(((f32[384,384]{1,0:T(8,128)}), f32[384,384]{1,0:T(8,128)}) %all-reduce.2.cloned.1.call-update) | async-done | bytes 589840 | tf_op jit(solution)/shard_map/psum | solution.py:66
  803.5 1.9 copy.10
  (21 shorter events, 0.1 us)
Async XLA Ops:
  7.2 1.8 copy-start
  7.2 3.2 copy-start.6
  7.2 33.2 %all-gather.4.cloned.1.call-start = ((), (), s32[]{:S(2)}) async-start(), calls=%async_computation | async-start | bytes 1966080 | tf_op jit(solution)/shard_map/all_gather | solution.py:54
  10.4 77.8 %all-gather.6.cloned.1.call-start = ((), (), s32[]{:S(2)}) async-start(), calls=%async_computation.1 | async-start | bytes 1966080 | tf_op jit(solution)/shard_map/all_gather | solution.py:54
  45.0 11.2 %collective-permute-start = (bf16[2,1536]{1,0:T(2,128)(2,1)S(1)}, bf16[2,1536]{1,0:T(2,128)(2,1)S(1)}, u32[]{:S(2)}, u32[]{:S(2)}) collective-permute-start(bf16[2,1536]{1,0:T(2,128)(2,1)S(1)} %get-tuple-element.9), channel_id=1, source_target_pairs={{0,4},{4,8},{8,12},{12,16},{16,20},{20,24},{24,28},{28,32},{32,36}... | collective-permute-start | bytes 18440 | tf_op jit(solution)/shard_map/ppermute | solution.py:20
  48.5 5.5 collective-permute-start.1
  53.1 3.2 copy-start.1
  59.3 76.5 %all-gather.8.cloned.1.call-start = ((), (), s32[]{:S(2)}) async-start(), calls=%async_computation.2 | async-start | bytes 1966080 | tf_op jit(solution)/shard_map/all_gather | solution.py:54
  92.8 8.3 %collective-permute-start.3 = (bf16[4,1536]{1,0:T(4,128)(2,1)S(1)}, bf16[4,1536]{1,0:T(4,128)(2,1)S(1)}, u32[]{:S(2)}, u32[]{:S(2)}) collective-permute-start(bf16[4,1536]{1,0:T(4,128)(2,1)S(1)} %get-tuple-element.8), channel_id=1, source_target_pairs={{4,0},{8,4},{12,8},{16,12},{20,16},{24,20},{28,24},{32,28},{36,32}... | collective-permute-start | bytes 36872 | tf_op jit(solution)/shard_map/ppermute | solution.py:21
  97.4 5.9 copy-start.3
  97.5 5.9 collective-permute-start.2
  106.4 697.1 %all-reduce.2.cloned.1.call-start = ((), (), s32[]{:S(2)}) async-start(), calls=%async_computation.3 | async-start | bytes 1179648 | tf_op jit(solution)/shard_map/psum | solution.py:66
  140.5 8.4 %collective-permute-start.5 = (bf16[8,1536]{1,0:T(8,128)(2,1)S(1)}, bf16[8,1536]{1,0:T(8,128)(2,1)S(1)}, u32[]{:S(2)}, u32[]{:S(2)}) collective-permute-start(bf16[8,1536]{1,0:T(8,128)(2,1)S(1)} %get-tuple-element.6), channel_id=1, source_target_pairs={{4,0},{8,4},{12,8},{16,12},{20,16},{24,20},{28,24},{32,28},{36,32}... | collective-permute-start | bytes 73736 | tf_op jit(solution)/shard_map/ppermute | solution.py:21
  145.3 5.9 copy-start.2
  145.3 5.9 collective-permute-start.4
  151.2 2.4 copy-start.4
  151.2 3.6 copy-start.5
Sparse Core Ops, SparseCore 0:
  10.5 29.8 all-gather.3
  59.5 28.6 all-gather.5
  106.5 29.3 all-gather.7
  155.0 648.5 all-reduce.1
where the time goes:
time: 815 us; the launch traced here: 812 us
  waiting for transfers between devices  737 us (90%)
  matrix products  25.6 us (3%)
  starting transfers between devices  18.1 us (2%)
  between operations  14.1 us (2%)
  other arithmetic  13.7 us (2%)
    psum x1, waiting for transfers between devices, body(): weight_grad = lax.psum(partial_grad, ('section', 'seq'))  648 us
    all_gather x3, waiting for transfers between devices, body(): full_rows = lax.all_gather(stream, 'chan', axis=1, tiled=True)  88.2 us
  transfers between devices with their start and end apart: 10, of which 5 were waited for; matrix products, arithmetic and copies ran while one was open for 2% of the time, Pallas kernels for 0%

commit v1 on v0

v1 whole, which is shorter than its diff:
```python
import functools

import jax
import jax.numpy as jnp
from jax import lax
from jax.experimental import pallas as pl
from jax.experimental.pallas import tpu as pltpu
from jax.sharding import PartitionSpec as P

PATCH = 128
FIRST_DILATION0 = 2
EPSILON = 1e-06
HALO = 16
PAD = 16

VMEM = pl.BlockSpec(memory_space=pltpu.VMEM)
SMEM = pl.BlockSpec(memory_space=pltpu.SMEM)
ANY = pl.BlockSpec(memory_space=pl.ANY)


def gelu(x):
    inner = x * (0.7978845608028654 + 0.035677408136300125 * (x * x))
    return (0.5 * x) * (1.0 + jnp.tanh(inner))


def norm_rows(ids, layer, pieces, gains_ref, normed, first, rows, width):
    wide = [p.astype(jnp.float32) for p in pieces]
    total = wide[0] * wide[0]
    for w in wide[1:]:
        total = total + w * w
    inverse = lax.rsqrt(jnp.sum(total, axis=-1, keepdims=True) * (1.0 / (4 * width)) + EPSILON)
    for k, w in enumerate(wide):
        value = gelu(w * inverse * gains_ref[layer, ids[0] ^ k])
        normed[pl.ds(PAD + first, rows), k * width : (k + 1) * width] = value.astype(jnp.bfloat16)


def in_sequence(ids, rows, bins, count):
    bin_at = lax.broadcasted_iota(jnp.int32, (rows, 1), 0) + (ids[1] * bins - HALO)
    return jnp.where((bin_at >= 0) & (bin_at < count), 1.0, 0.0)


def start_weights(ids, layer, w_hbm, w_vmem, sems, width):
    copies = []
    for t in range(3):
        for k in range(4):
            group = ids[0] ^ k
            copies.append(
                pltpu.make_async_copy(
                    w_hbm.at[layer, t, pl.ds(group * width, width), :],
                    w_vmem.at[t, pl.ds(k * width, width), :],
                    sems.at[t, k],
                )
            )
            copies[-1].start()
    return copies


def convolve(normed, w_vmem, first, rows, dilation):
    update = None
    for t in range(3):
        part = jnp.dot(
            normed[pl.ds(PAD + first + (t - 1) * dilation, rows), :],
            w_vmem[t],
            preferred_element_type=jnp.float32,
        )
        update = part if update is None else update + part
    return update


def clear_pads(normed, rows):
    zeros = jnp.zeros((PAD, normed.shape[1]), normed.dtype)
    normed[0:PAD, :] = zeros
    normed[PAD + rows : PAD + rows + PAD, :] = zeros


def first_layer(bins, count, ids, before, own, after, *refs):
    w_stem, (gains, w_hbm, out, normed, stream, w_vmem, sems) = refs[:6], refs[6:]
    width = out.shape[1]
    rows = bins + 2 * HALO
    copies = start_weights(ids, 0, w_hbm, w_vmem, sems, width)
    clear_pads(normed, rows)
    letters = jnp.concatenate([before[...], own[...], after[...]], axis=0)
    letters = letters.astype(jnp.float32).astype(jnp.bfloat16)
    lane = lax.broadcasted_iota(jnp.int32, (PATCH, 4 * PATCH), 1)
    row = lax.broadcasted_iota(jnp.int32, (PATCH, 4 * PATCH), 0)
    spread = jnp.where(lane // 4 == row, 1.0, 0.0).astype(jnp.bfloat16)
    repeated = jnp.dot(letters, spread, preferred_element_type=jnp.float32)
    base = (lax.broadcasted_iota(jnp.int32, (1, 4 * PATCH), 1) % 4).astype(jnp.float32)
    inside = in_sequence(ids, rows, bins, count)
    onehot = (jnp.where(repeated == base, 1.0, 0.0) * inside).astype(jnp.bfloat16)
    half = 2 * PATCH
    stream[:, 0:width] = jnp.dot(
        onehot, w_stem[0][...], preferred_element_type=jnp.float32
    ).astype(jnp.bfloat16)
    stream[:, width : 2 * width] = jnp.dot(
        onehot, w_stem[1][...], preferred_element_type=jnp.float32
    ).astype(jnp.bfloat16)
    for k in (2, 3):
        low, high = w_stem[2 * k - 2], w_stem[2 * k - 1]
        value = jnp.dot(onehot[:, :half], low[...], preferred_element_type=jnp.float32)
        value = value + jnp.dot(onehot[:, half:], high[...], preferred_element_type=jnp.float32)
        stream[:, k * width : (k + 1) * width] = value.astype(jnp.bfloat16)

    step = 32

    @pl.loop(0, rows // step)
    def _(i):
        first = pl.multiple_of(i * step, step)
        pieces = [stream[pl.ds(first, step), k * width : (k + 1) * width] for k in range(4)]
        norm_rows(ids, 0, pieces, gains, normed, first, step, width)

    for copy in copies:
        copy.wait()
    update = convolve(normed, w_vmem, 0, rows, FIRST_DILATION0)
    total = (stream[:, 0:width].astype(jnp.float32) + update) * inside
    out[...] = total.astype(jnp.bfloat16)


def middle_layer(bins, count, ids, s0, s1, s2, s3, gains, w_hbm, out, normed, w_vmem, sems):
    width = out.shape[1]
    rows = bins + 2 * HALO
    copies = start_weights(ids, 1, w_hbm, w_vmem, sems, width)
    clear_pads(normed, rows)
    step = 32

    @pl.loop(0, rows // step)
    def _(i):
        first = pl.multiple_of(i * step, step)
        pieces = [s[pl.ds(first, step), :] for s in (s0, s1, s2, s3)]
        norm_rows(ids, 1, pieces, gains, normed, first, step, width)

    for copy in copies:
        copy.wait()
    update = convolve(normed, w_vmem, 0, rows, 2 * FIRST_DILATION0)
    total = (s0[...].astype(jnp.float32) + update) * in_sequence(ids, rows, bins, count)
    out[...] = total.astype(jnp.bfloat16)


def last_layer(
    bins, ids, s0, s1, s2, s3, gains, w_hbm, upstream,
    out, g0, g1, g2, g3, normed, w_vmem, grad, sems,
):
    width = out.shape[1]
    rows = bins + 2 * HALO
    copies = start_weights(ids, 2, w_hbm, w_vmem, sems, width)
    step = 32

    @pl.loop(0, rows // step)
    def _(i):
        first = pl.multiple_of(i * step, step)
        pieces = [s[pl.ds(first, step), :] for s in (s0, s1, s2, s3)]
        norm_rows(ids, 2, pieces, gains, normed, first, step, width)

    for copy in copies:
        copy.wait()
    update = convolve(normed, w_vmem, HALO, bins, 4 * FIRST_DILATION0)
    total = (s0[HALO : HALO + bins, :].astype(jnp.float32) + update).astype(jnp.bfloat16)
    out[...] = total
    grad[...] = lax.dot_general(
        total, upstream[...], (((0,), (0,)), ((), ())), preferred_element_type=jnp.float32
    )
    quarter = width // 4
    g0[...] = grad[pl.ds(pl.multiple_of(ids[2] * quarter, 8), quarter), :]
    for k, g in ((1, g1), (2, g2), (3, g3)):
        at = pl.multiple_of((ids[2] ^ k) * quarter, 8)
        g[...] = grad[pl.ds(at, quarter), :].astype(jnp.bfloat16)


def assemble(ids, p0, p1, p2, p3, out):
    quarter = p0.shape[0]
    for k, p in enumerate((p0, p1, p2, p3)):
        at = pl.multiple_of((ids[2] ^ k) * quarter, 8)
        out[pl.ds(at, quarter), :] = p[...].astype(jnp.float32)


def pairs(size, partner):
    return [(i, partner(i)) for i in range(size)]


def body(zs, seq_count, bases, stem, gains, conv_weight, dec_weight, upstream):
    bins, width = upstream.shape[1], upstream.shape[2]
    rows = bins + 2 * HALO
    count = bins * seq_count
    seq, chan = lax.axis_index("seq"), lax.axis_index("chan")
    x, z = seq // zs, seq % zs
    x_half, z_half = ((x + 1) // 2) % 2, ((z + 1) // 2) % 2
    ids = jnp.stack([chan, seq, x_half * 2 + z_half]).astype(jnp.int32)

    across = functools.partial(lax.ppermute, axis_name="chan", perm=pairs(4, lambda i: i ^ 2))
    other_core = functools.partial(lax.ppermute, axis_name="chan", perm=pairs(4, lambda i: i ^ 1))
    far = functools.partial(
        lax.ppermute, axis_name=("section", "chan"), perm=pairs(8, lambda i: i ^ 6)
    )

    letters = bases.reshape(bins, PATCH)
    up = [(i, i + 1) for i in range(seq_count - 1)]
    down = [(j, i) for i, j in up]
    half = stem.shape[0] // 2
    w2a = across(stem[:half])
    w2b = far(stem[half:])
    w1 = other_core(stem)
    before = lax.ppermute(letters[bins - HALO :], "seq", up)
    after = lax.ppermute(letters[:HALO], "seq", down)
    w3a = other_core(w2a)
    w3b = other_core(w2b)

    gain_rows = gains.reshape(gains.shape[0], 4, 1, width)

    scratch = [
        pltpu.VMEM((rows + 2 * PAD, 4 * width), jnp.bfloat16),
    ]
    weights = [
        pltpu.VMEM((3, 4 * width, width), jnp.bfloat16),
        pltpu.SemaphoreType.DMA((3, 4)),
    ]
    params = pltpu.CompilerParams(vmem_limit_bytes=40 * 2**20)
    stream_shape = jax.ShapeDtypeStruct((rows, width), jnp.bfloat16)
    stream = pl.pallas_call(
        functools.partial(first_layer, bins, count),
        out_shape=stream_shape,
        in_specs=[SMEM] + [VMEM] * 10 + [ANY],
        out_specs=VMEM,
        scratch_shapes=scratch + [pltpu.VMEM((rows, 4 * width), jnp.bfloat16)] + weights,
        compiler_params=params,
        name="layer_zero",
    )(ids, before, letters, after, stem, w1, w2a, w2b, w3a, w3b, gain_rows, conv_weight)

    def gathered(own):
        remote = across(own)
        return own, other_core(own), remote, other_core(remote)

    stream = pl.pallas_call(
        functools.partial(middle_layer, bins, count),
        out_shape=stream_shape,
        in_specs=[SMEM] + [VMEM] * 5 + [ANY],
        out_specs=VMEM,
        scratch_shapes=scratch + weights,
        compiler_params=params,
        name="layer_one",
    )(ids, *gathered(stream), gain_rows, conv_weight)

    quarter = jax.ShapeDtypeStruct((width // 4, width), jnp.bfloat16)
    stream, g0, g1, g2, g3 = pl.pallas_call(
        functools.partial(last_layer, bins),
        out_shape=(
            jax.ShapeDtypeStruct((bins, width), jnp.bfloat16),
            jax.ShapeDtypeStruct((width // 4, width), jnp.float32),
            quarter,
            quarter,
            quarter,
        ),
        in_specs=[SMEM] + [VMEM] * 5 + [ANY, VMEM],
        out_specs=(VMEM,) * 5,
        scratch_shapes=scratch + weights[:1] + [pltpu.VMEM((width, width), jnp.float32)] + weights[1:],
        compiler_params=params,
        name="layer_two",
    )(ids, *gathered(stream), gain_rows, conv_weight, upstream[0])
    decoded = jnp.dot(stream, dec_weight, preferred_element_type=jnp.float32).astype(jnp.bfloat16)

    def over(fx, fz):
        def partner(i):
            return fx(i // zs) * zs + fz(i % zs)

        return functools.partial(lax.ppermute, axis_name="seq", perm=pairs(seq_count, partner))

    def same(i):
        return i

    def flip(i):
        return i ^ 1

    def xs_near(i):
        return 3 - i

    def zs_near(i):
        return (i + 1) % zs if i % 2 else (i - 1) % zs

    def zs_far(i):
        return {0: 3, 3: 0, 1: 6, 6: 1, 2: 5, 5: 2, 4: 7, 7: 4}[i]

    r2 = over(flip, same)(g2)
    r1 = over(same, flip)(g1)
    r3 = over(flip, flip)(g3)
    f32 = jnp.float32
    total = (g0 + r2.astype(f32)) + (r1.astype(f32) + r3.astype(f32))
    own = total.astype(jnp.bfloat16)
    rx = over(xs_near, same)(own)
    rz = over(same, zs_near)(own)
    rxz = over(xs_near, zs_near)(own)
    total = (own.astype(f32) + rx.astype(f32)) + (rz.astype(f32) + rxz.astype(f32))
    own = total.astype(jnp.bfloat16)
    other = lax.ppermute(own, "section", [(0, 1), (1, 0)])
    own = (own.astype(f32) + other.astype(f32)).astype(jnp.bfloat16)
    other = over(same, zs_far)(own)
    own = (own.astype(f32) + other.astype(f32)).astype(jnp.bfloat16)
    r2 = over(flip, same)(own)
    r1 = over(same, flip)(own)
    r3 = over(flip, flip)(own)
    weight_grad = pl.pallas_call(
        assemble,
        out_shape=jax.ShapeDtypeStruct((width, width), jnp.float32),
        in_specs=[SMEM] + [VMEM] * 4,
        out_specs=VMEM,
        name="assemble",
    )(ids, own, r1, r2, r3)
    return (decoded[None], weight_grad)


def solution(mesh):
    placed = (
        P("section", "seq"),
        P(None, "chan"),
        P(),
        P(None, None, None, "chan"),
        P("chan", None),
        P("section", "seq", "chan"),
    )
    seq_count = mesh.shape["seq"]
    return jax.shard_map(
        functools.partial(body, seq_count // 4, seq_count),
        mesh=mesh,
        in_specs=placed,
        out_specs=(P("section", "seq", "chan"), P("chan", None)),
        check_vma=False,
    )
```

time: 815 us -> 126 us (0.15)
  waiting for transfers between devices: 737 us -> 55.1 us
  Pallas kernels: 0 us -> 25.2 us
  matrix products: 25.6 us -> 1.14 us
  other arithmetic: 13.7 us -> 0.2 us
  between operations: 14.1 us -> 0.87 us
  starting transfers between devices: 18.1 us -> 28.3 us
  local copies, waits for them, and re-layouts: 3.78 us -> 13.2 us
    psum x1 -> x0, waiting for transfers between devices: 648 us -> none  [body(): weight_grad = lax.psum(partial_grad, ('section', 'seq'))]
    all_gather x3 -> x0, waiting for transfers between devices: 88.2 us -> none  [body(): full_rows = lax.all_gather(stream, 'chan', axis=1, tiled=True)]
    ppermute x6 -> x24, waiting for transfers between devices: 0.89 us -> 55.1 us  [the longest x2 21.9 us: gathered(): remote = across(own)]
    pallas_call x0 -> x4, Pallas kernels: none -> 25.2 us  [the longest x1 8.69 us: body(): pl.pallas_call(functools.partial(first_layer, bins, count), out_shape=str...]
    dot_general x11 -> x0, matrix products: 24.5 us -> none  [the longest x6 13.5 us: apply_convolution(): jnp.dot(padded[start:start + row_count], kernel_taps[offset], preferred_e...]
    ppermute x6 -> x24, starting transfers between devices: 18 us -> 28.3 us  [the longest x1 5.34 us: body(): rxz = over(xs_near, zs_near)(own)]
    unnamed x15 -> x22, local copies, waits for them, and re-layouts: 1.96 us -> 10.6 us
    convert_element_type x3 -> x4, other arithmetic: 8.35 us -> 0.13 us  [the longest x2 0.09 us: body(): own = total.astype(jnp.bfloat16)]
  transfers between devices with their start and end apart: 10 -> 24, of which waited for: 5 -> 18; matrix products, arithmetic and copies ran while one was open for 2% -> 2% of each run, Pallas kernels for 0% -> 0%
where the time goes in v1:
time: 126 us; the launch traced here: 124 us
  waiting for transfers between devices  55.1 us (44%)
  starting transfers between devices  28.3 us (22%)
  Pallas kernels  25.2 us (20%)
  local copies, waits for them, and re-layouts  13.2 us (10%)
    ppermute x2, waiting for transfers between devices, gathered(): remote = across(own)  21.9 us
    unnamed x22, local copies, waits for them, and re-layouts  10.6 us
    pallas_call x1, Pallas kernels, body(): pl.pallas_call(functools.partial(first_layer, bins, count), out_shape=str...  8.69 us
    pallas_call x1, Pallas kernels, body(): pl.pallas_call(functools.partial(last_layer, bins), out_shape=(jax.ShapeD...  7.43 us
    pallas_call x1, Pallas kernels, body(): pl.pallas_call(functools.partial(middle_layer, bins, count), out_shape=st...  7.24 us
    ppermute x1, starting transfers between devices, body(): rxz = over(xs_near, zs_near)(own)  5.34 us
    ppermute x1, waiting for transfers between devices, body(): w2b = far(stem[half:])  4.76 us
    ppermute x1, waiting for transfers between devices, body(): other = lax.ppermute(own, 'section', [(0, 1), (1, 0)])  4.64 us
  transfers between devices with their start and end apart: 24, of which 18 were waited for; matrix products, arithmetic and copies ran while one was open for 2% of the time, Pallas kernels for 0%

profile of v1, /device:TPU:32, one launch (start us, length us, event | category | flops | bytes accessed | tf_op | source)
XLA Modules:
  0.0 124.0 jit_solution(11223312571846246967)
XLA Ops:
  0.6 0.0 copy-start
  0.6 1.1 fusion.1
  1.8 3.1 %collective-permute-start.4 = (bf16[256,384]{1,0:T(8,128)(2,1)S(1)}, bf16[256,384]{1,0:T(8,128)(2,1)S(1)}, u32[]{:S(2)}, u32[]{:S(2)}) collective-permute-start(bf16[256,384]{1,0:T(8,128)(2,1)S(1)} %get-tuple-element.12), channel_id=1, source_target_pairs={{0,130},{1,131},{2,128},{3,129},{128,2},{129,3},{130,0},{131,1},{4... | collective-permute-start | bytes 589832 | tf_op jit(solution)/shard_map/ppermute | solution.py:200
  4.9 0.1 collective-permute-start.3
  5.0 4.8 %collective-permute-done.4.refs_3_ = bf16[256,384]{1,0:T(8,128)(2,1)S(1)} collective-permute-done((bf16[256,384]{1,0:T(8,128)(2,1)S(1)}, bf16[256,384]{1,0:T(8,128)(2,1)S(1)}, u32[]{:S(2)}, u32[]{:S(2)}) %collective-permute-start.4) | collective-permute-done | bytes 196640 | tf_op jit(solution)/shard_map/ppermute | solution.py:200
  9.8 1.5 %collective-permute-done.3.refs_2_ = bf16[256,384]{1,0:T(8,128)(2,1)S(1)} collective-permute-done((bf16[256,384]{1,0:T(8,128)(2,1)S(1)}, bf16[256,384]{1,0:T(8,128)(2,1)S(1)}, u32[]{:S(2)}, u32[]{:S(2)}) %collective-permute-start.3) | collective-permute-done | bytes 196640 | tf_op jit(solution)/shard_map/ppermute | solution.py:199
  11.2 0.7 fusion.2
  11.9 3.8 %collective-permute-start = (s32[16,128]{1,0:T(8,128)S(1)}, s32[16,128]{1,0:T(8,128)S(1)}, u32[]{:S(2)}, u32[]{:S(2)}) collective-permute-start(s32[16,128]{1,0:T(8,128)S(1)} %bitcast.14), channel_id=1, source_target_pairs={{0,4},{4,8},{8,12},{12,16},{16,20},{20,24},{24,28},{28,32},{32,36}... | collective-permute-start | bytes 24584 | tf_op jit(solution)/shard_map/ppermute | solution.py:202
  15.8 2.0 %collective-permute-start.1 = (s32[16,128]{1,0:T(8,128)S(1)}, s32[16,128]{1,0:T(8,128)S(1)}, u32[]{:S(2)}, u32[]{:S(2)}) collective-permute-start(s32[16,128]{1,0:T(8,128)S(1)} %bitcast.13), channel_id=1, source_target_pairs={{4,0},{8,4},{12,8},{16,12},{20,16},{24,20},{28,24},{32,28},{36,32}... | collective-permute-start | bytes 24584 | tf_op jit(solution)/shard_map/ppermute | solution.py:203
  17.9 0.1 pad_add_fusion.ids
  18.0 0.8 reshape.13.refs_6_.gains
  18.7 2.6 %collective-permute-done.1.after = s32[16,128]{1,0:T(8,128)S(1)} collective-permute-done((s32[16,128]{1,0:T(8,128)S(1)}, s32[16,128]{1,0:T(8,128)S(1)}, u32[]{:S(2)}, u32[]{:S(2)}) %collective-permute-start.1) | collective-permute-done | bytes 8224 | tf_op jit(solution)/shard_map/ppermute | solution.py:203
  21.3 4.0 %copy-done.1 = bf16[3,3,1536,384]{3,2,1,0:T(8,128)(2,1)S(1)} copy-done((bf16[3,3,1536,384]{3,2,1,0:T(8,128)(2,1)S(1)}, bf16[3,3,1536,384]{3,2,1,0:T(8,128)(2,1)}, u32[]{:S(2)}) %copy-start.1) | copy-done | bytes 10616856
  25.3 1.0 copy-done.3
  26.3 0.9 copy-done.5
  27.3 8.7 %layer_zero.1.s0 = bf16[544,384]{1,0:T(8,128)(2,1)S(1)} custom-call(s32[3]{0:T(128)S(1)} %pad_add_fusion.ids, s32[16,128]{1,0:T(8,128)S(1)} %collective-permute-done.before, s32[512,128]{1,0:T(8,128)S(1)} %bitcast.12, s32[16,128]{1,0:T(8,128)S(1)} %collective-permute-done.1.after, bf16[512,384]{1,0:T(8,128)(2,1)S(1)} %copy-done.3, ...), custom_call_target="tpu_custom_call" | custom-call | tf_op jit(solution)/shard_map/layer_zero/pallas_call | solution.py:218
  36.0 0.4 collective-permute-start.8
  36.4 10.5 %collective-permute-done.8.s2 = bf16[544,384]{1,0:T(8,128)(2,1)S(1)} collective-permute-done((bf16[544,384]{1,0:T(8,128)(2,1)S(1)}, bf16[544,384]{1,0:T(8,128)(2,1)S(1)}, u32[]{:S(2)}, u32[]{:S(2)}) %collective-permute-start.8) | collective-permute-done | bytes 417824 | tf_op jit(solution)/shard_map/ppermute | solution.py:229
  46.9 1.8 %collective-permute-done.9.s3 = bf16[544,384]{1,0:T(8,128)(2,1)S(1)} collective-permute-done((bf16[544,384]{1,0:T(8,128)(2,1)S(1)}, bf16[544,384]{1,0:T(8,128)(2,1)S(1)}, u32[]{:S(2)}, u32[]{:S(2)}) %collective-permute-start.9) | collective-permute-done | bytes 417824 | tf_op jit(solution)/shard_map/ppermute | solution.py:230
  48.6 4.0 %copy-done.2 = bf16[3,3,1536,384]{3,2,1,0:T(8,128)(2,1)S(1)} copy-done((bf16[3,3,1536,384]{3,2,1,0:T(8,128)(2,1)S(1)}, bf16[3,3,1536,384]{3,2,1,0:T(8,128)(2,1)}, u32[]{:S(2)}) %copy-start.2) | copy-done | bytes 10616856
  52.7 7.2 %layer_one.1.s0 = bf16[544,384]{1,0:T(8,128)(2,1)S(1)} custom-call(s32[3]{0:T(128)S(1)} %pad_add_fusion.ids, bf16[544,384]{1,0:T(8,128)(2,1)S(1)} %layer_zero.1.s0, bf16[544,384]{1,0:T(8,128)(2,1)S(1)} %collective-permute-done.7.s1, bf16[544,384]{1,0:T(8,128)(2,1)S(1)} %collective-permute-done.8.s2, bf16[544,384]{1,0:T(8,128)(2,1)S(1)} %collective-permute-done.9.s3, ...), custom_call_target="tpu_custom_call" | custom-call | tf_op jit(solution)/shard_map/layer_one/pallas_call | solution.py:232
  59.9 0.4 collective-permute-start.11
  60.3 11.4 %collective-permute-done.11.s2 = bf16[544,384]{1,0:T(8,128)(2,1)S(1)} collective-permute-done((bf16[544,384]{1,0:T(8,128)(2,1)S(1)}, bf16[544,384]{1,0:T(8,128)(2,1)S(1)}, u32[]{:S(2)}, u32[]{:S(2)}) %collective-permute-start.11) | collective-permute-done | bytes 417824 | tf_op jit(solution)/shard_map/ppermute | solution.py:229
  71.7 1.8 %collective-permute-done.12.s3 = bf16[544,384]{1,0:T(8,128)(2,1)S(1)} collective-permute-done((bf16[544,384]{1,0:T(8,128)(2,1)S(1)}, bf16[544,384]{1,0:T(8,128)(2,1)S(1)}, u32[]{:S(2)}, u32[]{:S(2)}) %collective-permute-start.12) | collective-permute-done | bytes 417824 | tf_op jit(solution)/shard_map/ppermute | solution.py:230
  73.4 7.4 %layer_two.1 = (bf16[512,384]{1,0:T(8,128)(2,1)S(1)}, f32[96,384]{1,0:T(8,128)S(1)}, bf16[96,384]{1,0:T(8,128)(2,1)S(1)}, bf16[96,384]{1,0:T(8,128)(2,1)S(1)}, bf16[96,384]{1,0:T(8,128)(2,1)S(1)}) custom-call(s32[3]{0:T(128)S(1)} %pad_add_fusion.ids, bf16[544,384]{1,0:T(8,128)(2,1)S(1)} %layer_one.1.s0, bf16[544,384]{1,0:T(8,128)(2,1)S(1)} %collective-permute-done.10.s1, ...), custom_call_target="tpu_custom_call" | custom-call | tf_op jit(solution)/shard_map/layer_two/pallas_call | solution.py:243
  80.9 1.6 %collective-permute-start.13 = (bf16[96,384]{1,0:T(8,128)(2,1)S(1)}, bf16[96,384]{1,0:T(8,128)(2,1)S(1)}, u32[]{:S(2)}, u32[]{:S(2)}) collective-permute-start(bf16[96,384]{1,0:T(8,128)(2,1)S(1)} %get-tuple-element.9), channel_id=1, source_target_pairs={{0,32},{4,36},{8,40},{12,44},{16,48},{20,52},{24,56},{28,60},{32,0... | collective-permute-start | bytes 221192 | tf_op jit(solution)/shard_map/ppermute | solution.py:281
  82.5 2.4 %collective-permute-start.14 = (bf16[96,384]{1,0:T(8,128)(2,1)S(1)}, bf16[96,384]{1,0:T(8,128)(2,1)S(1)}, u32[]{:S(2)}, u32[]{:S(2)}) collective-permute-start(bf16[96,384]{1,0:T(8,128)(2,1)S(1)} %get-tuple-element.10), channel_id=1, source_target_pairs={{0,4},{4,0},{8,12},{12,8},{16,20},{20,16},{24,28},{28,24},{32,36},... | collective-permute-start | bytes 221192 | tf_op jit(solution)/shard_map/ppermute | solution.py:282
  84.8 0.5 collective-permute-done.13
  85.3 2.2 %collective-permute-done.14 = bf16[96,384]{1,0:T(8,128)(2,1)S(1)} collective-permute-done((bf16[96,384]{1,0:T(8,128)(2,1)S(1)}, bf16[96,384]{1,0:T(8,128)(2,1)S(1)}, u32[]{:S(2)}, u32[]{:S(2)}) %collective-permute-start.14) | collective-permute-done | bytes 73760 | tf_op jit(solution)/shard_map/ppermute | solution.py:282
  87.6 2.5 %collective-permute-done.15 = bf16[96,384]{1,0:T(8,128)(2,1)S(1)} collective-permute-done((bf16[96,384]{1,0:T(8,128)(2,1)S(1)}, bf16[96,384]{1,0:T(8,128)(2,1)S(1)}, u32[]{:S(2)}, u32[]{:S(2)}) %collective-permute-start.15) | collective-permute-done | bytes 73760 | tf_op jit(solution)/shard_map/ppermute | solution.py:283
  90.1 5.3 %collective-permute-start.18 = (bf16[96,384]{1,0:T(8,128)(2,1)S(1)}, bf16[96,384]{1,0:T(8,128)(2,1)S(1)}, u32[]{:S(2)}, u32[]{:S(2)}) collective-permute-start(bf16[96,384]{1,0:T(8,128)(2,1)S(1)} %add_convert_fusion.3), channel_id=1, source_target_pairs={{0,124},{4,104},{8,100},{12,112},{16,108},{20,120},{24,116},{28,96... | collective-permute-start | bytes 221192 | tf_op jit(solution)/shard_map/ppermute | solution.py:289
  95.5 1.1 collective-permute-start.16
  96.6 1.9 %collective-permute-done.18 = bf16[96,384]{1,0:T(8,128)(2,1)S(1)} collective-permute-done((bf16[96,384]{1,0:T(8,128)(2,1)S(1)}, bf16[96,384]{1,0:T(8,128)(2,1)S(1)}, u32[]{:S(2)}, u32[]{:S(2)}) %collective-permute-start.18) | collective-permute-done | bytes 73760 | tf_op jit(solution)/shard_map/ppermute | solution.py:289
  98.5 1.4 %collective-permute-done.17 = bf16[96,384]{1,0:T(8,128)(2,1)S(1)} collective-permute-done((bf16[96,384]{1,0:T(8,128)(2,1)S(1)}, bf16[96,384]{1,0:T(8,128)(2,1)S(1)}, u32[]{:S(2)}, u32[]{:S(2)}) %collective-permute-start.17) | collective-permute-done | bytes 73760 | tf_op jit(solution)/shard_map/ppermute | solution.py:288
  99.8 1.2 collective-permute-done.16
  101.1 1.3 %collective-permute-start.19 = (bf16[96,384]{1,0:T(8,128)(2,1)S(1)}, bf16[96,384]{1,0:T(8,128)(2,1)S(1)}, u32[]{:S(2)}, u32[]{:S(2)}) collective-permute-start(bf16[96,384]{1,0:T(8,128)(2,1)S(1)} %add_convert_fusion.2), channel_id=1, source_target_pairs={{0,128},{128,0},{1,129},{129,1},{2,130},{130,2},{3,131},{131,3},{4... | collective-permute-start | bytes 221192 | tf_op jit(solution)/shard_map/ppermute | solution.py:292
  102.4 4.6 %collective-permute-done.19 = bf16[96,384]{1,0:T(8,128)(2,1)S(1)} collective-permute-done((bf16[96,384]{1,0:T(8,128)(2,1)S(1)}, bf16[96,384]{1,0:T(8,128)(2,1)S(1)}, u32[]{:S(2)}, u32[]{:S(2)}) %collective-permute-start.19) | collective-permute-done | bytes 73760 | tf_op jit(solution)/shard_map/ppermute | solution.py:292
  107.0 3.2 %collective-permute-start.20 = (bf16[96,384]{1,0:T(8,128)(2,1)S(1)}, bf16[96,384]{1,0:T(8,128)(2,1)S(1)}, u32[]{:S(2)}, u32[]{:S(2)}) collective-permute-start(bf16[96,384]{1,0:T(8,128)(2,1)S(1)} %add_convert_fusion.1), channel_id=1, source_target_pairs={{0,12},{4,24},{8,20},{12,0},{16,28},{20,8},{24,4},{28,16},{32,44},... | collective-permute-start | bytes 221192 | tf_op jit(solution)/shard_map/ppermute | solution.py:294
  110.2 4.3 %collective-permute-done.20 = bf16[96,384]{1,0:T(8,128)(2,1)S(1)} collective-permute-done((bf16[96,384]{1,0:T(8,128)(2,1)S(1)}, bf16[96,384]{1,0:T(8,128)(2,1)S(1)}, u32[]{:S(2)}, u32[]{:S(2)}) %collective-permute-start.20) | collective-permute-done | bytes 73760 | tf_op jit(solution)/shard_map/ppermute | solution.py:294
  114.6 0.1 collective-permute-start.23
  114.7 2.5 %collective-permute-start.22 = (bf16[96,384]{1,0:T(8,128)(2,1)S(1)}, bf16[96,384]{1,0:T(8,128)(2,1)S(1)}, u32[]{:S(2)}, u32[]{:S(2)}) collective-permute-start(bf16[96,384]{1,0:T(8,128)(2,1)S(1)} %add_convert_fusion.p0), channel_id=1, source_target_pairs={{0,32},{4,36},{8,40},{12,44},{16,48},{20,52},{24,56},{28,60},{32,0... | collective-permute-start | bytes 221192 | tf_op jit(solution)/shard_map/ppermute | solution.py:296
  117.2 1.0 collective-permute-start.21
  118.2 1.1 fusion
  119.3 0.7 collective-permute-done.23.p3
  120.0 0.2 collective-permute-done.22.p2
  120.3 1.2 collective-permute-done.21.p1
  121.5 0.6 copy-done.10
  122.2 1.9 %assemble.1 = f32[384,384]{1,0:T(8,128)} custom-call(s32[3]{0:T(128)} %copy-done.6, bf16[96,384]{1,0:T(8,128)(2,1)} %copy-done.7, bf16[96,384]{1,0:T(8,128)(2,1)} %copy-done.10, bf16[96,384]{1,0:T(8,128)(2,1)} %copy-done.9, bf16[96,384]{1,0:T(8,128)(2,1)} %copy-done.8), custom_call_target="tpu_custom_call" | custom-call | tf_op jit(solution)/shard_map/assemble/pallas_call | solution.py:299
  (35 shorter events, 0.2 us)
Async XLA Ops:
  0.6 117.5 %copy-start = (bf16[384,384]{1,0:T(8,128)(2,1)S(1)}, bf16[384,384]{1,0:T(8,128)(2,1)}, u32[]{:S(2)}) copy-start(bf16[384,384]{1,0:T(8,128)(2,1)} %param.10) | copy-start | bytes 884740
  1.8 8.0 %collective-permute-start.4 = (bf16[256,384]{1,0:T(8,128)(2,1)S(1)}, bf16[256,384]{1,0:T(8,128)(2,1)S(1)}, u32[]{:S(2)}, u32[]{:S(2)}) collective-permute-start(bf16[256,384]{1,0:T(8,128)(2,1)S(1)} %get-tuple-element.12), channel_id=1, source_target_pairs={{0,130},{1,131},{2,128},{3,129},{128,2},{129,3},{130,0},{131,1},{4... | collective-permute-start | bytes 589832 | tf_op jit(solution)/shard_map/ppermute | solution.py:200
  4.9 6.4 %collective-permute-start.3 = (bf16[256,384]{1,0:T(8,128)(2,1)S(1)}, bf16[256,384]{1,0:T(8,128)(2,1)S(1)}, u32[]{:S(2)}, u32[]{:S(2)}) collective-permute-start(bf16[256,384]{1,0:T(8,128)(2,1)S(1)} %get-tuple-element.13), channel_id=1, source_target_pairs={{0,2},{1,3},{2,0},{3,1},{4,6},{5,7},{6,4},{7,5},{8,10},{9,11},{10,... | collective-permute-start | bytes 589832 | tf_op jit(solution)/shard_map/ppermute | solution.py:199
  5.0 16.3 %collective-permute-start.2 = (bf16[512,384]{1,0:T(8,128)(2,1)}, bf16[512,384]{1,0:T(8,128)(2,1)S(1)}, u32[]{:S(2)}, u32[]{:S(2)}) collective-permute-start(bf16[512,384]{1,0:T(8,128)(2,1)} %refs_0_.1), channel_id=1, source_target_pairs={{0,1},{1,0},{2,3},{3,2},{4,5},{5,4},{6,7},{7,6},{8,9},{9,8},{10,11... | collective-permute-start | bytes 1179656 | tf_op jit(solution)/shard_map/ppermute | solution.py:201
  9.8 11.6 %collective-permute-start.6 = (bf16[256,384]{1,0:T(8,128)(2,1)S(1)}, bf16[256,384]{1,0:T(8,128)(2,1)S(1)}, u32[]{:S(2)}, u32[]{:S(2)}) collective-permute-start(bf16[256,384]{1,0:T(8,128)(2,1)S(1)} %collective-permute-done.4.refs_3_), channel_id=1, source_target_pairs={{0,1},{1,0},{2,3},{3,2},{4,5},{5,4},{6,7},{7,6},{8,9},{9,8},{10,11... | collective-permute-start | bytes 589832 | tf_op jit(solution)/shard_map/ppermute | solution.py:205
  11.2 10.1 %collective-permute-start.5 = (bf16[256,384]{1,0:T(8,128)(2,1)S(1)}, bf16[256,384]{1,0:T(8,128)(2,1)S(1)}, u32[]{:S(2)}, u32[]{:S(2)}) collective-permute-start(bf16[256,384]{1,0:T(8,128)(2,1)S(1)} %collective-permute-done.3.refs_2_), channel_id=1, source_target_pairs={{0,1},{1,0},{2,3},{3,2},{4,5},{5,4},{6,7},{7,6},{8,9},{9,8},{10,11... | collective-permute-start | bytes 589832 | tf_op jit(solution)/shard_map/ppermute | solution.py:204
  11.9 6.8 %collective-permute-start = (s32[16,128]{1,0:T(8,128)S(1)}, s32[16,128]{1,0:T(8,128)S(1)}, u32[]{:S(2)}, u32[]{:S(2)}) collective-permute-start(s32[16,128]{1,0:T(8,128)S(1)} %bitcast.14), channel_id=1, source_target_pairs={{0,4},{4,8},{8,12},{12,16},{16,20},{20,24},{24,28},{28,32},{32,36}... | collective-permute-start | bytes 24584 | tf_op jit(solution)/shard_map/ppermute | solution.py:202
  15.8 5.5 %collective-permute-start.1 = (s32[16,128]{1,0:T(8,128)S(1)}, s32[16,128]{1,0:T(8,128)S(1)}, u32[]{:S(2)}, u32[]{:S(2)}) collective-permute-start(s32[16,128]{1,0:T(8,128)S(1)} %bitcast.13), channel_id=1, source_target_pairs={{4,0},{8,4},{12,8},{16,12},{20,16},{24,20},{28,24},{32,28},{36,32}... | collective-permute-start | bytes 24584 | tf_op jit(solution)/shard_map/ppermute | solution.py:203
  18.0 55.5 %copy-start.6 = (s32[3]{0:T(128)}, s32[3]{0:T(128)S(1)}, u32[]{:S(2)}) copy-start(s32[3]{0:T(128)S(1)} %pad_add_fusion.ids) | copy-start | bytes 40
  21.3 4.0 %copy-start.1 = (bf16[3,3,1536,384]{3,2,1,0:T(8,128)(2,1)S(1)}, bf16[3,3,1536,384]{3,2,1,0:T(8,128)(2,1)}, u32[]{:S(2)}) copy-start(bf16[3,3,1536,384]{3,2,1,0:T(8,128)(2,1)} %w_hbm.3) | copy-start | bytes 31850500
  25.3 1.0 copy-start.3
  26.3 0.9 copy-start.5
  27.3 46.2 %copy-start.4 = (bf16[1,512,384]{2,1,0:T(8,128)(2,1)S(1)}, bf16[1,512,384]{2,1,0:T(8,128)(2,1)}, u32[]{:S(2)}) copy-start(bf16[1,512,384]{2,1,0:T(8,128)(2,1)} %param.11) | copy-start | bytes 1179652
  36.0 10.9 %collective-permute-start.8 = (bf16[544,384]{1,0:T(8,128)(2,1)S(1)}, bf16[544,384]{1,0:T(8,128)(2,1)S(1)}, u32[]{:S(2)}, u32[]{:S(2)}) collective-permute-start(bf16[544,384]{1,0:T(8,128)(2,1)S(1)} %layer_zero.1.s0), channel_id=1, source_target_pairs={{0,2},{1,3},{2,0},{3,1},{4,6},{5,7},{6,4},{7,5},{8,10},{9,11},{10,... | collective-permute-start | bytes 1253384 | tf_op jit(solution)/shard_map/ppermute | solution.py:229
  36.4 10.5 %collective-permute-start.7 = (bf16[544,384]{1,0:T(8,128)(2,1)S(1)}, bf16[544,384]{1,0:T(8,128)(2,1)S(1)}, u32[]{:S(2)}, u32[]{:S(2)}) collective-permute-start(bf16[544,384]{1,0:T(8,128)(2,1)S(1)} %layer_zero.1.s0), channel_id=1, source_target_pairs={{0,1},{1,0},{2,3},{3,2},{4,5},{5,4},{6,7},{7,6},{8,9},{9,8},{10,11... | collective-permute-start | bytes 1253384 | tf_op jit(solution)/shard_map/ppermute | solution.py:230
  46.9 1.8 %collective-permute-start.9 = (bf16[544,384]{1,0:T(8,128)(2,1)S(1)}, bf16[544,384]{1,0:T(8,128)(2,1)S(1)}, u32[]{:S(2)}, u32[]{:S(2)}) collective-permute-start(bf16[544,384]{1,0:T(8,128)(2,1)S(1)} %collective-permute-done.8.s2), channel_id=1, source_target_pairs={{0,1},{1,0},{2,3},{3,2},{4,5},{5,4},{6,7},{7,6},{8,9},{9,8},{10,11... | collective-permute-start | bytes 1253384 | tf_op jit(solution)/shard_map/ppermute | solution.py:230
  48.6 4.0 %copy-start.2 = (bf16[3,3,1536,384]{3,2,1,0:T(8,128)(2,1)S(1)}, bf16[3,3,1536,384]{3,2,1,0:T(8,128)(2,1)}, u32[]{:S(2)}) copy-start(bf16[3,3,1536,384]{3,2,1,0:T(8,128)(2,1)} %w_hbm.3) | copy-start | bytes 31850500
  59.9 11.8 %collective-permute-start.11 = (bf16[544,384]{1,0:T(8,128)(2,1)S(1)}, bf16[544,384]{1,0:T(8,128)(2,1)S(1)}, u32[]{:S(2)}, u32[]{:S(2)}) collective-permute-start(bf16[544,384]{1,0:T(8,128)(2,1)S(1)} %layer_one.1.s0), channel_id=1, source_target_pairs={{0,2},{1,3},{2,0},{3,1},{4,6},{5,7},{6,4},{7,5},{8,10},{9,11},{10,... | collective-permute-start | bytes 1253384 | tf_op jit(solution)/shard_map/ppermute | solution.py:229
  60.3 11.4 %collective-permute-start.10 = (bf16[544,384]{1,0:T(8,128)(2,1)S(1)}, bf16[544,384]{1,0:T(8,128)(2,1)S(1)}, u32[]{:S(2)}, u32[]{:S(2)}) collective-permute-start(bf16[544,384]{1,0:T(8,128)(2,1)S(1)} %layer_one.1.s0), channel_id=1, source_target_pairs={{0,1},{1,0},{2,3},{3,2},{4,5},{5,4},{6,7},{7,6},{8,9},{9,8},{10,11... | collective-permute-start | bytes 1253384 | tf_op jit(solution)/shard_map/ppermute | solution.py:230
  71.7 1.8 %collective-permute-start.12 = (bf16[544,384]{1,0:T(8,128)(2,1)S(1)}, bf16[544,384]{1,0:T(8,128)(2,1)S(1)}, u32[]{:S(2)}, u32[]{:S(2)}) collective-permute-start(bf16[544,384]{1,0:T(8,128)(2,1)S(1)} %collective-permute-done.11.s2), channel_id=1, source_target_pairs={{0,1},{1,0},{2,3},{3,2},{4,5},{5,4},{6,7},{7,6},{8,9},{9,8},{10,11... | collective-permute-start | bytes 1253384 | tf_op jit(solution)/shard_map/ppermute | solution.py:230
  80.9 4.4 %collective-permute-start.13 = (bf16[96,384]{1,0:T(8,128)(2,1)S(1)}, bf16[96,384]{1,0:T(8,128)(2,1)S(1)}, u32[]{:S(2)}, u32[]{:S(2)}) collective-permute-start(bf16[96,384]{1,0:T(8,128)(2,1)S(1)} %get-tuple-element.9), channel_id=1, source_target_pairs={{0,32},{4,36},{8,40},{12,44},{16,48},{20,52},{24,56},{28,60},{32,0... | collective-permute-start | bytes 221192 | tf_op jit(solution)/shard_map/ppermute | solution.py:281
  82.5 5.1 %collective-permute-start.14 = (bf16[96,384]{1,0:T(8,128)(2,1)S(1)}, bf16[96,384]{1,0:T(8,128)(2,1)S(1)}, u32[]{:S(2)}, u32[]{:S(2)}) collective-permute-start(bf16[96,384]{1,0:T(8,128)(2,1)S(1)} %get-tuple-element.10), channel_id=1, source_target_pairs={{0,4},{4,0},{8,12},{12,8},{16,20},{20,16},{24,28},{28,24},{32,36},... | collective-permute-start | bytes 221192 | tf_op jit(solution)/shard_map/ppermute | solution.py:282
  84.8 5.3 %collective-permute-start.15 = (bf16[96,384]{1,0:T(8,128)(2,1)S(1)}, bf16[96,384]{1,0:T(8,128)(2,1)S(1)}, u32[]{:S(2)}, u32[]{:S(2)}) collective-permute-start(bf16[96,384]{1,0:T(8,128)(2,1)S(1)} %get-tuple-element.11), channel_id=1, source_target_pairs={{0,36},{4,32},{8,44},{12,40},{16,52},{20,48},{24,60},{28,56},{32,4... | collective-permute-start | bytes 221192 | tf_op jit(solution)/shard_map/ppermute | solution.py:283
  90.1 8.3 %collective-permute-start.18 = (bf16[96,384]{1,0:T(8,128)(2,1)S(1)}, bf16[96,384]{1,0:T(8,128)(2,1)S(1)}, u32[]{:S(2)}, u32[]{:S(2)}) collective-permute-start(bf16[96,384]{1,0:T(8,128)(2,1)S(1)} %add_convert_fusion.3), channel_id=1, source_target_pairs={{0,124},{4,104},{8,100},{12,112},{16,108},{20,120},{24,116},{28,96... | collective-permute-start | bytes 221192 | tf_op jit(solution)/shard_map/ppermute | solution.py:289
  95.5 4.4 %collective-permute-start.17 = (bf16[96,384]{1,0:T(8,128)(2,1)S(1)}, bf16[96,384]{1,0:T(8,128)(2,1)S(1)}, u32[]{:S(2)}, u32[]{:S(2)}) collective-permute-start(bf16[96,384]{1,0:T(8,128)(2,1)S(1)} %add_convert_fusion.3), channel_id=1, source_target_pairs={{0,28},{4,8},{8,4},{12,16},{16,12},{20,24},{24,20},{28,0},{32,60},... | collective-permute-start | bytes 221192 | tf_op jit(solution)/shard_map/ppermute | solution.py:288
  95.5 5.6 %collective-permute-start.16 = (bf16[96,384]{1,0:T(8,128)(2,1)S(1)}, bf16[96,384]{1,0:T(8,128)(2,1)S(1)}, u32[]{:S(2)}, u32[]{:S(2)}) collective-permute-start(bf16[96,384]{1,0:T(8,128)(2,1)S(1)} %add_convert_fusion.3), channel_id=1, source_target_pairs={{0,96},{4,100},{8,104},{12,108},{16,112},{20,116},{24,120},{28,124... | collective-permute-start | bytes 221192 | tf_op jit(solution)/shard_map/ppermute | solution.py:287
  101.1 5.9 %collective-permute-start.19 = (bf16[96,384]{1,0:T(8,128)(2,1)S(1)}, bf16[96,384]{1,0:T(8,128)(2,1)S(1)}, u32[]{:S(2)}, u32[]{:S(2)}) collective-permute-start(bf16[96,384]{1,0:T(8,128)(2,1)S(1)} %add_convert_fusion.2), channel_id=1, source_target_pairs={{0,128},{128,0},{1,129},{129,1},{2,130},{130,2},{3,131},{131,3},{4... | collective-permute-start | bytes 221192 | tf_op jit(solution)/shard_map/ppermute | solution.py:292
  107.0 7.5 %collective-permute-start.20 = (bf16[96,384]{1,0:T(8,128)(2,1)S(1)}, bf16[96,384]{1,0:T(8,128)(2,1)S(1)}, u32[]{:S(2)}, u32[]{:S(2)}) collective-permute-start(bf16[96,384]{1,0:T(8,128)(2,1)S(1)} %add_convert_fusion.1), channel_id=1, source_target_pairs={{0,12},{4,24},{8,20},{12,0},{16,28},{20,8},{24,4},{28,16},{32,44},... | collective-permute-start | bytes 221192 | tf_op jit(solution)/shard_map/ppermute | solution.py:294
  114.6 6.9 %copy-start.7 = (bf16[96,384]{1,0:T(8,128)(2,1)}, bf16[96,384]{1,0:T(8,128)(2,1)S(1)}, u32[]{:S(2)}) copy-start(bf16[96,384]{1,0:T(8,128)(2,1)S(1)} %add_convert_fusion.p0) | copy-start | bytes 221188
  114.6 5.4 %collective-permute-start.23 = (bf16[96,384]{1,0:T(8,128)(2,1)S(1)}, bf16[96,384]{1,0:T(8,128)(2,1)S(1)}, u32[]{:S(2)}, u32[]{:S(2)}) collective-permute-start(bf16[96,384]{1,0:T(8,128)(2,1)S(1)} %add_convert_fusion.p0), channel_id=1, source_target_pairs={{0,36},{4,32},{8,44},{12,40},{16,52},{20,48},{24,60},{28,56},{32,4... | collective-permute-start | bytes 221192 | tf_op jit(solution)/shard_map/ppermute | solution.py:298
  114.7 5.6 %collective-permute-start.22 = (bf16[96,384]{1,0:T(8,128)(2,1)S(1)}, bf16[96,384]{1,0:T(8,128)(2,1)S(1)}, u32[]{:S(2)}, u32[]{:S(2)}) collective-permute-start(bf16[96,384]{1,0:T(8,128)(2,1)S(1)} %add_convert_fusion.p0), channel_id=1, source_target_pairs={{0,32},{4,36},{8,40},{12,44},{16,48},{20,52},{24,56},{28,60},{32,0... | collective-permute-start | bytes 221192 | tf_op jit(solution)/shard_map/ppermute | solution.py:296
  117.2 4.4 %collective-permute-start.21 = (bf16[96,384]{1,0:T(8,128)(2,1)S(1)}, bf16[96,384]{1,0:T(8,128)(2,1)S(1)}, u32[]{:S(2)}, u32[]{:S(2)}) collective-permute-start(bf16[96,384]{1,0:T(8,128)(2,1)S(1)} %add_convert_fusion.p0), channel_id=1, source_target_pairs={{0,4},{4,0},{8,12},{12,8},{16,20},{20,16},{24,28},{28,24},{32,36},... | collective-permute-start | bytes 221192 | tf_op jit(solution)/shard_map/ppermute | solution.py:297
  120.0 1.5 %copy-start.8 = (bf16[96,384]{1,0:T(8,128)(2,1)}, bf16[96,384]{1,0:T(8,128)(2,1)S(1)}, u32[]{:S(2)}) copy-start(bf16[96,384]{1,0:T(8,128)(2,1)S(1)} %collective-permute-done.23.p3) | copy-start | bytes 221188
  120.3 1.2 %copy-start.9 = (bf16[96,384]{1,0:T(8,128)(2,1)}, bf16[96,384]{1,0:T(8,128)(2,1)S(1)}, u32[]{:S(2)}) copy-start(bf16[96,384]{1,0:T(8,128)(2,1)S(1)} %collective-permute-done.22.p2) | copy-start | bytes 221188
  121.5 0.6 copy-start.10

commit v2 on v0

v2 whole, which is shorter than its diff:
```python
import functools

import jax
import jax.numpy as jnp
from jax import lax
from jax.experimental import pallas as pl
from jax.experimental.pallas import tpu as pltpu
from jax.sharding import PartitionSpec as P

PATCH = 128
FIRST_DILATION0 = 2
EPSILON = 1e-06
HALO = 16
STEP = 32
PAD = 16

VMEM = pl.BlockSpec(memory_space=pltpu.VMEM)
SMEM = pl.BlockSpec(memory_space=pltpu.SMEM)
HBM = pl.BlockSpec(memory_space=pltpu.HBM)


def gelu(x):
    inner = x * (0.7978845608028654 + 0.035677408136300125 * (x * x))
    return (0.5 * x) * (1.0 + jnp.tanh(inner))


def in_sequence(ids, first, rows, bins, count):
    bin_at = lax.broadcasted_iota(jnp.int32, (rows, 1), 0) + (ids[1] * bins - HALO + first)
    return jnp.where((bin_at >= 0) & (bin_at < count), 1.0, 0.0)


def norm_rows(ids, layer, pieces, gains, normed, at):
    rows, width = pieces[0].shape
    wide = [p.astype(jnp.float32) for p in pieces]
    total = wide[0] * wide[0]
    for w in wide[1:]:
        total = total + w * w
    inverse = lax.rsqrt(jnp.sum(total, axis=-1, keepdims=True) * (1.0 / (4 * width)) + EPSILON)
    for k, w in enumerate(wide):
        at_lane = pl.multiple_of((ids[0] ^ k) * width, 128)
        value = gelu(w * inverse * gains[layer : layer + 1, pl.ds(at_lane, width)])
        normed[at : at + rows, k * width : (k + 1) * width] = value.astype(jnp.bfloat16)


def norm_segment(ids, layer, read, count, gains, normed, at):
    for first in range(0, count, STEP):
        rows = min(STEP, count - first)
        norm_rows(ids, layer, read(first, rows), gains, normed, at + first)


def convolve(normed, weights, copies, at, rows, dilation):
    update = None
    for t in range(3):
        for copy in copies[t] if copies else ():
            copy.wait()
        first = at + (t - 1) * dilation
        part = jnp.dot(
            normed[first : first + rows, :], weights[t], preferred_element_type=jnp.float32
        )
        update = part if update is None else update + part
    return update


def clear(ref, first, rows):
    ref[first : first + rows, :] = jnp.zeros((rows, ref.shape[1]), ref.dtype)


def start_weights(ids, layer, w_hbm, out, sems):
    width = out.shape[2]
    taps = []
    for t in range(3):
        taps.append([])
        for k in range(4):
            copy = pltpu.make_async_copy(
                w_hbm.at[layer, t, pl.ds((ids[0] ^ k) * width, width), :],
                out.at[t, pl.ds(k * width, width), :],
                sems.at[t, k],
            )
            copy.start()
            taps[-1].append(copy)
    return taps


def one_hot(bins, count, ids, before, own, after, stem_hbm, onehot, stem, sem):
    copy = pltpu.make_async_copy(stem_hbm, stem, sem)
    copy.start()
    letters = jnp.concatenate([before[...], own[...], after[...]], axis=0)
    letters = letters.astype(jnp.float32).astype(jnp.bfloat16)
    lane = lax.broadcasted_iota(jnp.int32, (PATCH, 4 * PATCH), 1)
    row = lax.broadcasted_iota(jnp.int32, (PATCH, 4 * PATCH), 0)
    spread = jnp.where(lane // 4 == row, 1.0, 0.0).astype(jnp.bfloat16)
    repeated = jnp.dot(letters, spread, preferred_element_type=jnp.float32)
    base = (lax.broadcasted_iota(jnp.int32, (1, 4 * PATCH), 1) % 4).astype(jnp.float32)
    inside = in_sequence(ids, 0, bins + 2 * HALO, bins, count)
    onehot[...] = (jnp.where(repeated == base, 1.0, 0.0) * inside).astype(jnp.bfloat16)
    copy.wait()


def first_layer(span, bins, count, ids, onehot, own, w1, w2a, w2b, w3a, w3b, gains, w_in, out, *refs):
    low, high = span
    if low == 0:
        weights, normed, stream, sems = refs
        copies = start_weights(ids, 0, w_in, weights, sems)
    else:
        weights, copies, (normed, stream) = w_in, None, refs
    width = out.shape[1]
    first, last = max(low - HALO, 0), min(high + HALO, bins + 2 * HALO)
    rows = last - first
    clear(normed, 0, PAD)
    clear(normed, PAD + rows, PAD)
    stem = jnp.concatenate(
        [
            own[...],
            w1[...],
            jnp.concatenate([w2a[...], w2b[...]], axis=0),
            jnp.concatenate([w3a[...], w3b[...]], axis=0),
        ],
        axis=1,
    )
    stream[...] = jnp.dot(
        onehot[first:last, :], stem, preferred_element_type=jnp.float32
    ).astype(jnp.bfloat16)

    def read(at, n):
        return [stream[at : at + n, k * width : (k + 1) * width] for k in range(4)]

    norm_segment(ids, 0, read, rows, gains, normed, PAD)
    update = convolve(normed, weights, copies, PAD + low - first, high - low, FIRST_DILATION0)
    total = stream[low - first : high - first, 0:width].astype(jnp.float32) + update
    inside = in_sequence(ids, low, high - low, bins, count)
    out[...] = (total * inside).astype(jnp.bfloat16)


def front(layer, dilation, span, bins, count, ids, *refs):
    pieces, (gains, w_hbm, out, weights, normed, sems) = refs[:4], refs[4:]
    low, high = span
    rows = high + HALO
    copies = start_weights(ids, layer, w_hbm, weights, sems)
    clear(normed, 0, PAD)

    def read(at, n):
        return [p[at : at + n, :] for p in pieces]

    norm_segment(ids, layer, read, rows, gains, normed, PAD)
    update = convolve(normed, weights, copies, PAD + low, high - low, dilation)
    total = pieces[0][low:high, :].astype(jnp.float32) + update
    if count:
        total = total * in_sequence(ids, low, high - low, bins, count)
    out[...] = total.astype(jnp.bfloat16)


def back(layer, dilation, span, bins, count, ids, *refs):
    fronts, backs, (gains, weights, out, normed) = refs[:4], refs[4:8], refs[8:]
    low, high = span
    first = low - HALO
    joint = fronts[0].shape[0]
    rows = joint + backs[0].shape[0] - first
    clear(normed, PAD + rows, PAD)

    def read_front(at, n):
        return [p[first + at : first + at + n, :] for p in fronts]

    def read_back(at, n):
        return [p[at : at + n, :] for p in backs]

    norm_segment(ids, layer, read_front, joint - first, gains, normed, PAD)
    norm_segment(ids, layer, read_back, backs[0].shape[0], gains, normed, PAD + joint - first)
    update = convolve(normed, weights, None, PAD + HALO, high - low, dilation)
    own = jnp.concatenate([fronts[0][low:joint, :], backs[0][0 : high - joint, :]], axis=0)
    total = own.astype(jnp.float32) + update
    if count:
        total = total * in_sequence(ids, low, high - low, bins, count)
    out[...] = total.astype(jnp.bfloat16)


def gradient(stream, upstream):
    return lax.dot_general(
        stream, upstream, (((0,), (0,)), ((), ())), preferred_element_type=jnp.float32
    )


def last_front(span, bins, ids, *refs):
    refs, (upstream, out, grad, weights, normed, sems) = refs[:6], refs[6:]
    front(2, 4 * FIRST_DILATION0, span, bins, 0, ids, *refs, out, weights, normed, sems)
    low, high = span
    grad[...] = gradient(out[...], upstream[low - HALO : high - HALO, :])


def last_back(span, bins, ids, *refs):
    refs, (upstream, before, out, g0, g1, g2, g3, normed, grad) = refs[:10], refs[10:]
    back(2, 4 * FIRST_DILATION0, span, bins, 0, ids, *refs, out, normed)
    low, high = span
    grad[...] = before[...] + gradient(out[...], upstream[low - HALO : high - HALO, :])
    quarter = g0.shape[0]
    g0[...] = grad[pl.ds(pl.multiple_of(ids[2] * quarter, 8), quarter), :]
    for k, g in ((1, g1), (2, g2), (3, g3)):
        at = pl.multiple_of((ids[2] ^ k) * quarter, 8)
        g[...] = grad[pl.ds(at, quarter), :].astype(jnp.bfloat16)


def decode(front_rows, back_rows, weights, out):
    cut = front_rows.shape[0]
    for part, first in ((front_rows, 0), (back_rows, cut)):
        value = jnp.dot(part[...], weights[...], preferred_element_type=jnp.float32)
        out[first : first + part.shape[0], :] = value.astype(jnp.bfloat16)


def assemble(ids, p0, p1, p2, p3, out):
    quarter = p0.shape[0]
    for k, p in enumerate((p0, p1, p2, p3)):
        at = pl.multiple_of((ids[2] ^ k) * quarter, 8)
        out[pl.ds(at, quarter), :] = p[...].astype(jnp.float32)


def tie(value, *done):
    return lax.optimization_barrier((value, *done))[0]


def pairs(size, partner):
    return [(i, partner(i)) for i in range(size)]


def call(name, kernel, outs, in_specs, scratch=(), flops=0, megabytes=52):
    many = isinstance(outs, (list, tuple))
    return pl.pallas_call(
        kernel,
        out_shape=tuple(outs) if many else outs,
        in_specs=in_specs,
        out_specs=(VMEM,) * len(outs) if many else VMEM,
        scratch_shapes=list(scratch),
        compiler_params=pltpu.CompilerParams(vmem_limit_bytes=megabytes * 2**20),
        cost_estimate=pl.CostEstimate(flops=flops, bytes_accessed=2**20, transcendentals=0),
        name=name,
    )


def body(zs, seq_count, bases, stem, gains, conv_weight, dec_weight, upstream):
    bins, width = upstream.shape[1], upstream.shape[2]
    rows = bins + 2 * HALO
    count = bins * seq_count
    bf16, f32 = jnp.bfloat16, jnp.float32
    seq, chan = lax.axis_index("seq"), lax.axis_index("chan")
    x, z = seq // zs, seq % zs
    x_half, z_half = ((x + 1) // 2) % 2, ((z + 1) // 2) % 2
    ids = jnp.stack([chan, seq, x_half * 2 + z_half]).astype(jnp.int32)

    across = functools.partial(lax.ppermute, axis_name="chan", perm=pairs(4, lambda i: i ^ 2))
    other_core = functools.partial(lax.ppermute, axis_name="chan", perm=pairs(4, lambda i: i ^ 1))
    far = functools.partial(
        lax.ppermute, axis_name=("section", "chan"), perm=pairs(8, lambda i: i ^ 6)
    )

    letters = bases.reshape(bins, PATCH)
    up = [(i, i + 1) for i in range(seq_count - 1)]
    down = [(j, i) for i, j in up]
    half = stem.shape[0] // 2
    before = lax.ppermute(letters[bins - HALO :], "seq", up)
    after = lax.ppermute(letters[:HALO], "seq", down)
    w2a = across(stem[:half])
    w2b = far(stem[half:])
    w1 = other_core(stem)
    onehot, stem = call(
        "one_hot",
        functools.partial(one_hot, bins, count),
        [jax.ShapeDtypeStruct((rows, 4 * PATCH), bf16), jax.ShapeDtypeStruct(stem.shape, bf16)],
        [SMEM] + [VMEM] * 3 + [HBM],
        [pltpu.SemaphoreType.DMA],
        megabytes=8,
        flops=10**9,
    )(ids, before, letters, after, stem)
    w2a = tie(w2a, before, after)
    w3a = other_core(w2a)
    w2b = tie(w2b, onehot)
    w3b = other_core(w2b)

    def shape(n):
        return jax.ShapeDtypeStruct((n, width), bf16)

    def work(n):
        return 2 * n * 3 * 4 * width * width

    def normed(n):
        return pltpu.VMEM((n + 2 * PAD, 4 * width), bf16)

    def exchange(own):
        return own, other_core(own), across(own)

    def finish(sent, *done):
        own, beside, remote = sent
        remote = tie(remote, *done)
        return own, beside, remote, other_core(remote)

    cut = bins // 2 + 3 * HALO
    layer_weights = jax.ShapeDtypeStruct((3, 4 * width, width), bf16)
    weight_sems = pltpu.SemaphoreType.DMA((3, 4))
    inputs = (onehot, stem, w1, w2a, w2b, w3a, w3b, gains)
    part, weights = call(
        "zero_front",
        functools.partial(first_layer, (0, cut), bins, count),
        [shape(cut), layer_weights],
        [SMEM] + [VMEM] * 8 + [HBM],
        [normed(cut + HALO), pltpu.VMEM((cut + HALO, 4 * width), bf16), weight_sems],
        flops=work(cut),
    )(ids, *inputs, conv_weight)
    sent_front = exchange(part)
    part = call(
        "zero_back",
        functools.partial(first_layer, (cut, rows), bins, count),
        shape(rows - cut),
        [SMEM] + [VMEM] * 9,
        [normed(rows - cut + HALO), pltpu.VMEM((rows - cut + HALO, 4 * width), bf16)],
        flops=work(rows - cut),
    )(ids, *inputs, weights)
    sent_back = exchange(part)
    fronts = finish(sent_front, part)

    cut = cut - HALO
    part, weights = call(
        "one_front",
        functools.partial(front, 1, 2 * FIRST_DILATION0, (0, cut), bins, count),
        [shape(cut), layer_weights],
        [SMEM] + [VMEM] * 5 + [HBM],
        [normed(cut + HALO), weight_sems],
        flops=work(cut),
    )(ids, *fronts, gains, conv_weight)
    sent_front = exchange(part)
    backs = finish(sent_back, part)
    part = call(
        "one_back",
        functools.partial(back, 1, 2 * FIRST_DILATION0, (cut, rows), bins, count),
        shape(rows - cut),
        [SMEM] + [VMEM] * 10,
        [normed(rows - cut + HALO)],
        flops=work(rows - cut),
    )(ids, *fronts, *backs, gains, weights)
    sent_back = exchange(part)
    fronts = finish(sent_front, part)

    cut = cut - HALO
    front_rows, front_grad, weights = call(
        "two_front",
        functools.partial(last_front, (HALO, cut), bins),
        [shape(cut - HALO), jax.ShapeDtypeStruct((width, width), f32), layer_weights],
        [SMEM] + [VMEM] * 5 + [HBM, VMEM],
        [normed(cut + HALO), weight_sems],
        flops=work(cut - HALO),
    )(ids, *fronts, gains, conv_weight, upstream[0])
    backs = finish(sent_back, front_rows)
    back_rows, g0, g1, g2, g3 = call(
        "two_back",
        functools.partial(last_back, (cut, rows - HALO), bins),
        [shape(rows - HALO - cut), jax.ShapeDtypeStruct((width // 4, width), f32)]
        + [shape(width // 4)] * 3,
        [SMEM] + [VMEM] * 12,
        [normed(rows - cut + HALO), pltpu.VMEM((width, width), f32)],
        flops=work(rows - HALO - cut),
    )(ids, *fronts, *backs, gains, weights, upstream[0], front_grad)
    decoded = call(
        "decode",
        decode,
        shape(bins),
        [VMEM] * 3,
        flops=2 * bins * width * width,
        megabytes=8,
    )(front_rows, back_rows, dec_weight)

    def over(fx, fz):
        def partner(i):
            return fx(i // zs) * zs + fz(i % zs)

        return functools.partial(lax.ppermute, axis_name="seq", perm=pairs(seq_count, partner))

    def same(i):
        return i

    def flip(i):
        return i ^ 1

    def xs_near(i):
        return 3 - i

    def zs_near(i):
        return (i + 1) % zs if i % 2 else (i - 1) % zs

    def zs_far(i):
        return {0: 3, 3: 0, 1: 6, 6: 1, 2: 5, 5: 2, 4: 7, 7: 4}[i]

    r2 = over(flip, same)(g2)
    r1 = over(same, flip)(g1)
    r3 = over(flip, flip)(g3)
    total = (g0 + r2.astype(f32)) + (r1.astype(f32) + r3.astype(f32))
    own = total.astype(bf16)
    rx = over(xs_near, same)(own)
    rz = over(same, zs_near)(own)
    rxz = over(xs_near, zs_near)(own)
    total = (own.astype(f32) + rx.astype(f32)) + (rz.astype(f32) + rxz.astype(f32))
    own = total.astype(bf16)
    other = lax.ppermute(own, "section", [(0, 1), (1, 0)])
    own = (own.astype(f32) + other.astype(f32)).astype(bf16)
    other = over(same, zs_far)(own)
    own = (own.astype(f32) + other.astype(f32)).astype(bf16)
    r2 = over(flip, same)(own)
    r1 = over(same, flip)(own)
    r3 = over(flip, flip)(own)
    weight_grad = call(
        "assemble",
        assemble,
        jax.ShapeDtypeStruct((width, width), f32),
        [SMEM] + [VMEM] * 4,
        megabytes=8,
    )(ids, own, r1, r2, r3)
    return (decoded[None], weight_grad)


def solution(mesh):
    placed = (
        P("section", "seq"),
        P(None, "chan"),
        P(),
        P(None, None, None, "chan"),
        P("chan", None),
        P("section", "seq", "chan"),
    )
    seq_count = mesh.shape["seq"]
    return jax.shard_map(
        functools.partial(body, seq_count // 4, seq_count),
        mesh=mesh,
        in_specs=placed,
        out_specs=(P("section", "seq", "chan"), P("chan", None)),
        check_vma=False,
    )
```

time: 815 us -> 107 us (0.13)
  waiting for transfers between devices: 737 us -> 33.8 us
  Pallas kernels: 0 us -> 36 us
  matrix products: 25.6 us -> 0 us
  starting transfers between devices: 18.1 us -> 31.7 us
  other arithmetic: 13.7 us -> 0.2 us
  between operations: 14.1 us -> 0.83 us
    psum x1 -> x0, waiting for transfers between devices: 648 us -> none  [body(): weight_grad = lax.psum(partial_grad, ('section', 'seq'))]
    all_gather x3 -> x0, waiting for transfers between devices: 88.2 us -> none  [body(): full_rows = lax.all_gather(stream, 'chan', axis=1, tiled=True)]
    pallas_call x0 -> x9, Pallas kernels: none -> 36 us  [the longest x1 7.03 us: body(): call('zero_front', functools.partial(first_layer, (0, cut), bins, count),...]
    ppermute x6 -> x30, waiting for transfers between devices: 0.89 us -> 33.8 us  [the longest x8 5.53 us: exchange(): return (own, other_core(own), across(own))]
    dot_general x12 -> x0, matrix products: 25.6 us -> none  [the longest x6 13.5 us: apply_convolution(): jnp.dot(padded[start:start + row_count], kernel_taps[offset], preferred_e...]
    ppermute x6 -> x30, starting transfers between devices: 18 us -> 31.7 us  [the longest x1 3.93 us: body(): r1 = over(same, flip)(g1)]
    convert_element_type x3 -> x4, other arithmetic: 8.35 us -> 0.13 us  [the longest x2 0.08 us: body(): own = total.astype(bf16)]
  transfers between devices with their start and end apart: 10 -> 30, of which waited for: 5 -> 19; matrix products, arithmetic and copies ran while one was open for 2% -> 1% of each run, Pallas kernels for 0% -> 21%
where the time goes in v2:
time: 107 us
  Pallas kernels  36 us (34%)
  waiting for transfers between devices  33.8 us (32%)
  starting transfers between devices  31.7 us (30%)
  local copies, waits for them, and re-layouts  4.55 us (4%)
    pallas_call x1, Pallas kernels, body(): call('zero_front', functools.partial(first_layer, (0, cut), bins, count),...  7.03 us
    pallas_call x1, Pallas kernels, body(): call('two_front', functools.partial(last_front, (HALO, cut), bins), [shap...  6.47 us
    pallas_call x1, Pallas kernels, body(): call('one_front', functools.partial(front, 1, 2 * FIRST_DILATION0, (0, cu...  5.82 us
    ppermute x8, waiting for transfers between devices, exchange(): return (own, other_core(own), across(own))  5.53 us
    pallas_call x1, Pallas kernels, body(): call('two_back', functools.partial(last_back, (cut, rows - HALO), bins),...  4.67 us
    pallas_call x1, Pallas kernels, body(): call('zero_back', functools.partial(first_layer, (cut, rows), bins, count...  4.51 us
    ppermute x1, waiting for transfers between devices, body(): other = lax.ppermute(own, 'section', [(0, 1), (1, 0)])  4.5 us
    ppermute x1, waiting for transfers between devices, body(): other = over(same, zs_far)(own)  4.24 us
  transfers between devices with their start and end apart: 30, of which 19 were waited for; matrix products, arithmetic and copies ran while one was open for 1% of the time, Pallas kernels for 21%

profile of v2, /device:TPU:32, one launch (start us, length us, event | category | flops | bytes accessed | tf_op | source)
XLA Modules:
  0.0 107.1 jit_solution(16342536838956750538)
XLA Ops:
  0.6 0.7 fusion.1
  1.4 3.8 %collective-permute-start = (s32[16,128]{1,0:T(8,128)S(1)}, s32[16,128]{1,0:T(8,128)S(1)}, u32[]{:S(2)}, u32[]{:S(2)}) collective-permute-start(s32[16,128]{1,0:T(8,128)S(1)} %bitcast.13), channel_id=1, source_target_pairs={{0,4},{4,8},{8,12},{12,16},{16,20},{20,24},{24,28},{28,32},{32,36}... | collective-permute-start | bytes 24584 | tf_op jit(solution)/shard_map/ppermute | solution.py:257
  5.2 2.0 %collective-permute-start.1 = (s32[16,128]{1,0:T(8,128)S(1)}, s32[16,128]{1,0:T(8,128)S(1)}, u32[]{:S(2)}, u32[]{:S(2)}) collective-permute-start(s32[16,128]{1,0:T(8,128)S(1)} %bitcast.12), channel_id=1, source_target_pairs={{4,0},{8,4},{12,8},{16,12},{20,16},{24,20},{28,24},{32,28},{36,32}... | collective-permute-start | bytes 24584 | tf_op jit(solution)/shard_map/ppermute | solution.py:258
  7.3 1.1 fusion
  8.4 3.1 %collective-permute-start.4 = (bf16[256,384]{1,0:T(8,128)(2,1)S(1)}, bf16[256,384]{1,0:T(8,128)(2,1)S(1)}, u32[]{:S(2)}, u32[]{:S(2)}) collective-permute-start(bf16[256,384]{1,0:T(8,128)(2,1)S(1)} %get-tuple-element.42), channel_id=1, source_target_pairs={{0,130},{1,131},{2,128},{3,129},{128,2},{129,3},{130,0},{131,1},{4... | collective-permute-start | bytes 589832 | tf_op jit(solution)/shard_map/ppermute | solution.py:260
  11.7 1.0 copy-done.5
  12.7 0.9 copy-done.7
  13.6 1.0 one_hot.1
  14.7 0.8 copy-done
  15.5 3.0 %collective-permute-done.3.w2a = bf16[256,384]{1,0:T(8,128)(2,1)S(1)} collective-permute-done((bf16[256,384]{1,0:T(8,128)(2,1)S(1)}, bf16[256,384]{1,0:T(8,128)(2,1)S(1)}, u32[]{:S(2)}, u32[]{:S(2)}) %collective-permute-start.3) | collective-permute-done | bytes 196640 | tf_op jit(solution)/shard_map/ppermute | solution.py:259
  18.5 0.5 collective-permute-start.6
  19.0 0.9 collective-permute-done.5.w3a
  20.2 7.0 %zero_front.1 = (bf16[304,384]{1,0:T(8,128)(2,1)S(1)}, bf16[3,1536,384]{2,1,0:T(8,128)(2,1)}) custom-call(s32[3]{0:T(128)S(1)} %pad_add_fusion.ids, bf16[544,512]{1,0:T(8,128)(2,1)} %copy-done, bf16[512,384]{1,0:T(8,128)(2,1)S(1)} %get-tuple-element.23.own, bf16[512,384]{1,0:T(8,128)(2,1)S(1)} %collective-permute-done.2.w1, ...), custom_call_target="tpu_custom_call" | custom-call | flops 1075838976 | bytes 1048576 | tf_op jit(solution)/shard_map/zero_front/pallas_call | solution.py:297
  27.3 0.4 collective-permute-start.8
  27.7 4.5 %zero_back.1.refs_4_ = bf16[240,384]{1,0:T(8,128)(2,1)S(1)} custom-call(s32[3]{0:T(128)S(1)} %pad_add_fusion.ids, bf16[544,512]{1,0:T(8,128)(2,1)} %copy-done, bf16[512,384]{1,0:T(8,128)(2,1)S(1)} %get-tuple-element.23.own, bf16[512,384]{1,0:T(8,128)(2,1)S(1)} %collective-permute-done.2.w1, bf16[256,384]{1,0:T(8,128)(2,1)S(1)} %collective-permute-done.3.w2a, ...), custom_call_target="tpu_custom_call" | custom-call | flops 849346560 | bytes 1048576 | tf_op jit(solution)/shard_map/zero_back/pallas_call | solution.py:306
  32.2 3.0 %collective-permute-done.8.refs_2_ = bf16[304,384]{1,0:T(8,128)(2,1)S(1)} collective-permute-done((bf16[304,384]{1,0:T(8,128)(2,1)S(1)}, bf16[304,384]{1,0:T(8,128)(2,1)S(1)}, u32[]{:S(2)}, u32[]{:S(2)}) %collective-permute-start.8) | collective-permute-done | bytes 233504 | tf_op jit(solution)/shard_map/ppermute | solution.py:286
  35.7 1.0 collective-permute-done.9.refs_3_
  36.7 5.8 %one_front.1 = (bf16[288,384]{1,0:T(8,128)(2,1)S(1)}, bf16[3,1536,384]{2,1,0:T(8,128)(2,1)}) custom-call(s32[3]{0:T(128)S(1)} %pad_add_fusion.ids, bf16[304,384]{1,0:T(8,128)(2,1)S(1)} %get-tuple-element.26.refs_0_, bf16[304,384]{1,0:T(8,128)(2,1)S(1)} %collective-permute-done.7.refs_1_, bf16[304,384]{1,0:T(8,128)(2,1)S(1)} %collective-permute-done.8.refs_2_, ...), custom_call_target="tpu_custom_call" | custom-call | flops 1019215872 | bytes 1048576 | tf_op jit(solution)/shard_map/one_front/pallas_call | solution.py:318
  42.7 0.9 collective-permute-start.11
  43.7 0.4 collective-permute-done.14.refs_7_
  44.0 3.9 %one_back.1.refs_4_ = bf16[256,384]{1,0:T(8,128)(2,1)S(1)} custom-call(s32[3]{0:T(128)S(1)} %pad_add_fusion.ids, bf16[304,384]{1,0:T(8,128)(2,1)S(1)} %get-tuple-element.26.refs_0_, bf16[304,384]{1,0:T(8,128)(2,1)S(1)} %collective-permute-done.7.refs_1_, bf16[304,384]{1,0:T(8,128)(2,1)S(1)} %collective-permute-done.8.refs_2_, ...), custom_call_target="tpu_custom_call" | custom-call | flops 905969664 | bytes 1048576 | tf_op jit(solution)/shard_map/one_back/pallas_call | solution.py:328
  47.9 2.5 %collective-permute-done.11.refs_2_ = bf16[288,384]{1,0:T(8,128)(2,1)S(1)} collective-permute-done((bf16[288,384]{1,0:T(8,128)(2,1)S(1)}, bf16[288,384]{1,0:T(8,128)(2,1)S(1)}, u32[]{:S(2)}, u32[]{:S(2)}) %collective-permute-start.11) | collective-permute-done | bytes 221216 | tf_op jit(solution)/shard_map/ppermute | solution.py:286
  50.5 0.8 collective-permute-start.17
  51.5 0.5 collective-permute-done.15.refs_3_
  51.9 6.5 %two_front.1 = (bf16[256,384]{1,0:T(8,128)(2,1)S(1)}, f32[384,384]{1,0:T(8,128)}, bf16[3,1536,384]{2,1,0:T(8,128)(2,1)}) custom-call(s32[3]{0:T(128)S(1)} %pad_add_fusion.ids, bf16[288,384]{1,0:T(8,128)(2,1)S(1)} %get-tuple-element.29.refs_0_, bf16[288,384]{1,0:T(8,128)(2,1)S(1)} %collective-permute-done.10.refs_1_, ...), custom_call_target="tpu_custom_call" | custom-call | flops 905969664 | bytes 1048576 | tf_op jit(solution)/shard_map/two_front/pallas_call | solution.py:340
  58.4 0.4 collective-permute-start.18
  58.9 1.3 %collective-permute-done.18.refs_7_ = bf16[256,384]{1,0:T(8,128)(2,1)S(1)} collective-permute-done((bf16[256,384]{1,0:T(8,128)(2,1)S(1)}, bf16[256,384]{1,0:T(8,128)(2,1)S(1)}, u32[]{:S(2)}, u32[]{:S(2)}) %collective-permute-start.18) | collective-permute-done | bytes 196640 | tf_op jit(solution)/shard_map/ppermute | solution.py:291
  60.2 4.7 %two_back.1 = (bf16[256,384]{1,0:T(8,128)(2,1)S(1)}, f32[96,384]{1,0:T(8,128)S(1)}, bf16[96,384]{1,0:T(8,128)(2,1)S(1)}, bf16[96,384]{1,0:T(8,128)(2,1)S(1)}, bf16[96,384]{1,0:T(8,128)(2,1)S(1)}) custom-call(s32[3]{0:T(128)S(1)} %pad_add_fusion.ids, bf16[288,384]{1,0:T(8,128)(2,1)S(1)} %get-tuple-element.29.refs_0_, ...), custom_call_target="tpu_custom_call" | custom-call | flops 905969664 | bytes 1048576 | tf_op jit(solution)/shard_map/two_back/pallas_call | solution.py:349
  64.9 1.6 %collective-permute-start.19 = (bf16[96,384]{1,0:T(8,128)(2,1)S(1)}, bf16[96,384]{1,0:T(8,128)(2,1)S(1)}, u32[]{:S(2)}, u32[]{:S(2)}) collective-permute-start(bf16[96,384]{1,0:T(8,128)(2,1)S(1)} %get-tuple-element.39), channel_id=1, source_target_pairs={{0,32},{4,36},{8,40},{12,44},{16,48},{20,52},{24,56},{28,60},{32,0... | collective-permute-start | bytes 221192 | tf_op jit(solution)/shard_map/ppermute | solution.py:388
  66.5 3.9 %collective-permute-start.20 = (bf16[96,384]{1,0:T(8,128)(2,1)S(1)}, bf16[96,384]{1,0:T(8,128)(2,1)S(1)}, u32[]{:S(2)}, u32[]{:S(2)}) collective-permute-start(bf16[96,384]{1,0:T(8,128)(2,1)S(1)} %get-tuple-element.40), channel_id=1, source_target_pairs={{0,4},{4,0},{8,12},{12,8},{16,20},{20,16},{24,28},{28,24},{32,36},... | collective-permute-start | bytes 221192 | tf_op jit(solution)/shard_map/ppermute | solution.py:389
  70.4 2.8 %collective-permute-done.20 = bf16[96,384]{1,0:T(8,128)(2,1)S(1)} collective-permute-done((bf16[96,384]{1,0:T(8,128)(2,1)S(1)}, bf16[96,384]{1,0:T(8,128)(2,1)S(1)}, u32[]{:S(2)}, u32[]{:S(2)}) %collective-permute-start.20) | collective-permute-done | bytes 73760 | tf_op jit(solution)/shard_map/ppermute | solution.py:389
  73.1 2.5 %collective-permute-done.21 = bf16[96,384]{1,0:T(8,128)(2,1)S(1)} collective-permute-done((bf16[96,384]{1,0:T(8,128)(2,1)S(1)}, bf16[96,384]{1,0:T(8,128)(2,1)S(1)}, u32[]{:S(2)}, u32[]{:S(2)}) %collective-permute-start.21) | collective-permute-done | bytes 73760 | tf_op jit(solution)/shard_map/ppermute | solution.py:390
  75.7 2.6 %collective-permute-start.24 = (bf16[96,384]{1,0:T(8,128)(2,1)S(1)}, bf16[96,384]{1,0:T(8,128)(2,1)S(1)}, u32[]{:S(2)}, u32[]{:S(2)}) collective-permute-start(bf16[96,384]{1,0:T(8,128)(2,1)S(1)} %add_convert_fusion.3), channel_id=1, source_target_pairs={{0,124},{4,104},{8,100},{12,112},{16,108},{20,120},{24,116},{28,96... | collective-permute-start | bytes 221192 | tf_op jit(solution)/shard_map/ppermute | solution.py:395
  78.3 1.0 collective-permute-start.23
  79.3 1.1 %collective-permute-start.22 = (bf16[96,384]{1,0:T(8,128)(2,1)S(1)}, bf16[96,384]{1,0:T(8,128)(2,1)S(1)}, u32[]{:S(2)}, u32[]{:S(2)}) collective-permute-start(bf16[96,384]{1,0:T(8,128)(2,1)S(1)} %add_convert_fusion.3), channel_id=1, source_target_pairs={{0,96},{4,100},{8,104},{12,108},{16,112},{20,116},{24,120},{28,124... | collective-permute-start | bytes 221192 | tf_op jit(solution)/shard_map/ppermute | solution.py:393
  80.5 1.9 %collective-permute-done.24 = bf16[96,384]{1,0:T(8,128)(2,1)S(1)} collective-permute-done((bf16[96,384]{1,0:T(8,128)(2,1)S(1)}, bf16[96,384]{1,0:T(8,128)(2,1)S(1)}, u32[]{:S(2)}, u32[]{:S(2)}) %collective-permute-start.24) | collective-permute-done | bytes 73760 | tf_op jit(solution)/shard_map/ppermute | solution.py:395
  82.7 2.2 %collective-permute-done.22 = bf16[96,384]{1,0:T(8,128)(2,1)S(1)} collective-permute-done((bf16[96,384]{1,0:T(8,128)(2,1)S(1)}, bf16[96,384]{1,0:T(8,128)(2,1)S(1)}, u32[]{:S(2)}, u32[]{:S(2)}) %collective-permute-start.22) | collective-permute-done | bytes 73760 | tf_op jit(solution)/shard_map/ppermute | solution.py:393
  84.9 1.4 %collective-permute-start.25 = (bf16[96,384]{1,0:T(8,128)(2,1)S(1)}, bf16[96,384]{1,0:T(8,128)(2,1)S(1)}, u32[]{:S(2)}, u32[]{:S(2)}) collective-permute-start(bf16[96,384]{1,0:T(8,128)(2,1)S(1)} %add_convert_fusion.2), channel_id=1, source_target_pairs={{0,128},{128,0},{1,129},{129,1},{2,130},{130,2},{3,131},{131,3},{4... | collective-permute-start | bytes 221192 | tf_op jit(solution)/shard_map/ppermute | solution.py:398
  86.4 4.5 %collective-permute-done.25 = bf16[96,384]{1,0:T(8,128)(2,1)S(1)} collective-permute-done((bf16[96,384]{1,0:T(8,128)(2,1)S(1)}, bf16[96,384]{1,0:T(8,128)(2,1)S(1)}, u32[]{:S(2)}, u32[]{:S(2)}) %collective-permute-start.25) | collective-permute-done | bytes 73760 | tf_op jit(solution)/shard_map/ppermute | solution.py:398
  90.9 3.2 %collective-permute-start.26 = (bf16[96,384]{1,0:T(8,128)(2,1)S(1)}, bf16[96,384]{1,0:T(8,128)(2,1)S(1)}, u32[]{:S(2)}, u32[]{:S(2)}) collective-permute-start(bf16[96,384]{1,0:T(8,128)(2,1)S(1)} %add_convert_fusion.1), channel_id=1, source_target_pairs={{0,12},{4,24},{8,20},{12,0},{16,28},{20,8},{24,4},{28,16},{32,44},... | collective-permute-start | bytes 221192 | tf_op jit(solution)/shard_map/ppermute | solution.py:400
  94.1 4.2 %collective-permute-done.26 = bf16[96,384]{1,0:T(8,128)(2,1)S(1)} collective-permute-done((bf16[96,384]{1,0:T(8,128)(2,1)S(1)}, bf16[96,384]{1,0:T(8,128)(2,1)S(1)}, u32[]{:S(2)}, u32[]{:S(2)}) %collective-permute-start.26) | collective-permute-done | bytes 73760 | tf_op jit(solution)/shard_map/ppermute | solution.py:400
  98.5 2.8 %collective-permute-start.28 = (bf16[96,384]{1,0:T(8,128)(2,1)S(1)}, bf16[96,384]{1,0:T(8,128)(2,1)S(1)}, u32[]{:S(2)}, u32[]{:S(2)}) collective-permute-start(bf16[96,384]{1,0:T(8,128)(2,1)S(1)} %add_convert_fusion.p0), channel_id=1, source_target_pairs={{0,32},{4,36},{8,40},{12,44},{16,48},{20,52},{24,56},{28,60},{32,0... | collective-permute-start | bytes 221192 | tf_op jit(solution)/shard_map/ppermute | solution.py:402
  101.3 0.6 collective-permute-start.27
  102.0 1.1 %decode.1 = bf16[512,384]{1,0:T(8,128)(2,1)} custom-call(bf16[256,384]{1,0:T(8,128)(2,1)S(1)} %get-tuple-element.33.front_rows, bf16[256,384]{1,0:T(8,128)(2,1)S(1)} %get-tuple-element.37.back_rows, bf16[384,384]{1,0:T(8,128)(2,1)S(1)} %copy-done.6), custom_call_target="tpu_custom_call" | custom-call | flops 150994944 | bytes 1048576 | tf_op jit(solution)/shard_map/decode/pallas_call | solution.py:358
  103.1 0.7 collective-permute-done.29.p3
  103.8 0.6 collective-permute-done.28.p2
  104.4 1.2 %collective-permute-done.27.p1 = bf16[96,384]{1,0:T(8,128)(2,1)S(1)} collective-permute-done((bf16[96,384]{1,0:T(8,128)(2,1)S(1)}, bf16[96,384]{1,0:T(8,128)(2,1)S(1)}, u32[]{:S(2)}, u32[]{:S(2)}) %collective-permute-start.27) | collective-permute-done | bytes 73760 | tf_op jit(solution)/shard_map/ppermute | solution.py:403
  105.7 1.4 %assemble.1 = f32[384,384]{1,0:T(8,128)} custom-call(s32[3]{0:T(128)S(1)} %pad_add_fusion.ids, bf16[96,384]{1,0:T(8,128)(2,1)S(1)} %add_convert_fusion.p0, bf16[96,384]{1,0:T(8,128)(2,1)S(1)} %collective-permute-done.27.p1, bf16[96,384]{1,0:T(8,128)(2,1)S(1)} %collective-permute-done.28.p2, bf16[96,384]{1,0:T(8,128)(2,1)S(1)} %collective-permute-done.29.p3), custom_call_target="tpu_custom_call" | custom-call | bytes 1048576 | tf_op jit(solution)/shard_map/assemble/pallas_call | solution.py:405
  (44 shorter events, 2.2 us)
Async XLA Ops:
  0.6 19.6 %copy-start.4 = (f32[3,1536]{1,0:T(4,128)S(1)}, f32[3,1536]{1,0:T(4,128)}, u32[]{:S(2)}) copy-start(f32[3,1536]{1,0:T(4,128)} %refs_8_.3) | copy-start | bytes 55300
  1.4 10.3 %collective-permute-start = (s32[16,128]{1,0:T(8,128)S(1)}, s32[16,128]{1,0:T(8,128)S(1)}, u32[]{:S(2)}, u32[]{:S(2)}) collective-permute-start(s32[16,128]{1,0:T(8,128)S(1)} %bitcast.13), channel_id=1, source_target_pairs={{0,4},{4,8},{8,12},{12,16},{16,20},{20,24},{24,28},{28,32},{32,36}... | collective-permute-start | bytes 24584 | tf_op jit(solution)/shard_map/ppermute | solution.py:257
  5.2 6.5 %collective-permute-start.1 = (s32[16,128]{1,0:T(8,128)S(1)}, s32[16,128]{1,0:T(8,128)S(1)}, u32[]{:S(2)}, u32[]{:S(2)}) collective-permute-start(s32[16,128]{1,0:T(8,128)S(1)} %bitcast.12), channel_id=1, source_target_pairs={{4,0},{8,4},{12,8},{16,12},{20,16},{24,20},{28,24},{32,28},{36,32}... | collective-permute-start | bytes 24584 | tf_op jit(solution)/shard_map/ppermute | solution.py:258
  7.2 12.7 %collective-permute-start.2 = (bf16[512,384]{1,0:T(8,128)(2,1)}, bf16[512,384]{1,0:T(8,128)(2,1)S(1)}, u32[]{:S(2)}, u32[]{:S(2)}) collective-permute-start(bf16[512,384]{1,0:T(8,128)(2,1)} %stem_hbm.1), channel_id=1, source_target_pairs={{0,1},{1,0},{2,3},{3,2},{4,5},{5,4},{6,7},{7,6},{8,9},{9,8},{10,11... | collective-permute-start | bytes 1179656 | tf_op jit(solution)/shard_map/ppermute | solution.py:261
  8.4 10.1 %collective-permute-start.4 = (bf16[256,384]{1,0:T(8,128)(2,1)S(1)}, bf16[256,384]{1,0:T(8,128)(2,1)S(1)}, u32[]{:S(2)}, u32[]{:S(2)}) collective-permute-start(bf16[256,384]{1,0:T(8,128)(2,1)S(1)} %get-tuple-element.42), channel_id=1, source_target_pairs={{0,130},{1,131},{2,128},{3,129},{128,2},{129,3},{130,0},{131,1},{4... | collective-permute-start | bytes 589832 | tf_op jit(solution)/shard_map/ppermute | solution.py:260
  11.5 7.0 %collective-permute-start.3 = (bf16[256,384]{1,0:T(8,128)(2,1)S(1)}, bf16[256,384]{1,0:T(8,128)(2,1)S(1)}, u32[]{:S(2)}, u32[]{:S(2)}) collective-permute-start(bf16[256,384]{1,0:T(8,128)(2,1)S(1)} %get-tuple-element.43), channel_id=1, source_target_pairs={{0,2},{1,3},{2,0},{3,1},{4,6},{5,7},{6,4},{7,5},{8,10},{9,11},{10,... | collective-permute-start | bytes 589832 | tf_op jit(solution)/shard_map/ppermute | solution.py:259
  11.7 1.0 copy-start.5
  12.7 0.9 copy-start.7
  14.7 0.8 copy-start
  18.5 1.4 %collective-permute-start.5 = (bf16[256,384]{1,0:T(8,128)(2,1)S(1)}, bf16[256,384]{1,0:T(8,128)(2,1)S(1)}, u32[]{:S(2)}, u32[]{:S(2)}) collective-permute-start(bf16[256,384]{1,0:T(8,128)(2,1)S(1)} %collective-permute-done.3.w2a), channel_id=1, source_target_pairs={{0,1},{1,0},{2,3},{3,2},{4,5},{5,4},{6,7},{7,6},{8,9},{9,8},{10,11... | collective-permute-start | bytes 589832 | tf_op jit(solution)/shard_map/ppermute | solution.py:272
  18.5 1.7 %collective-permute-start.6 = (bf16[256,384]{1,0:T(8,128)(2,1)S(1)}, bf16[256,384]{1,0:T(8,128)(2,1)S(1)}, u32[]{:S(2)}, u32[]{:S(2)}) collective-permute-start(bf16[256,384]{1,0:T(8,128)(2,1)S(1)} %collective-permute-done.4.w2b), channel_id=1, source_target_pairs={{0,1},{1,0},{2,3},{3,2},{4,5},{5,4},{6,7},{7,6},{8,9},{9,8},{10,11... | collective-permute-start | bytes 589832 | tf_op jit(solution)/shard_map/ppermute | solution.py:274
  27.3 7.9 %collective-permute-start.8 = (bf16[304,384]{1,0:T(8,128)(2,1)S(1)}, bf16[304,384]{1,0:T(8,128)(2,1)S(1)}, u32[]{:S(2)}, u32[]{:S(2)}) collective-permute-start(bf16[304,384]{1,0:T(8,128)(2,1)S(1)} %get-tuple-element.26.refs_0_), channel_id=1, source_target_pairs={{0,2},{1,3},{2,0},{3,1},{4,6},{5,7},{6,4},{7,5},{8,10},{9,11},{10,... | collective-permute-start | bytes 700424 | tf_op jit(solution)/shard_map/ppermute | solution.py:286
  27.6 8.1 %collective-permute-start.7 = (bf16[304,384]{1,0:T(8,128)(2,1)S(1)}, bf16[304,384]{1,0:T(8,128)(2,1)S(1)}, u32[]{:S(2)}, u32[]{:S(2)}) collective-permute-start(bf16[304,384]{1,0:T(8,128)(2,1)S(1)} %get-tuple-element.26.refs_0_), channel_id=1, source_target_pairs={{0,1},{1,0},{2,3},{3,2},{4,5},{5,4},{6,7},{7,6},{8,9},{9,8},{10,11... | collective-permute-start | bytes 700424 | tf_op jit(solution)/shard_map/ppermute | solution.py:286
  35.2 1.5 %collective-permute-start.9 = (bf16[304,384]{1,0:T(8,128)(2,1)S(1)}, bf16[304,384]{1,0:T(8,128)(2,1)S(1)}, u32[]{:S(2)}, u32[]{:S(2)}) collective-permute-start(bf16[304,384]{1,0:T(8,128)(2,1)S(1)} %collective-permute-done.8.refs_2_), channel_id=1, source_target_pairs={{0,1},{1,0},{2,3},{3,2},{4,5},{5,4},{6,7},{7,6},{8,9},{9,8},{10,11... | collective-permute-start | bytes 700424 | tf_op jit(solution)/shard_map/ppermute | solution.py:291
  35.2 7.3 %collective-permute-start.13 = (bf16[240,384]{1,0:T(8,128)(2,1)S(1)}, bf16[240,384]{1,0:T(8,128)(2,1)S(1)}, u32[]{:S(2)}, u32[]{:S(2)}) collective-permute-start(bf16[240,384]{1,0:T(8,128)(2,1)S(1)} %zero_back.1.refs_4_), channel_id=1, source_target_pairs={{0,2},{1,3},{2,0},{3,1},{4,6},{5,7},{6,4},{7,5},{8,10},{9,11},{10,... | collective-permute-start | bytes 552968 | tf_op jit(solution)/shard_map/ppermute | solution.py:286
  35.5 8.2 %collective-permute-start.12 = (bf16[240,384]{1,0:T(8,128)(2,1)S(1)}, bf16[240,384]{1,0:T(8,128)(2,1)S(1)}, u32[]{:S(2)}, u32[]{:S(2)}) collective-permute-start(bf16[240,384]{1,0:T(8,128)(2,1)S(1)} %zero_back.1.refs_4_), channel_id=1, source_target_pairs={{0,1},{1,0},{2,3},{3,2},{4,5},{5,4},{6,7},{7,6},{8,9},{9,8},{10,11... | collective-permute-start | bytes 552968 | tf_op jit(solution)/shard_map/ppermute | solution.py:286
  42.5 9.4 %copy-start.1 = (bf16[1,512,384]{2,1,0:T(8,128)(2,1)S(1)}, bf16[1,512,384]{2,1,0:T(8,128)(2,1)}, u32[]{:S(2)}) copy-start(bf16[1,512,384]{2,1,0:T(8,128)(2,1)} %param.11) | copy-start | bytes 1179652
  42.5 1.5 %collective-permute-start.14 = (bf16[240,384]{1,0:T(8,128)(2,1)S(1)}, bf16[240,384]{1,0:T(8,128)(2,1)S(1)}, u32[]{:S(2)}, u32[]{:S(2)}) collective-permute-start(bf16[240,384]{1,0:T(8,128)(2,1)S(1)} %collective-permute-done.13.refs_6_), channel_id=1, source_target_pairs={{0,1},{1,0},{2,3},{3,2},{4,5},{5,4},{6,7},{7,6},{8,9},{9,8},{10,11... | collective-permute-start | bytes 552968 | tf_op jit(solution)/shard_map/ppermute | solution.py:291
  42.7 7.7 %collective-permute-start.11 = (bf16[288,384]{1,0:T(8,128)(2,1)S(1)}, bf16[288,384]{1,0:T(8,128)(2,1)S(1)}, u32[]{:S(2)}, u32[]{:S(2)}) collective-permute-start(bf16[288,384]{1,0:T(8,128)(2,1)S(1)} %get-tuple-element.29.refs_0_), channel_id=1, source_target_pairs={{0,2},{1,3},{2,0},{3,1},{4,6},{5,7},{6,4},{7,5},{8,10},{9,11},{10,... | collective-permute-start | bytes 663560 | tf_op jit(solution)/shard_map/ppermute | solution.py:286
  43.7 7.8 %collective-permute-start.10 = (bf16[288,384]{1,0:T(8,128)(2,1)S(1)}, bf16[288,384]{1,0:T(8,128)(2,1)S(1)}, u32[]{:S(2)}, u32[]{:S(2)}) collective-permute-start(bf16[288,384]{1,0:T(8,128)(2,1)S(1)} %get-tuple-element.29.refs_0_), channel_id=1, source_target_pairs={{0,1},{1,0},{2,3},{3,2},{4,5},{5,4},{6,7},{7,6},{8,9},{9,8},{10,11... | collective-permute-start | bytes 663560 | tf_op jit(solution)/shard_map/ppermute | solution.py:286
  50.4 8.0 %copy-start.2 = (bf16[288,384]{1,0:T(8,128)(2,1)}, bf16[288,384]{1,0:T(8,128)(2,1)S(1)}, u32[]{:S(2)}) copy-start(bf16[288,384]{1,0:T(8,128)(2,1)S(1)} %collective-permute-done.11.refs_2_) | copy-start | bytes 663556
  50.5 1.5 %collective-permute-start.15 = (bf16[288,384]{1,0:T(8,128)(2,1)S(1)}, bf16[288,384]{1,0:T(8,128)(2,1)S(1)}, u32[]{:S(2)}, u32[]{:S(2)}) collective-permute-start(bf16[288,384]{1,0:T(8,128)(2,1)S(1)} %collective-permute-done.11.refs_2_), channel_id=1, source_target_pairs={{0,1},{1,0},{2,3},{3,2},{4,5},{5,4},{6,7},{7,6},{8,9},{9,8},{10,11... | collective-permute-start | bytes 663560 | tf_op jit(solution)/shard_map/ppermute | solution.py:291
  50.5 8.0 %collective-permute-start.17 = (bf16[256,384]{1,0:T(8,128)(2,1)S(1)}, bf16[256,384]{1,0:T(8,128)(2,1)S(1)}, u32[]{:S(2)}, u32[]{:S(2)}) collective-permute-start(bf16[256,384]{1,0:T(8,128)(2,1)S(1)} %one_back.1.refs_4_), channel_id=1, source_target_pairs={{0,2},{1,3},{2,0},{3,1},{4,6},{5,7},{6,4},{7,5},{8,10},{9,11},{10,... | collective-permute-start | bytes 589832 | tf_op jit(solution)/shard_map/ppermute | solution.py:286
  51.2 7.7 %collective-permute-start.16 = (bf16[256,384]{1,0:T(8,128)(2,1)S(1)}, bf16[256,384]{1,0:T(8,128)(2,1)S(1)}, u32[]{:S(2)}, u32[]{:S(2)}) collective-permute-start(bf16[256,384]{1,0:T(8,128)(2,1)S(1)} %one_back.1.refs_4_), channel_id=1, source_target_pairs={{0,1},{1,0},{2,3},{3,2},{4,5},{5,4},{6,7},{7,6},{8,9},{9,8},{10,11... | collective-permute-start | bytes 589832 | tf_op jit(solution)/shard_map/ppermute | solution.py:286
  51.9 6.5 %copy-start.3 = (bf16[288,384]{1,0:T(8,128)(2,1)}, bf16[288,384]{1,0:T(8,128)(2,1)S(1)}, u32[]{:S(2)}) copy-start(bf16[288,384]{1,0:T(8,128)(2,1)S(1)} %collective-permute-done.15.refs_3_) | copy-start | bytes 663556
  58.4 1.7 %collective-permute-start.18 = (bf16[256,384]{1,0:T(8,128)(2,1)S(1)}, bf16[256,384]{1,0:T(8,128)(2,1)S(1)}, u32[]{:S(2)}, u32[]{:S(2)}) collective-permute-start(bf16[256,384]{1,0:T(8,128)(2,1)S(1)} %collective-permute-done.17.refs_6_), channel_id=1, source_target_pairs={{0,1},{1,0},{2,3},{3,2},{4,5},{5,4},{6,7},{7,6},{8,9},{9,8},{10,11... | collective-permute-start | bytes 589832 | tf_op jit(solution)/shard_map/ppermute | solution.py:291
  60.2 41.8 %copy-start.6 = (bf16[384,384]{1,0:T(8,128)(2,1)S(1)}, bf16[384,384]{1,0:T(8,128)(2,1)}, u32[]{:S(2)}) copy-start(bf16[384,384]{1,0:T(8,128)(2,1)} %weights.1) | copy-start | bytes 884740
  64.9 5.5 %collective-permute-start.19 = (bf16[96,384]{1,0:T(8,128)(2,1)S(1)}, bf16[96,384]{1,0:T(8,128)(2,1)S(1)}, u32[]{:S(2)}, u32[]{:S(2)}) collective-permute-start(bf16[96,384]{1,0:T(8,128)(2,1)S(1)} %get-tuple-element.39), channel_id=1, source_target_pairs={{0,32},{4,36},{8,40},{12,44},{16,48},{20,52},{24,56},{28,60},{32,0... | collective-permute-start | bytes 221192 | tf_op jit(solution)/shard_map/ppermute | solution.py:388
  66.5 6.7 %collective-permute-start.20 = (bf16[96,384]{1,0:T(8,128)(2,1)S(1)}, bf16[96,384]{1,0:T(8,128)(2,1)S(1)}, u32[]{:S(2)}, u32[]{:S(2)}) collective-permute-start(bf16[96,384]{1,0:T(8,128)(2,1)S(1)} %get-tuple-element.40), channel_id=1, source_target_pairs={{0,4},{4,0},{8,12},{12,8},{16,20},{20,16},{24,28},{28,24},{32,36},... | collective-permute-start | bytes 221192 | tf_op jit(solution)/shard_map/ppermute | solution.py:389
  70.4 5.3 %collective-permute-start.21 = (bf16[96,384]{1,0:T(8,128)(2,1)S(1)}, bf16[96,384]{1,0:T(8,128)(2,1)S(1)}, u32[]{:S(2)}, u32[]{:S(2)}) collective-permute-start(bf16[96,384]{1,0:T(8,128)(2,1)S(1)} %get-tuple-element.41), channel_id=1, source_target_pairs={{0,36},{4,32},{8,44},{12,40},{16,52},{20,48},{24,60},{28,56},{32,4... | collective-permute-start | bytes 221192 | tf_op jit(solution)/shard_map/ppermute | solution.py:390
  75.7 6.7 %collective-permute-start.24 = (bf16[96,384]{1,0:T(8,128)(2,1)S(1)}, bf16[96,384]{1,0:T(8,128)(2,1)S(1)}, u32[]{:S(2)}, u32[]{:S(2)}) collective-permute-start(bf16[96,384]{1,0:T(8,128)(2,1)S(1)} %add_convert_fusion.3), channel_id=1, source_target_pairs={{0,124},{4,104},{8,100},{12,112},{16,108},{20,120},{24,116},{28,96... | collective-permute-start | bytes 221192 | tf_op jit(solution)/shard_map/ppermute | solution.py:395
  78.3 4.4 %collective-permute-start.23 = (bf16[96,384]{1,0:T(8,128)(2,1)S(1)}, bf16[96,384]{1,0:T(8,128)(2,1)S(1)}, u32[]{:S(2)}, u32[]{:S(2)}) collective-permute-start(bf16[96,384]{1,0:T(8,128)(2,1)S(1)} %add_convert_fusion.3), channel_id=1, source_target_pairs={{0,28},{4,8},{8,4},{12,16},{16,12},{20,24},{24,20},{28,0},{32,60},... | collective-permute-start | bytes 221192 | tf_op jit(solution)/shard_map/ppermute | solution.py:394
  79.3 5.6 %collective-permute-start.22 = (bf16[96,384]{1,0:T(8,128)(2,1)S(1)}, bf16[96,384]{1,0:T(8,128)(2,1)S(1)}, u32[]{:S(2)}, u32[]{:S(2)}) collective-permute-start(bf16[96,384]{1,0:T(8,128)(2,1)S(1)} %add_convert_fusion.3), channel_id=1, source_target_pairs={{0,96},{4,100},{8,104},{12,108},{16,112},{20,116},{24,120},{28,124... | collective-permute-start | bytes 221192 | tf_op jit(solution)/shard_map/ppermute | solution.py:393
  84.9 5.9 %collective-permute-start.25 = (bf16[96,384]{1,0:T(8,128)(2,1)S(1)}, bf16[96,384]{1,0:T(8,128)(2,1)S(1)}, u32[]{:S(2)}, u32[]{:S(2)}) collective-permute-start(bf16[96,384]{1,0:T(8,128)(2,1)S(1)} %add_convert_fusion.2), channel_id=1, source_target_pairs={{0,128},{128,0},{1,129},{129,1},{2,130},{130,2},{3,131},{131,3},{4... | collective-permute-start | bytes 221192 | tf_op jit(solution)/shard_map/ppermute | solution.py:398
  90.9 7.5 %collective-permute-start.26 = (bf16[96,384]{1,0:T(8,128)(2,1)S(1)}, bf16[96,384]{1,0:T(8,128)(2,1)S(1)}, u32[]{:S(2)}, u32[]{:S(2)}) collective-permute-start(bf16[96,384]{1,0:T(8,128)(2,1)S(1)} %add_convert_fusion.1), channel_id=1, source_target_pairs={{0,12},{4,24},{8,20},{12,0},{16,28},{20,8},{24,4},{28,16},{32,44},... | collective-permute-start | bytes 221192 | tf_op jit(solution)/shard_map/ppermute | solution.py:400
  98.4 5.4 %collective-permute-start.29 = (bf16[96,384]{1,0:T(8,128)(2,1)S(1)}, bf16[96,384]{1,0:T(8,128)(2,1)S(1)}, u32[]{:S(2)}, u32[]{:S(2)}) collective-permute-start(bf16[96,384]{1,0:T(8,128)(2,1)S(1)} %add_convert_fusion.p0), channel_id=1, source_target_pairs={{0,36},{4,32},{8,44},{12,40},{16,52},{20,48},{24,60},{28,56},{32,4... | collective-permute-start | bytes 221192 | tf_op jit(solution)/shard_map/ppermute | solution.py:404
  98.5 6.0 %collective-permute-start.28 = (bf16[96,384]{1,0:T(8,128)(2,1)S(1)}, bf16[96,384]{1,0:T(8,128)(2,1)S(1)}, u32[]{:S(2)}, u32[]{:S(2)}) collective-permute-start(bf16[96,384]{1,0:T(8,128)(2,1)S(1)} %add_convert_fusion.p0), channel_id=1, source_target_pairs={{0,32},{4,36},{8,40},{12,44},{16,48},{20,52},{24,56},{28,60},{32,0... | collective-permute-start | bytes 221192 | tf_op jit(solution)/shard_map/ppermute | solution.py:402
  101.3 4.4 %collective-permute-start.27 = (bf16[96,384]{1,0:T(8,128)(2,1)S(1)}, bf16[96,384]{1,0:T(8,128)(2,1)S(1)}, u32[]{:S(2)}, u32[]{:S(2)}) collective-permute-start(bf16[96,384]{1,0:T(8,128)(2,1)S(1)} %add_convert_fusion.p0), channel_id=1, source_target_pairs={{0,4},{4,0},{8,12},{12,8},{16,20},{20,16},{24,28},{28,24},{32,36},... | collective-permute-start | bytes 221192 | tf_op jit(solution)/shard_map/ppermute | solution.py:403

commit v3 on v2

--- a/solution.py
+++ b/solution.py
@@ -48,11 +48,9 @@
         norm_rows(ids, layer, read(first, rows), gains, normed, at + first)
 
 
-def convolve(normed, weights, copies, at, rows, dilation):
+def convolve(normed, weights, at, rows, dilation):
     update = None
     for t in range(3):
-        for copy in copies[t] if copies else ():
-            copy.wait()
         first = at + (t - 1) * dilation
         part = jnp.dot(
             normed[first : first + rows, :], weights[t], preferred_element_type=jnp.float32
@@ -67,25 +65,28 @@
 
 def start_weights(ids, layer, w_hbm, out, sems):
     width = out.shape[2]
-    taps = []
+    copies = []
     for t in range(3):
-        taps.append([])
         for k in range(4):
-            copy = pltpu.make_async_copy(
-                w_hbm.at[layer, t, pl.ds((ids[0] ^ k) * width, width), :],
-                out.at[t, pl.ds(k * width, width), :],
-                sems.at[t, k],
+            copies.append(
+                pltpu.make_async_copy(
+                    w_hbm.at[layer, t, pl.ds((ids[0] ^ k) * width, width), :],
+                    out.at[t, pl.ds(k * width, width), :],
+                    sems.at[t, k],
+                )
             )
-            copy.start()
-            taps[-1].append(copy)
-    return taps
-
-
-def one_hot(bins, count, ids, before, own, after, stem_hbm, onehot, stem, sem):
-    copy = pltpu.make_async_copy(stem_hbm, stem, sem)
-    copy.start()
+            copies[-1].start()
+    return copies
+
+
+def wait_all(copies):
+    for copy in copies:
+        copy.wait()
+
+
+def one_hot(bins, count, ids, before, own, after, w_hbm, onehot, weights, sems):
+    copies = start_weights(ids, 0, w_hbm, weights, sems)
     letters = jnp.concatenate([before[...], own[...], after[...]], axis=0)
-    letters = letters.astype(jnp.float32).astype(jnp.bfloat16)
     lane = lax.broadcasted_iota(jnp.int32, (PATCH, 4 * PATCH), 1)
     row = lax.broadcasted_iota(jnp.int32, (PATCH, 4 * PATCH), 0)
     spread = jnp.where(lane // 4 == row, 1.0, 0.0).astype(jnp.bfloat16)
@@ -93,16 +94,16 @@
     base = (lax.broadcasted_iota(jnp.int32, (1, 4 * PATCH), 1) % 4).astype(jnp.float32)
     inside = in_sequence(ids, 0, bins + 2 * HALO, bins, count)
     onehot[...] = (jnp.where(repeated == base, 1.0, 0.0) * inside).astype(jnp.bfloat16)
-    copy.wait()
-
-
-def first_layer(span, bins, count, ids, onehot, own, w1, w2a, w2b, w3a, w3b, gains, w_in, out, *refs):
+    wait_all(copies)
+
+
+def first_layer(span, bins, count, ids, onehot, own_a, own_b, w1, w2a, w2b, w3a, w3b, gains, weights, *refs):
     low, high = span
     if low == 0:
-        weights, normed, stream, sems = refs
-        copies = start_weights(ids, 0, w_in, weights, sems)
+        copies, (out, normed, stream) = [], refs
     else:
-        weights, copies, (normed, stream) = w_in, None, refs
+        w_hbm, out, later, normed, stream, sems = refs
+        copies = start_weights(ids, 1, w_hbm, later, sems)
     width = out.shape[1]
     first, last = max(low - HALO, 0), min(high + HALO, bins + 2 * HALO)
     rows = last - first
@@ -110,7 +111,7 @@
     clear(normed, PAD + rows, PAD)
     stem = jnp.concatenate(
         [
-            own[...],
+            jnp.concatenate([own_a[...], own_b[...]], axis=0),
             w1[...],
             jnp.concatenate([w2a[...], w2b[...]], axis=0),
             jnp.concatenate([w3a[...], w3b[...]], axis=0),
@@ -125,24 +126,24 @@
         return [stream[at : at + n, k * width : (k + 1) * width] for k in range(4)]
 
     norm_segment(ids, 0, read, rows, gains, normed, PAD)
-    update = convolve(normed, weights, copies, PAD + low - first, high - low, FIRST_DILATION0)
+    update = convolve(normed, weights, PAD + low - first, high - low, FIRST_DILATION0)
     total = stream[low - first : high - first, 0:width].astype(jnp.float32) + update
     inside = in_sequence(ids, low, high - low, bins, count)
     out[...] = (total * inside).astype(jnp.bfloat16)
+    wait_all(copies)
 
 
 def front(layer, dilation, span, bins, count, ids, *refs):
-    pieces, (gains, w_hbm, out, weights, normed, sems) = refs[:4], refs[4:]
+    pieces, (gains, weights, out, normed) = refs[:4], refs[4:]
     low, high = span
     rows = high + HALO
-    copies = start_weights(ids, layer, w_hbm, weights, sems)
     clear(normed, 0, PAD)
 
     def read(at, n):
         return [p[at : at + n, :] for p in pieces]
 
     norm_segment(ids, layer, read, rows, gains, normed, PAD)
-    update = convolve(normed, weights, copies, PAD + low, high - low, dilation)
+    update = convolve(normed, weights, PAD + low, high - low, dilation)
     total = pieces[0][low:high, :].astype(jnp.float32) + update
     if count:
         total = total * in_sequence(ids, low, high - low, bins, count)
@@ -150,7 +151,13 @@
 
 
 def back(layer, dilation, span, bins, count, ids, *refs):
-    fronts, backs, (gains, weights, out, normed) = refs[:4], refs[4:8], refs[8:]
+    fronts, backs, (gains, weights) = refs[:4], refs[4:8], refs[8:10]
+    copies = []
+    if len(refs) == 15:
+        w_hbm, out, later, normed, sems = refs[10:]
+        copies = start_weights(ids, layer + 1, w_hbm, later, sems)
+    else:
+        out, normed = refs[10:]
     low, high = span
     first = low - HALO
     joint = fronts[0].shape[0]
@@ -165,12 +172,13 @@
 
     norm_segment(ids, layer, read_front, joint - first, gains, normed, PAD)
     norm_segment(ids, layer, read_back, backs[0].shape[0], gains, normed, PAD + joint - first)
-    update = convolve(normed, weights, None, PAD + HALO, high - low, dilation)
+    update = convolve(normed, weights, PAD + HALO, high - low, dilation)
     own = jnp.concatenate([fronts[0][low:joint, :], backs[0][0 : high - joint, :]], axis=0)
     total = own.astype(jnp.float32) + update
     if count:
         total = total * in_sequence(ids, low, high - low, bins, count)
     out[...] = total.astype(jnp.bfloat16)
+    wait_all(copies)
 
 
 def gradient(stream, upstream):
@@ -180,8 +188,8 @@
 
 
 def last_front(span, bins, ids, *refs):
-    refs, (upstream, out, grad, weights, normed, sems) = refs[:6], refs[6:]
-    front(2, 4 * FIRST_DILATION0, span, bins, 0, ids, *refs, out, weights, normed, sems)
+    refs, (upstream, out, grad, normed) = refs[:6], refs[6:]
+    front(2, 4 * FIRST_DILATION0, span, bins, 0, ids, *refs, out, normed)
     low, high = span
     grad[...] = gradient(out[...], upstream[low - HALO : high - HALO, :])
 
@@ -220,7 +228,7 @@
     return [(i, partner(i)) for i in range(size)]
 
 
-def call(name, kernel, outs, in_specs, scratch=(), flops=0, megabytes=52):
+def call(name, kernel, outs, in_specs, scratch=(), flops=0, megabytes=40):
     many = isinstance(outs, (list, tuple))
     return pl.pallas_call(
         kernel,
@@ -250,28 +258,29 @@
         lax.ppermute, axis_name=("section", "chan"), perm=pairs(8, lambda i: i ^ 6)
     )
 
-    letters = bases.reshape(bins, PATCH)
+    letters = lax.optimization_barrier(bases.reshape(bins, PATCH).astype(bf16))
     up = [(i, i + 1) for i in range(seq_count - 1)]
     down = [(j, i) for i, j in up]
     half = stem.shape[0] // 2
+    stem_a, stem_b = lax.optimization_barrier((stem[:half], stem[half:]))
+    w2a = across(stem_a)
+    w2b = far(stem_b)
+    w1 = other_core(stem)
     before = lax.ppermute(letters[bins - HALO :], "seq", up)
     after = lax.ppermute(letters[:HALO], "seq", down)
-    w2a = across(stem[:half])
-    w2b = far(stem[half:])
-    w1 = other_core(stem)
-    onehot, stem = call(
+    w2a, before, after = lax.optimization_barrier((w2a, before, after))
+    w3a = other_core(w2a)
+    w3b = other_core(w2b)
+    layer_weights = jax.ShapeDtypeStruct((3, 4 * width, width), bf16)
+    weight_sems = pltpu.SemaphoreType.DMA((3, 4))
+    onehot, weights = call(
         "one_hot",
         functools.partial(one_hot, bins, count),
-        [jax.ShapeDtypeStruct((rows, 4 * PATCH), bf16), jax.ShapeDtypeStruct(stem.shape, bf16)],
+        [jax.ShapeDtypeStruct((rows, 4 * PATCH), bf16), layer_weights],
         [SMEM] + [VMEM] * 3 + [HBM],
-        [pltpu.SemaphoreType.DMA],
-        megabytes=8,
+        [weight_sems],
         flops=10**9,
-    )(ids, before, letters, after, stem)
-    w2a = tie(w2a, before, after)
-    w3a = other_core(w2a)
-    w2b = tie(w2b, onehot)
-    w3b = other_core(w2b)
+    )(ids, before, letters, after, conv_weight)
 
     def shape(n):
         return jax.ShapeDtypeStruct((n, width), bf16)
@@ -291,60 +300,58 @@
         return own, beside, remote, other_core(remote)
 
     cut = bins // 2 + 3 * HALO
-    layer_weights = jax.ShapeDtypeStruct((3, 4 * width, width), bf16)
-    weight_sems = pltpu.SemaphoreType.DMA((3, 4))
-    inputs = (onehot, stem, w1, w2a, w2b, w3a, w3b, gains)
-    part, weights = call(
+    inputs = (onehot, stem_a, stem_b, w1, w2a, w2b, w3a, w3b, gains, weights)
+    part = call(
         "zero_front",
         functools.partial(first_layer, (0, cut), bins, count),
-        [shape(cut), layer_weights],
-        [SMEM] + [VMEM] * 8 + [HBM],
-        [normed(cut + HALO), pltpu.VMEM((cut + HALO, 4 * width), bf16), weight_sems],
+        shape(cut),
+        [SMEM] + [VMEM] * 10,
+        [normed(cut + HALO), pltpu.VMEM((cut + HALO, 4 * width), bf16)],
         flops=work(cut),
-    )(ids, *inputs, conv_weight)
+    )(ids, *inputs)
     sent_front = exchange(part)
-    part = call(
+    part, weights = call(
         "zero_back",
         functools.partial(first_layer, (cut, rows), bins, count),
-        shape(rows - cut),
-        [SMEM] + [VMEM] * 9,
-        [normed(rows - cut + HALO), pltpu.VMEM((rows - cut + HALO, 4 * width), bf16)],
+        [shape(rows - cut), layer_weights],
+        [SMEM] + [VMEM] * 10 + [HBM],
+        [normed(rows - cut + HALO), pltpu.VMEM((rows - cut + HALO, 4 * width), bf16), weight_sems],
         flops=work(rows - cut),
-    )(ids, *inputs, weights)
+    )(ids, *inputs, conv_weight)
     sent_back = exchange(part)
     fronts = finish(sent_front, part)
 
     cut = cut - HALO
-    part, weights = call(
+    part = call(
         "one_front",
         functools.partial(front, 1, 2 * FIRST_DILATION0, (0, cut), bins, count),
-        [shape(cut), layer_weights],
-        [SMEM] + [VMEM] * 5 + [HBM],
-        [normed(cut + HALO), weight_sems],
+        shape(cut),
+        [SMEM] + [VMEM] * 6,
+        [normed(cut + HALO)],
         flops=work(cut),
-    )(ids, *fronts, gains, conv_weight)
+    )(ids, *fronts, gains, weights)
     sent_front = exchange(part)
     backs = finish(sent_back, part)
-    part = call(
+    part, weights = call(
         "one_back",
         functools.partial(back, 1, 2 * FIRST_DILATION0, (cut, rows), bins, count),
-        shape(rows - cut),
-        [SMEM] + [VMEM] * 10,
-        [normed(rows - cut + HALO)],
+        [shape(rows - cut), layer_weights],
+        [SMEM] + [VMEM] * 10 + [HBM],
+        [normed(rows - cut + HALO), weight_sems],
         flops=work(rows - cut),
-    )(ids, *fronts, *backs, gains, weights)
+    )(ids, *fronts, *backs, gains, weights, conv_weight)
     sent_back = exchange(part)
     fronts = finish(sent_front, part)
 
     cut = cut - HALO
-    front_rows, front_grad, weights = call(
+    front_rows, front_grad = call(
         "two_front",
         functools.partial(last_front, (HALO, cut), bins),
-        [shape(cut - HALO), jax.ShapeDtypeStruct((width, width), f32), layer_weights],
-        [SMEM] + [VMEM] * 5 + [HBM, VMEM],
-        [normed(cut + HALO), weight_sems],
+        [shape(cut - HALO), jax.ShapeDtypeStruct((width, width), f32)],
+        [SMEM] + [VMEM] * 7,
+        [normed(cut + HALO)],
         flops=work(cut - HALO),
-    )(ids, *fronts, gains, conv_weight, upstream[0])
+    )(ids, *fronts, gains, weights, upstream[0])
     backs = finish(sent_back, front_rows)
     back_rows, g0, g1, g2, g3 = call(
         "two_back",

time: 107 us -> 103 us (0.963)
  Pallas kernels: 36 us -> 25.8 us
  waiting for transfers between devices: 33.8 us -> 39.9 us
  local copies, waits for them, and re-layouts: 4.55 us -> 1.08 us
  starting transfers between devices: 31.7 us -> 33.5 us
  other arithmetic: 0.2 us -> 1.85 us
    ppermute x8, waiting for transfers between devices: 5.53 us -> 10.3 us  [exchange(): return (own, other_core(own), across(own))]
    ppermute x1, starting transfers between devices: 1.58 us -> 5.61 us  [body(): r2 = over(flip, same)(g2)]
    pallas_call x1, Pallas kernels: 6.47 us -> 2.73 us  [body(): call('two_front', functools.partial(last_front, (HALO, cut), bins), [shap...]
    pallas_call x1, Pallas kernels: 7.03 us -> 3.35 us  [body(): call('zero_front', functools.partial(first_layer, (0, cut), bins, count),...]
    pallas_call x1, Pallas kernels: 5.82 us -> 2.62 us  [body(): call('one_front', functools.partial(front, 1, 2 * FIRST_DILATION0, (0, cu...]
    ppermute x2, waiting for transfers between devices: 2.99 us -> 0.01 us  [the longest x1 0.01 us: body(): w2a = across(stem_a)]
    ppermute x1, waiting for transfers between devices: 4.24 us -> 7.1 us  [body(): other = over(same, zs_far)(own)]
    unnamed x16 -> x6, local copies, waits for them, and re-layouts: 2.76 us -> 0.01 us
  transfers between devices with their start and end apart: 30 -> 30, of which waited for: 19 -> 19; matrix products, arithmetic and copies ran while one was open for 1% -> 3% of each run, Pallas kernels for 21% -> 18%
where the time goes in v3:
time: 103 us
  waiting for transfers between devices  39.9 us (39%)
  starting transfers between devices  33.5 us (33%)
  Pallas kernels  25.8 us (25%)
  other arithmetic  1.85 us (2%)
  local copies, waits for them, and re-layouts  1.08 us (1%)
    ppermute x8, waiting for transfers between devices, exchange(): return (own, other_core(own), across(own))  10.3 us
    ppermute x1, waiting for transfers between devices, body(): other = over(same, zs_far)(own)  7.1 us
    ppermute x1, starting transfers between devices, body(): r2 = over(flip, same)(g2)  5.61 us
    ppermute x1, waiting for transfers between devices, body(): other = lax.ppermute(own, 'section', [(0, 1), (1, 0)])  5.08 us
    pallas_call x1, Pallas kernels, body(): call('zero_back', functools.partial(first_layer, (cut, rows), bins, count...  4.7 us
    pallas_call x1, Pallas kernels, body(): call('one_back', functools.partial(back, 1, 2 * FIRST_DILATION0, (cut, ro...  4.41 us
    ppermute x1, starting transfers between devices, body(): r1 = over(same, flip)(g1)  4.13 us
    ppermute x1, starting transfers between devices, body(): before = lax.ppermute(letters[bins - HALO:], 'seq', up)  3.83 us
  transfers between devices with their start and end apart: 30, of which 19 were waited for; matrix products, arithmetic and copies ran while one was open for 3% of the time, Pallas kernels for 18%

profile of v3, /device:TPU:32, one launch (start us, length us, event | category | flops | bytes accessed | tf_op | source)
XLA Modules:
  0.0 103.0 jit_solution(433902041432087075)
XLA Ops:
  0.7 1.1 %fusion = (bf16[256,384]{1,0:T(8,128)(2,1)S(1)}, bf16[256,384]{1,0:T(8,128)(2,1)S(1)}) fusion(bf16[512,384]{1,0:T(8,128)(2,1)} %param.7), kind=kLoop, calls=%fused_computation.6 | loop fusion | bytes 786432 | tf_op jit(solution)/shard_map/slice | solution.py:265
  1.8 1.7 %collective-permute-start = (bf16[256,384]{1,0:T(8,128)(2,1)S(1)}, bf16[256,384]{1,0:T(8,128)(2,1)S(1)}, u32[]{:S(2)}, u32[]{:S(2)}) collective-permute-start(bf16[256,384]{1,0:T(8,128)(2,1)S(1)} %get-tuple-element.24.own_a), channel_id=1, source_target_pairs={{0,2},{1,3},{2,0},{3,1},{4,6},{5,7},{6,4},{7,5},{8,10},{9,11},{10,... | collective-permute-start | bytes 589832 | tf_op jit(solution)/shard_map/ppermute | solution.py:266
  3.5 2.2 %collective-permute-start.4 = (bf16[256,384]{1,0:T(8,128)(2,1)S(1)}, bf16[256,384]{1,0:T(8,128)(2,1)S(1)}, u32[]{:S(2)}, u32[]{:S(2)}) collective-permute-start(bf16[256,384]{1,0:T(8,128)(2,1)S(1)} %get-tuple-element.28.own_b), channel_id=1, source_target_pairs={{0,130},{1,131},{2,128},{3,129},{128,2},{129,3},{130,0},{131,1},{4... | collective-permute-start | bytes 589832 | tf_op jit(solution)/shard_map/ppermute | solution.py:267
  5.6 1.6 %convert_reduce_fusion = bf16[65536]{0:T(1024)(128)(2,1)S(1)} fusion(s32[1,65536]{1,0:T(1,128)} %param.6), kind=kLoop, calls=%fused_computation | loop fusion | flops 65536 | bytes 393216 | tf_op jit(solution)/shard_map/convert_element_type | solution.py:261
  7.3 2.0 %collective-permute-start.2 = (bf16[16,128]{1,0:T(8,128)(2,1)S(1)}, bf16[16,128]{1,0:T(8,128)(2,1)S(1)}, u32[]{:S(2)}, u32[]{:S(2)}) collective-permute-start(bf16[16,128]{1,0:T(8,128)(2,1)S(1)} %get-tuple-element.48), channel_id=1, source_target_pairs={{4,0},{8,4},{12,8},{16,12},{20,16},{24,20},{28,24},{32,28},{36,32}... | collective-permute-start | bytes 12296 | tf_op jit(solution)/shard_map/ppermute | solution.py:270
  9.3 3.8 %collective-permute-start.1 = (bf16[16,128]{1,0:T(8,128)(2,1)S(1)}, bf16[16,128]{1,0:T(8,128)(2,1)S(1)}, u32[]{:S(2)}, u32[]{:S(2)}) collective-permute-start(bf16[16,128]{1,0:T(8,128)(2,1)S(1)} %get-tuple-element.49), channel_id=1, source_target_pairs={{0,4},{4,8},{8,12},{12,16},{16,20},{20,24},{24,28},{28,32},{32,36}... | collective-permute-start | bytes 12296 | tf_op jit(solution)/shard_map/ppermute | solution.py:269
  13.3 1.6 %collective-permute-done.1.before = bf16[16,128]{1,0:T(8,128)(2,1)S(1)} collective-permute-done((bf16[16,128]{1,0:T(8,128)(2,1)S(1)}, bf16[16,128]{1,0:T(8,128)(2,1)S(1)}, u32[]{:S(2)}, u32[]{:S(2)}) %collective-permute-start.1) | collective-permute-done | bytes 4128 | tf_op jit(solution)/shard_map/ppermute | solution.py:269
  14.8 0.5 collective-permute-start.6
  15.4 2.6 %one_hot.1 = (bf16[544,512]{1,0:T(8,128)(2,1)S(1)}, bf16[3,1536,384]{2,1,0:T(8,128)(2,1)S(1)}) custom-call(s32[3]{0:T(128)S(1)} %pad_add_fusion.ids, bf16[16,128]{1,0:T(8,128)(2,1)S(1)} %collective-permute-done.1.before, bf16[512,128]{1,0:T(8,128)(2,1)S(1)} %bitcast.9, bf16[16,128]{1,0:T(8,128)(2,1)S(1)} %collective-permute-done.2.after, ...), custom_call_target="tpu_custom_call" | custom-call | flops 1000000000 | bytes 1048576 | tf_op jit(solution)/shard_map/one_hot/pallas_call | solution.py:276
  18.1 3.3 %zero_front.1.refs_0_ = bf16[304,384]{1,0:T(8,128)(2,1)S(1)} custom-call(s32[3]{0:T(128)S(1)} %pad_add_fusion.ids, bf16[544,512]{1,0:T(8,128)(2,1)S(1)} %get-tuple-element.27.onehot, bf16[256,384]{1,0:T(8,128)(2,1)S(1)} %get-tuple-element.24.own_a, bf16[256,384]{1,0:T(8,128)(2,1)S(1)} %get-tuple-element.28.own_b, ...), custom_call_target="tpu_custom_call" | custom-call | flops 1075838976 | bytes 1048576 | tf_op jit(solution)/shard_map/zero_front/pallas_call | solution.py:304
  21.5 0.8 collective-permute-start.8
  22.2 4.7 %zero_back.1 = (bf16[240,384]{1,0:T(8,128)(2,1)S(1)}, bf16[3,1536,384]{2,1,0:T(8,128)(2,1)S(1)}) custom-call(s32[3]{0:T(128)S(1)} %pad_add_fusion.ids, bf16[544,512]{1,0:T(8,128)(2,1)S(1)} %get-tuple-element.27.onehot, bf16[256,384]{1,0:T(8,128)(2,1)S(1)} %get-tuple-element.24.own_a, bf16[256,384]{1,0:T(8,128)(2,1)S(1)} %get-tuple-element.28.own_b, ...), custom_call_target="tpu_custom_call" | custom-call | flops 849346560 | bytes 1048576 | tf_op jit(solution)/shard_map/zero_back/pallas_call | solution.py:313
  26.9 2.3 %collective-permute-done.8.refs_2_ = bf16[304,384]{1,0:T(8,128)(2,1)S(1)} collective-permute-done((bf16[304,384]{1,0:T(8,128)(2,1)S(1)}, bf16[304,384]{1,0:T(8,128)(2,1)S(1)}, u32[]{:S(2)}, u32[]{:S(2)}) %collective-permute-start.8) | collective-permute-done | bytes 233504 | tf_op jit(solution)/shard_map/ppermute | solution.py:295
  29.2 0.7 collective-permute-start.13
  29.9 0.2 collective-permute-start.12
  30.1 0.6 collective-permute-done.9.refs_3_
  30.7 2.6 %one_front.1.refs_0_ = bf16[288,384]{1,0:T(8,128)(2,1)S(1)} custom-call(s32[3]{0:T(128)S(1)} %pad_add_fusion.ids, bf16[304,384]{1,0:T(8,128)(2,1)S(1)} %zero_front.1.refs_0_, bf16[304,384]{1,0:T(8,128)(2,1)S(1)} %collective-permute-done.7.refs_1_, bf16[304,384]{1,0:T(8,128)(2,1)S(1)} %collective-permute-done.8.refs_2_, ...), custom_call_target="tpu_custom_call" | custom-call | flops 1019215872 | bytes 1048576 | tf_op jit(solution)/shard_map/one_front/pallas_call | solution.py:325
  33.4 2.9 %collective-permute-done.13.refs_6_ = bf16[240,384]{1,0:T(8,128)(2,1)S(1)} collective-permute-done((bf16[240,384]{1,0:T(8,128)(2,1)S(1)}, bf16[240,384]{1,0:T(8,128)(2,1)S(1)}, u32[]{:S(2)}, u32[]{:S(2)}) %collective-permute-start.13) | collective-permute-done | bytes 184352 | tf_op jit(solution)/shard_map/ppermute | solution.py:295
  36.3 0.7 collective-permute-start.11
  37.0 0.2 collective-permute-start.10
  37.2 0.5 collective-permute-done.14.refs_7_
  37.7 4.4 %one_back.1 = (bf16[256,384]{1,0:T(8,128)(2,1)S(1)}, bf16[3,1536,384]{2,1,0:T(8,128)(2,1)S(1)}) custom-call(s32[3]{0:T(128)S(1)} %pad_add_fusion.ids, bf16[304,384]{1,0:T(8,128)(2,1)S(1)} %zero_front.1.refs_0_, bf16[304,384]{1,0:T(8,128)(2,1)S(1)} %collective-permute-done.7.refs_1_, bf16[304,384]{1,0:T(8,128)(2,1)S(1)} %collective-permute-done.8.refs_2_, ...), custom_call_target="tpu_custom_call" | custom-call | flops 905969664 | bytes 1048576 | tf_op jit(solution)/shard_map/one_back/pallas_call | solution.py:335
  42.1 2.0 %collective-permute-done.11.refs_2_ = bf16[288,384]{1,0:T(8,128)(2,1)S(1)} collective-permute-done((bf16[288,384]{1,0:T(8,128)(2,1)S(1)}, bf16[288,384]{1,0:T(8,128)(2,1)S(1)}, u32[]{:S(2)}, u32[]{:S(2)}) %collective-permute-start.11) | collective-permute-done | bytes 221216 | tf_op jit(solution)/shard_map/ppermute | solution.py:295
  44.1 0.7 collective-permute-start.17
  44.8 0.2 collective-permute-start.16
  45.0 0.6 collective-permute-done.15.refs_3_
  45.6 2.7 %two_front.1 = (bf16[256,384]{1,0:T(8,128)(2,1)S(1)}, f32[384,384]{1,0:T(8,128)S(1)}) custom-call(s32[3]{0:T(128)S(1)} %pad_add_fusion.ids, bf16[288,384]{1,0:T(8,128)(2,1)S(1)} %one_front.1.refs_0_, bf16[288,384]{1,0:T(8,128)(2,1)S(1)} %collective-permute-done.10.refs_1_, bf16[288,384]{1,0:T(8,128)(2,1)S(1)} %collective-permute-done.11.refs_2_, ...), custom_call_target="tpu_custom_call" | custom-call | flops 905969664 | bytes 1048576 | tf_op jit(solution)/shard_map/two_front/pallas_call | solution.py:347
  48.3 3.1 %collective-permute-done.17.refs_6_ = bf16[256,384]{1,0:T(8,128)(2,1)S(1)} collective-permute-done((bf16[256,384]{1,0:T(8,128)(2,1)S(1)}, bf16[256,384]{1,0:T(8,128)(2,1)S(1)}, u32[]{:S(2)}, u32[]{:S(2)}) %collective-permute-start.17) | collective-permute-done | bytes 196640 | tf_op jit(solution)/shard_map/ppermute | solution.py:295
  51.5 1.4 %collective-permute-done.18.refs_7_ = bf16[256,384]{1,0:T(8,128)(2,1)S(1)} collective-permute-done((bf16[256,384]{1,0:T(8,128)(2,1)S(1)}, bf16[256,384]{1,0:T(8,128)(2,1)S(1)}, u32[]{:S(2)}, u32[]{:S(2)}) %collective-permute-start.18) | collective-permute-done | bytes 196640 | tf_op jit(solution)/shard_map/ppermute | solution.py:300
  52.9 2.8 %two_back.1 = (bf16[256,384]{1,0:T(8,128)(2,1)S(1)}, f32[96,384]{1,0:T(8,128)S(1)}, bf16[96,384]{1,0:T(8,128)(2,1)S(1)}, bf16[96,384]{1,0:T(8,128)(2,1)S(1)}, bf16[96,384]{1,0:T(8,128)(2,1)S(1)}) custom-call(s32[3]{0:T(128)S(1)} %pad_add_fusion.ids, bf16[288,384]{1,0:T(8,128)(2,1)S(1)} %one_front.1.refs_0_, ...), custom_call_target="tpu_custom_call" | custom-call | flops 905969664 | bytes 1048576 | tf_op jit(solution)/shard_map/two_back/pallas_call | solution.py:356
  55.7 5.6 %collective-permute-start.19 = (bf16[96,384]{1,0:T(8,128)(2,1)S(1)}, bf16[96,384]{1,0:T(8,128)(2,1)S(1)}, u32[]{:S(2)}, u32[]{:S(2)}) collective-permute-start(bf16[96,384]{1,0:T(8,128)(2,1)S(1)} %get-tuple-element.43), channel_id=1, source_target_pairs={{0,32},{4,36},{8,40},{12,44},{16,48},{20,52},{24,56},{28,60},{32,0... | collective-permute-start | bytes 221192 | tf_op jit(solution)/shard_map/ppermute | solution.py:395
  61.3 4.1 %collective-permute-start.20 = (bf16[96,384]{1,0:T(8,128)(2,1)S(1)}, bf16[96,384]{1,0:T(8,128)(2,1)S(1)}, u32[]{:S(2)}, u32[]{:S(2)}) collective-permute-start(bf16[96,384]{1,0:T(8,128)(2,1)S(1)} %get-tuple-element.44), channel_id=1, source_target_pairs={{0,4},{4,0},{8,12},{12,8},{16,20},{20,16},{24,28},{28,24},{32,36},... | collective-permute-start | bytes 221192 | tf_op jit(solution)/shard_map/ppermute | solution.py:396
  65.4 2.7 %collective-permute-done.20 = bf16[96,384]{1,0:T(8,128)(2,1)S(1)} collective-permute-done((bf16[96,384]{1,0:T(8,128)(2,1)S(1)}, bf16[96,384]{1,0:T(8,128)(2,1)S(1)}, u32[]{:S(2)}, u32[]{:S(2)}) %collective-permute-start.20) | collective-permute-done | bytes 73760 | tf_op jit(solution)/shard_map/ppermute | solution.py:396
  68.2 2.5 %collective-permute-done.21 = bf16[96,384]{1,0:T(8,128)(2,1)S(1)} collective-permute-done((bf16[96,384]{1,0:T(8,128)(2,1)S(1)}, bf16[96,384]{1,0:T(8,128)(2,1)S(1)}, u32[]{:S(2)}, u32[]{:S(2)}) %collective-permute-start.21) | collective-permute-done | bytes 73760 | tf_op jit(solution)/shard_map/ppermute | solution.py:397
  70.8 3.5 %collective-permute-start.23 = (bf16[96,384]{1,0:T(8,128)(2,1)S(1)}, bf16[96,384]{1,0:T(8,128)(2,1)S(1)}, u32[]{:S(2)}, u32[]{:S(2)}) collective-permute-start(bf16[96,384]{1,0:T(8,128)(2,1)S(1)} %add_convert_fusion.3), channel_id=1, source_target_pairs={{0,28},{4,8},{8,4},{12,16},{16,12},{20,24},{24,20},{28,0},{32,60},... | collective-permute-start | bytes 221192 | tf_op jit(solution)/shard_map/ppermute | solution.py:401
  74.4 1.1 %collective-permute-start.22 = (bf16[96,384]{1,0:T(8,128)(2,1)S(1)}, bf16[96,384]{1,0:T(8,128)(2,1)S(1)}, u32[]{:S(2)}, u32[]{:S(2)}) collective-permute-start(bf16[96,384]{1,0:T(8,128)(2,1)S(1)} %add_convert_fusion.3), channel_id=1, source_target_pairs={{0,96},{4,100},{8,104},{12,108},{16,112},{20,116},{24,120},{28,124... | collective-permute-start | bytes 221192 | tf_op jit(solution)/shard_map/ppermute | solution.py:400
  75.5 1.9 %collective-permute-done.24 = bf16[96,384]{1,0:T(8,128)(2,1)S(1)} collective-permute-done((bf16[96,384]{1,0:T(8,128)(2,1)S(1)}, bf16[96,384]{1,0:T(8,128)(2,1)S(1)}, u32[]{:S(2)}, u32[]{:S(2)}) %collective-permute-start.24) | collective-permute-done | bytes 73760 | tf_op jit(solution)/shard_map/ppermute | solution.py:402
  77.5 2.4 %collective-permute-done.22 = bf16[96,384]{1,0:T(8,128)(2,1)S(1)} collective-permute-done((bf16[96,384]{1,0:T(8,128)(2,1)S(1)}, bf16[96,384]{1,0:T(8,128)(2,1)S(1)}, u32[]{:S(2)}, u32[]{:S(2)}) %collective-permute-start.22) | collective-permute-done | bytes 73760 | tf_op jit(solution)/shard_map/ppermute | solution.py:400
  80.0 0.9 collective-permute-start.25
  80.8 5.1 %collective-permute-done.25 = bf16[96,384]{1,0:T(8,128)(2,1)S(1)} collective-permute-done((bf16[96,384]{1,0:T(8,128)(2,1)S(1)}, bf16[96,384]{1,0:T(8,128)(2,1)S(1)}, u32[]{:S(2)}, u32[]{:S(2)}) %collective-permute-start.25) | collective-permute-done | bytes 73760 | tf_op jit(solution)/shard_map/ppermute | solution.py:405
  85.9 0.8 collective-permute-start.26
  86.7 7.1 %collective-permute-done.26 = bf16[96,384]{1,0:T(8,128)(2,1)S(1)} collective-permute-done((bf16[96,384]{1,0:T(8,128)(2,1)S(1)}, bf16[96,384]{1,0:T(8,128)(2,1)S(1)}, u32[]{:S(2)}, u32[]{:S(2)}) %collective-permute-start.26) | collective-permute-done | bytes 73760 | tf_op jit(solution)/shard_map/ppermute | solution.py:407
  93.9 3.3 %collective-permute-start.28 = (bf16[96,384]{1,0:T(8,128)(2,1)S(1)}, bf16[96,384]{1,0:T(8,128)(2,1)S(1)}, u32[]{:S(2)}, u32[]{:S(2)}) collective-permute-start(bf16[96,384]{1,0:T(8,128)(2,1)S(1)} %add_convert_fusion.p0), channel_id=1, source_target_pairs={{0,32},{4,36},{8,40},{12,44},{16,48},{20,52},{24,56},{28,60},{32,0... | collective-permute-start | bytes 221192 | tf_op jit(solution)/shard_map/ppermute | solution.py:409
  97.4 1.1 %decode.1 = bf16[512,384]{1,0:T(8,128)(2,1)} custom-call(bf16[256,384]{1,0:T(8,128)(2,1)S(1)} %get-tuple-element.38.front_rows, bf16[256,384]{1,0:T(8,128)(2,1)S(1)} %get-tuple-element.41.back_rows, bf16[384,384]{1,0:T(8,128)(2,1)S(1)} %copy-done.2), custom_call_target="tpu_custom_call" | custom-call | flops 150994944 | bytes 1048576 | tf_op jit(solution)/shard_map/decode/pallas_call | solution.py:365
  98.5 0.7 collective-permute-done.29.p3
  99.2 0.8 collective-permute-done.28.p2
  100.0 1.6 %collective-permute-done.27.p1 = bf16[96,384]{1,0:T(8,128)(2,1)S(1)} collective-permute-done((bf16[96,384]{1,0:T(8,128)(2,1)S(1)}, bf16[96,384]{1,0:T(8,128)(2,1)S(1)}, u32[]{:S(2)}, u32[]{:S(2)}) %collective-permute-start.27) | collective-permute-done | bytes 73760 | tf_op jit(solution)/shard_map/ppermute | solution.py:410
  101.6 1.4 %assemble.1 = f32[384,384]{1,0:T(8,128)} custom-call(s32[3]{0:T(128)S(1)} %pad_add_fusion.ids, bf16[96,384]{1,0:T(8,128)(2,1)S(1)} %add_convert_fusion.p0, bf16[96,384]{1,0:T(8,128)(2,1)S(1)} %collective-permute-done.27.p1, bf16[96,384]{1,0:T(8,128)(2,1)S(1)} %collective-permute-done.28.p2, bf16[96,384]{1,0:T(8,128)(2,1)S(1)} %collective-permute-done.29.p3), custom_call_target="tpu_custom_call" | custom-call | bytes 1048576 | tf_op jit(solution)/shard_map/assemble/pallas_call | solution.py:412
  (35 shorter events, 0.8 us)
Async XLA Ops:
  0.6 17.5 %collective-permute-start.3 = (bf16[512,384]{1,0:T(8,128)(2,1)}, bf16[512,384]{1,0:T(8,128)(2,1)S(1)}, u32[]{:S(2)}, u32[]{:S(2)}) collective-permute-start(bf16[512,384]{1,0:T(8,128)(2,1)} %param.7), channel_id=1, source_target_pairs={{0,1},{1,0},{2,3},{3,2},{4,5},{5,4},{6,7},{7,6},{8,9},{9,8},{10,11... | collective-permute-start | bytes 1179656 | tf_op jit(solution)/shard_map/ppermute | solution.py:268
  1.8 13.0 %collective-permute-start = (bf16[256,384]{1,0:T(8,128)(2,1)S(1)}, bf16[256,384]{1,0:T(8,128)(2,1)S(1)}, u32[]{:S(2)}, u32[]{:S(2)}) collective-permute-start(bf16[256,384]{1,0:T(8,128)(2,1)S(1)} %get-tuple-element.24.own_a), channel_id=1, source_target_pairs={{0,2},{1,3},{2,0},{3,1},{4,6},{5,7},{6,4},{7,5},{8,10},{9,11},{10,... | collective-permute-start | bytes 589832 | tf_op jit(solution)/shard_map/ppermute | solution.py:266
  3.5 11.4 %collective-permute-start.4 = (bf16[256,384]{1,0:T(8,128)(2,1)S(1)}, bf16[256,384]{1,0:T(8,128)(2,1)S(1)}, u32[]{:S(2)}, u32[]{:S(2)}) collective-permute-start(bf16[256,384]{1,0:T(8,128)(2,1)S(1)} %get-tuple-element.28.own_b), channel_id=1, source_target_pairs={{0,130},{1,131},{2,128},{3,129},{128,2},{129,3},{130,0},{131,1},{4... | collective-permute-start | bytes 589832 | tf_op jit(solution)/shard_map/ppermute | solution.py:267
  7.3 6.0 %collective-permute-start.2 = (bf16[16,128]{1,0:T(8,128)(2,1)S(1)}, bf16[16,128]{1,0:T(8,128)(2,1)S(1)}, u32[]{:S(2)}, u32[]{:S(2)}) collective-permute-start(bf16[16,128]{1,0:T(8,128)(2,1)S(1)} %get-tuple-element.48), channel_id=1, source_target_pairs={{4,0},{8,4},{12,8},{16,12},{20,16},{24,20},{28,24},{32,28},{36,32}... | collective-permute-start | bytes 12296 | tf_op jit(solution)/shard_map/ppermute | solution.py:270
  9.3 5.5 %collective-permute-start.1 = (bf16[16,128]{1,0:T(8,128)(2,1)S(1)}, bf16[16,128]{1,0:T(8,128)(2,1)S(1)}, u32[]{:S(2)}, u32[]{:S(2)}) collective-permute-start(bf16[16,128]{1,0:T(8,128)(2,1)S(1)} %get-tuple-element.49), channel_id=1, source_target_pairs={{0,4},{4,8},{8,12},{12,16},{16,20},{20,24},{24,28},{28,32},{32,36}... | collective-permute-start | bytes 12296 | tf_op jit(solution)/shard_map/ppermute | solution.py:269
  14.8 3.2 %collective-permute-start.5 = (bf16[256,384]{1,0:T(8,128)(2,1)S(1)}, bf16[256,384]{1,0:T(8,128)(2,1)S(1)}, u32[]{:S(2)}, u32[]{:S(2)}) collective-permute-start(bf16[256,384]{1,0:T(8,128)(2,1)S(1)} %collective-permute-done.w2a), channel_id=1, source_target_pairs={{0,1},{1,0},{2,3},{3,2},{4,5},{5,4},{6,7},{7,6},{8,9},{9,8},{10,11... | collective-permute-start | bytes 589832 | tf_op jit(solution)/shard_map/ppermute | solution.py:272
  14.8 3.2 %collective-permute-start.6 = (bf16[256,384]{1,0:T(8,128)(2,1)S(1)}, bf16[256,384]{1,0:T(8,128)(2,1)S(1)}, u32[]{:S(2)}, u32[]{:S(2)}) collective-permute-start(bf16[256,384]{1,0:T(8,128)(2,1)S(1)} %collective-permute-done.4.w2b), channel_id=1, source_target_pairs={{0,1},{1,0},{2,3},{3,2},{4,5},{5,4},{6,7},{7,6},{8,9},{9,8},{10,11... | collective-permute-start | bytes 589832 | tf_op jit(solution)/shard_map/ppermute | solution.py:273
  15.4 2.7 %copy-start.1 = (f32[3,1536]{1,0:T(4,128)S(1)}, f32[3,1536]{1,0:T(4,128)}, u32[]{:S(2)}) copy-start(f32[3,1536]{1,0:T(4,128)} %refs_8_.3) | copy-start | bytes 55300
  21.5 7.8 %collective-permute-start.8 = (bf16[304,384]{1,0:T(8,128)(2,1)S(1)}, bf16[304,384]{1,0:T(8,128)(2,1)S(1)}, u32[]{:S(2)}, u32[]{:S(2)}) collective-permute-start(bf16[304,384]{1,0:T(8,128)(2,1)S(1)} %zero_front.1.refs_0_), channel_id=1, source_target_pairs={{0,2},{1,3},{2,0},{3,1},{4,6},{5,7},{6,4},{7,5},{8,10},{9,11},{10,... | collective-permute-start | bytes 700424 | tf_op jit(solution)/shard_map/ppermute | solution.py:295
  22.2 7.9 %collective-permute-start.7 = (bf16[304,384]{1,0:T(8,128)(2,1)S(1)}, bf16[304,384]{1,0:T(8,128)(2,1)S(1)}, u32[]{:S(2)}, u32[]{:S(2)}) collective-permute-start(bf16[304,384]{1,0:T(8,128)(2,1)S(1)} %zero_front.1.refs_0_), channel_id=1, source_target_pairs={{0,1},{1,0},{2,3},{3,2},{4,5},{5,4},{6,7},{7,6},{8,9},{9,8},{10,11... | collective-permute-start | bytes 700424 | tf_op jit(solution)/shard_map/ppermute | solution.py:295
  29.2 1.5 %collective-permute-start.9 = (bf16[304,384]{1,0:T(8,128)(2,1)S(1)}, bf16[304,384]{1,0:T(8,128)(2,1)S(1)}, u32[]{:S(2)}, u32[]{:S(2)}) collective-permute-start(bf16[304,384]{1,0:T(8,128)(2,1)S(1)} %collective-permute-done.8.refs_2_), channel_id=1, source_target_pairs={{0,1},{1,0},{2,3},{3,2},{4,5},{5,4},{6,7},{7,6},{8,9},{9,8},{10,11... | collective-permute-start | bytes 700424 | tf_op jit(solution)/shard_map/ppermute | solution.py:300
  29.2 7.1 %collective-permute-start.13 = (bf16[240,384]{1,0:T(8,128)(2,1)S(1)}, bf16[240,384]{1,0:T(8,128)(2,1)S(1)}, u32[]{:S(2)}, u32[]{:S(2)}) collective-permute-start(bf16[240,384]{1,0:T(8,128)(2,1)S(1)} %get-tuple-element.31.refs_4_), channel_id=1, source_target_pairs={{0,2},{1,3},{2,0},{3,1},{4,6},{5,7},{6,4},{7,5},{8,10},{9,11},{10,... | collective-permute-start | bytes 552968 | tf_op jit(solution)/shard_map/ppermute | solution.py:295
  29.9 7.3 %collective-permute-start.12 = (bf16[240,384]{1,0:T(8,128)(2,1)S(1)}, bf16[240,384]{1,0:T(8,128)(2,1)S(1)}, u32[]{:S(2)}, u32[]{:S(2)}) collective-permute-start(bf16[240,384]{1,0:T(8,128)(2,1)S(1)} %get-tuple-element.31.refs_4_), channel_id=1, source_target_pairs={{0,1},{1,0},{2,3},{3,2},{4,5},{5,4},{6,7},{7,6},{8,9},{9,8},{10,11... | collective-permute-start | bytes 552968 | tf_op jit(solution)/shard_map/ppermute | solution.py:295
  33.4 12.3 %copy-start = (bf16[1,512,384]{2,1,0:T(8,128)(2,1)S(1)}, bf16[1,512,384]{2,1,0:T(8,128)(2,1)}, u32[]{:S(2)}) copy-start(bf16[1,512,384]{2,1,0:T(8,128)(2,1)} %param.11) | copy-start | bytes 1179652
  36.3 1.4 %collective-permute-start.14 = (bf16[240,384]{1,0:T(8,128)(2,1)S(1)}, bf16[240,384]{1,0:T(8,128)(2,1)S(1)}, u32[]{:S(2)}, u32[]{:S(2)}) collective-permute-start(bf16[240,384]{1,0:T(8,128)(2,1)S(1)} %collective-permute-done.13.refs_6_), channel_id=1, source_target_pairs={{0,1},{1,0},{2,3},{3,2},{4,5},{5,4},{6,7},{7,6},{8,9},{9,8},{10,11... | collective-permute-start | bytes 552968 | tf_op jit(solution)/shard_map/ppermute | solution.py:300
  36.3 7.8 %collective-permute-start.11 = (bf16[288,384]{1,0:T(8,128)(2,1)S(1)}, bf16[288,384]{1,0:T(8,128)(2,1)S(1)}, u32[]{:S(2)}, u32[]{:S(2)}) collective-permute-start(bf16[288,384]{1,0:T(8,128)(2,1)S(1)} %one_front.1.refs_0_), channel_id=1, source_target_pairs={{0,2},{1,3},{2,0},{3,1},{4,6},{5,7},{6,4},{7,5},{8,10},{9,11},{10,... | collective-permute-start | bytes 663560 | tf_op jit(solution)/shard_map/ppermute | solution.py:295
  37.0 8.1 %collective-permute-start.10 = (bf16[288,384]{1,0:T(8,128)(2,1)S(1)}, bf16[288,384]{1,0:T(8,128)(2,1)S(1)}, u32[]{:S(2)}, u32[]{:S(2)}) collective-permute-start(bf16[288,384]{1,0:T(8,128)(2,1)S(1)} %one_front.1.refs_0_), channel_id=1, source_target_pairs={{0,1},{1,0},{2,3},{3,2},{4,5},{5,4},{6,7},{7,6},{8,9},{9,8},{10,11... | collective-permute-start | bytes 663560 | tf_op jit(solution)/shard_map/ppermute | solution.py:295
  44.1 1.5 %collective-permute-start.15 = (bf16[288,384]{1,0:T(8,128)(2,1)S(1)}, bf16[288,384]{1,0:T(8,128)(2,1)S(1)}, u32[]{:S(2)}, u32[]{:S(2)}) collective-permute-start(bf16[288,384]{1,0:T(8,128)(2,1)S(1)} %collective-permute-done.11.refs_2_), channel_id=1, source_target_pairs={{0,1},{1,0},{2,3},{3,2},{4,5},{5,4},{6,7},{7,6},{8,9},{9,8},{10,11... | collective-permute-start | bytes 663560 | tf_op jit(solution)/shard_map/ppermute | solution.py:300
  44.1 7.3 %collective-permute-start.17 = (bf16[256,384]{1,0:T(8,128)(2,1)S(1)}, bf16[256,384]{1,0:T(8,128)(2,1)S(1)}, u32[]{:S(2)}, u32[]{:S(2)}) collective-permute-start(bf16[256,384]{1,0:T(8,128)(2,1)S(1)} %get-tuple-element.35.refs_4_), channel_id=1, source_target_pairs={{0,2},{1,3},{2,0},{3,1},{4,6},{5,7},{6,4},{7,5},{8,10},{9,11},{10,... | collective-permute-start | bytes 589832 | tf_op jit(solution)/shard_map/ppermute | solution.py:295
  44.8 6.6 %collective-permute-start.16 = (bf16[256,384]{1,0:T(8,128)(2,1)S(1)}, bf16[256,384]{1,0:T(8,128)(2,1)S(1)}, u32[]{:S(2)}, u32[]{:S(2)}) collective-permute-start(bf16[256,384]{1,0:T(8,128)(2,1)S(1)} %get-tuple-element.35.refs_4_), channel_id=1, source_target_pairs={{0,1},{1,0},{2,3},{3,2},{4,5},{5,4},{6,7},{7,6},{8,9},{9,8},{10,11... | collective-permute-start | bytes 589832 | tf_op jit(solution)/shard_map/ppermute | solution.py:295
  51.4 1.4 %collective-permute-start.18 = (bf16[256,384]{1,0:T(8,128)(2,1)S(1)}, bf16[256,384]{1,0:T(8,128)(2,1)S(1)}, u32[]{:S(2)}, u32[]{:S(2)}) collective-permute-start(bf16[256,384]{1,0:T(8,128)(2,1)S(1)} %collective-permute-done.17.refs_6_), channel_id=1, source_target_pairs={{0,1},{1,0},{2,3},{3,2},{4,5},{5,4},{6,7},{7,6},{8,9},{9,8},{10,11... | collective-permute-start | bytes 589832 | tf_op jit(solution)/shard_map/ppermute | solution.py:300
  52.9 44.5 %copy-start.2 = (bf16[384,384]{1,0:T(8,128)(2,1)S(1)}, bf16[384,384]{1,0:T(8,128)(2,1)}, u32[]{:S(2)}) copy-start(bf16[384,384]{1,0:T(8,128)(2,1)} %weights.1) | copy-start | bytes 884740
  55.7 9.7 %collective-permute-start.19 = (bf16[96,384]{1,0:T(8,128)(2,1)S(1)}, bf16[96,384]{1,0:T(8,128)(2,1)S(1)}, u32[]{:S(2)}, u32[]{:S(2)}) collective-permute-start(bf16[96,384]{1,0:T(8,128)(2,1)S(1)} %get-tuple-element.43), channel_id=1, source_target_pairs={{0,32},{4,36},{8,40},{12,44},{16,48},{20,52},{24,56},{28,60},{32,0... | collective-permute-start | bytes 221192 | tf_op jit(solution)/shard_map/ppermute | solution.py:395
  61.3 6.9 %collective-permute-start.20 = (bf16[96,384]{1,0:T(8,128)(2,1)S(1)}, bf16[96,384]{1,0:T(8,128)(2,1)S(1)}, u32[]{:S(2)}, u32[]{:S(2)}) collective-permute-start(bf16[96,384]{1,0:T(8,128)(2,1)S(1)} %get-tuple-element.44), channel_id=1, source_target_pairs={{0,4},{4,0},{8,12},{12,8},{16,20},{20,16},{24,28},{28,24},{32,36},... | collective-permute-start | bytes 221192 | tf_op jit(solution)/shard_map/ppermute | solution.py:396
  65.4 5.3 %collective-permute-start.21 = (bf16[96,384]{1,0:T(8,128)(2,1)S(1)}, bf16[96,384]{1,0:T(8,128)(2,1)S(1)}, u32[]{:S(2)}, u32[]{:S(2)}) collective-permute-start(bf16[96,384]{1,0:T(8,128)(2,1)S(1)} %get-tuple-element.45), channel_id=1, source_target_pairs={{0,36},{4,32},{8,44},{12,40},{16,52},{20,48},{24,60},{28,56},{32,4... | collective-permute-start | bytes 221192 | tf_op jit(solution)/shard_map/ppermute | solution.py:397
  70.7 6.7 %collective-permute-start.24 = (bf16[96,384]{1,0:T(8,128)(2,1)S(1)}, bf16[96,384]{1,0:T(8,128)(2,1)S(1)}, u32[]{:S(2)}, u32[]{:S(2)}) collective-permute-start(bf16[96,384]{1,0:T(8,128)(2,1)S(1)} %add_convert_fusion.3), channel_id=1, source_target_pairs={{0,124},{4,104},{8,100},{12,112},{16,108},{20,120},{24,116},{28,96... | collective-permute-start | bytes 221192 | tf_op jit(solution)/shard_map/ppermute | solution.py:402
  70.8 6.7 %collective-permute-start.23 = (bf16[96,384]{1,0:T(8,128)(2,1)S(1)}, bf16[96,384]{1,0:T(8,128)(2,1)S(1)}, u32[]{:S(2)}, u32[]{:S(2)}) collective-permute-start(bf16[96,384]{1,0:T(8,128)(2,1)S(1)} %add_convert_fusion.3), channel_id=1, source_target_pairs={{0,28},{4,8},{8,4},{12,16},{16,12},{20,24},{24,20},{28,0},{32,60},... | collective-permute-start | bytes 221192 | tf_op jit(solution)/shard_map/ppermute | solution.py:401
  74.4 5.6 %collective-permute-start.22 = (bf16[96,384]{1,0:T(8,128)(2,1)S(1)}, bf16[96,384]{1,0:T(8,128)(2,1)S(1)}, u32[]{:S(2)}, u32[]{:S(2)}) collective-permute-start(bf16[96,384]{1,0:T(8,128)(2,1)S(1)} %add_convert_fusion.3), channel_id=1, source_target_pairs={{0,96},{4,100},{8,104},{12,108},{16,112},{20,116},{24,120},{28,124... | collective-permute-start | bytes 221192 | tf_op jit(solution)/shard_map/ppermute | solution.py:400
  80.0 5.9 %collective-permute-start.25 = (bf16[96,384]{1,0:T(8,128)(2,1)S(1)}, bf16[96,384]{1,0:T(8,128)(2,1)S(1)}, u32[]{:S(2)}, u32[]{:S(2)}) collective-permute-start(bf16[96,384]{1,0:T(8,128)(2,1)S(1)} %add_convert_fusion.2), channel_id=1, source_target_pairs={{0,128},{128,0},{1,129},{129,1},{2,130},{130,2},{3,131},{131,3},{4... | collective-permute-start | bytes 221192 | tf_op jit(solution)/shard_map/ppermute | solution.py:405
  85.9 7.9 %collective-permute-start.26 = (bf16[96,384]{1,0:T(8,128)(2,1)S(1)}, bf16[96,384]{1,0:T(8,128)(2,1)S(1)}, u32[]{:S(2)}, u32[]{:S(2)}) collective-permute-start(bf16[96,384]{1,0:T(8,128)(2,1)S(1)} %add_convert_fusion.1), channel_id=1, source_target_pairs={{0,12},{4,24},{8,20},{12,0},{16,28},{20,8},{24,4},{28,16},{32,44},... | collective-permute-start | bytes 221192 | tf_op jit(solution)/shard_map/ppermute | solution.py:407
  93.8 5.4 %collective-permute-start.29 = (bf16[96,384]{1,0:T(8,128)(2,1)S(1)}, bf16[96,384]{1,0:T(8,128)(2,1)S(1)}, u32[]{:S(2)}, u32[]{:S(2)}) collective-permute-start(bf16[96,384]{1,0:T(8,128)(2,1)S(1)} %add_convert_fusion.p0), channel_id=1, source_target_pairs={{0,36},{4,32},{8,44},{12,40},{16,52},{20,48},{24,60},{28,56},{32,4... | collective-permute-start | bytes 221192 | tf_op jit(solution)/shard_map/ppermute | solution.py:411
  93.9 6.0 %collective-permute-start.28 = (bf16[96,384]{1,0:T(8,128)(2,1)S(1)}, bf16[96,384]{1,0:T(8,128)(2,1)S(1)}, u32[]{:S(2)}, u32[]{:S(2)}) collective-permute-start(bf16[96,384]{1,0:T(8,128)(2,1)S(1)} %add_convert_fusion.p0), channel_id=1, source_target_pairs={{0,32},{4,36},{8,40},{12,44},{16,48},{20,52},{24,56},{28,60},{32,0... | collective-permute-start | bytes 221192 | tf_op jit(solution)/shard_map/ppermute | solution.py:409
  97.2 4.4 %collective-permute-start.27 = (bf16[96,384]{1,0:T(8,128)(2,1)S(1)}, bf16[96,384]{1,0:T(8,128)(2,1)S(1)}, u32[]{:S(2)}, u32[]{:S(2)}) collective-permute-start(bf16[96,384]{1,0:T(8,128)(2,1)S(1)} %add_convert_fusion.p0), channel_id=1, source_target_pairs={{0,4},{4,0},{8,12},{12,8},{16,20},{20,16},{24,28},{28,24},{32,36},... | collective-permute-start | bytes 221192 | tf_op jit(solution)/shard_map/ppermute | solution.py:410

commit v4 on v3

--- a/solution.py
+++ b/solution.py
@@ -53,7 +53,7 @@
     for t in range(3):
         first = at + (t - 1) * dilation
         part = jnp.dot(
-            normed[first : first + rows, :], weights[t], preferred_element_type=jnp.float32
+            normed[first : first + rows, :], weights[t][...], preferred_element_type=jnp.float32
         )
         update = part if update is None else update + part
     return update
@@ -63,16 +63,16 @@
     ref[first : first + rows, :] = jnp.zeros((rows, ref.shape[1]), ref.dtype)
 
 
-def start_weights(ids, layer, w_hbm, out, sems):
-    width = out.shape[2]
+def start_weights(ids, layer, taps, w_hbm, outs, sems):
     copies = []
-    for t in range(3):
+    for n, (t, out) in enumerate(zip(taps, outs)):
+        width = out.shape[1]
         for k in range(4):
             copies.append(
                 pltpu.make_async_copy(
                     w_hbm.at[layer, t, pl.ds((ids[0] ^ k) * width, width), :],
-                    out.at[t, pl.ds(k * width, width), :],
-                    sems.at[t, k],
+                    out.at[pl.ds(k * width, width), :],
+                    sems.at[n, k],
                 )
             )
             copies[-1].start()
@@ -84,8 +84,8 @@
         copy.wait()
 
 
-def one_hot(bins, count, ids, before, own, after, w_hbm, onehot, weights, sems):
-    copies = start_weights(ids, 0, w_hbm, weights, sems)
+def one_hot(bins, count, ids, before, own, after, w_hbm, onehot, *refs):
+    copies = start_weights(ids, 0, range(3), w_hbm, refs[:3], refs[3])
     letters = jnp.concatenate([before[...], own[...], after[...]], axis=0)
     lane = lax.broadcasted_iota(jnp.int32, (PATCH, 4 * PATCH), 1)
     row = lax.broadcasted_iota(jnp.int32, (PATCH, 4 * PATCH), 0)
@@ -97,13 +97,20 @@
     wait_all(copies)
 
 
-def first_layer(span, bins, count, ids, onehot, own_a, own_b, w1, w2a, w2b, w3a, w3b, gains, weights, *refs):
+def fetching(kernel, inputs, results, layer, taps):
+    def run(ids, *refs):
+        ins, (w_hbm, *refs) = refs[:inputs], refs[inputs:]
+        outs, later, refs = refs[:results], refs[results : results + len(taps)], refs[results + len(taps) :]
+        copies = start_weights(ids, layer, taps, w_hbm, later, refs[-1])
+        kernel(ids, *ins, *outs, *refs[:-1])
+        wait_all(copies)
+
+    return run
+
+
+def first_layer(span, bins, count, ids, onehot, own_a, own_b, w1, w2a, w2b, w3a, w3b, gains, *refs):
     low, high = span
-    if low == 0:
-        copies, (out, normed, stream) = [], refs
-    else:
-        w_hbm, out, later, normed, stream, sems = refs
-        copies = start_weights(ids, 1, w_hbm, later, sems)
+    weights, (out, normed, stream) = refs[:3], refs[3:]
     width = out.shape[1]
     first, last = max(low - HALO, 0), min(high + HALO, bins + 2 * HALO)
     rows = last - first
@@ -130,11 +137,10 @@
     total = stream[low - first : high - first, 0:width].astype(jnp.float32) + update
     inside = in_sequence(ids, low, high - low, bins, count)
     out[...] = (total * inside).astype(jnp.bfloat16)
-    wait_all(copies)
 
 
 def front(layer, dilation, span, bins, count, ids, *refs):
-    pieces, (gains, weights, out, normed) = refs[:4], refs[4:]
+    pieces, gains, weights, (out, normed) = refs[:4], refs[4], refs[5:8], refs[8:]
     low, high = span
     rows = high + HALO
     clear(normed, 0, PAD)
@@ -151,13 +157,7 @@
 
 
 def back(layer, dilation, span, bins, count, ids, *refs):
-    fronts, backs, (gains, weights) = refs[:4], refs[4:8], refs[8:10]
-    copies = []
-    if len(refs) == 15:
-        w_hbm, out, later, normed, sems = refs[10:]
-        copies = start_weights(ids, layer + 1, w_hbm, later, sems)
-    else:
-        out, normed = refs[10:]
+    fronts, backs, gains, weights, (out, normed) = refs[:4], refs[4:8], refs[8], refs[9:12], refs[12:]
     low, high = span
     first = low - HALO
     joint = fronts[0].shape[0]
@@ -178,7 +178,6 @@
     if count:
         total = total * in_sequence(ids, low, high - low, bins, count)
     out[...] = total.astype(jnp.bfloat16)
-    wait_all(copies)
 
 
 def gradient(stream, upstream):
@@ -188,22 +187,24 @@
 
 
 def last_front(span, bins, ids, *refs):
-    refs, (upstream, out, grad, normed) = refs[:6], refs[6:]
+    refs, (upstream, out, grad, normed) = refs[:8], refs[8:]
     front(2, 4 * FIRST_DILATION0, span, bins, 0, ids, *refs, out, normed)
     low, high = span
     grad[...] = gradient(out[...], upstream[low - HALO : high - HALO, :])
 
 
 def last_back(span, bins, ids, *refs):
-    refs, (upstream, before, out, g0, g1, g2, g3, normed, grad) = refs[:10], refs[10:]
+    refs, (upstream, before, out, g0, g1, g2, g3, normed, grad) = refs[:12], refs[12:]
     back(2, 4 * FIRST_DILATION0, span, bins, 0, ids, *refs, out, normed)
     low, high = span
     grad[...] = before[...] + gradient(out[...], upstream[low - HALO : high - HALO, :])
     quarter = g0.shape[0]
-    g0[...] = grad[pl.ds(pl.multiple_of(ids[2] * quarter, 8), quarter), :]
-    for k, g in ((1, g1), (2, g2), (3, g3)):
-        at = pl.multiple_of((ids[2] ^ k) * quarter, 8)
-        g[...] = grad[pl.ds(at, quarter), :].astype(jnp.bfloat16)
+    for k, g in enumerate((g0, g1, g2, g3)):
+        g[...] = grad[pl.ds(quarter_at(ids, k, quarter), quarter), :].astype(g.dtype)
+
+
+def quarter_at(ids, k, quarter):
+    return pl.multiple_of((ids[2] ^ (ids[2 + k] if k else 0)) * quarter, 8)
 
 
 def decode(front_rows, back_rows, weights, out):
@@ -216,8 +217,7 @@
 def assemble(ids, p0, p1, p2, p3, out):
     quarter = p0.shape[0]
     for k, p in enumerate((p0, p1, p2, p3)):
-        at = pl.multiple_of((ids[2] ^ k) * quarter, 8)
-        out[pl.ds(at, quarter), :] = p[...].astype(jnp.float32)
+        out[pl.ds(quarter_at(ids, k, quarter), quarter), :] = p[...].astype(jnp.float32)
 
 
 def tie(value, *done):
@@ -250,7 +250,9 @@
     seq, chan = lax.axis_index("seq"), lax.axis_index("chan")
     x, z = seq // zs, seq % zs
     x_half, z_half = ((x + 1) // 2) % 2, ((z + 1) // 2) % 2
-    ids = jnp.stack([chan, seq, x_half * 2 + z_half]).astype(jnp.int32)
+    core = chan % 2
+    ids = jnp.stack([chan, seq, x_half * 2 + z_half, 2 - core, 1 + core, 3 + 0 * core])
+    ids = ids.astype(jnp.int32)
 
     across = functools.partial(lax.ppermute, axis_name="chan", perm=pairs(4, lambda i: i ^ 2))
     other_core = functools.partial(lax.ppermute, axis_name="chan", perm=pairs(4, lambda i: i ^ 1))
@@ -258,7 +260,7 @@
         lax.ppermute, axis_name=("section", "chan"), perm=pairs(8, lambda i: i ^ 6)
     )
 
-    letters = lax.optimization_barrier(bases.reshape(bins, PATCH).astype(bf16))
+    letters = bases.reshape(bins, PATCH)
     up = [(i, i + 1) for i in range(seq_count - 1)]
     down = [(j, i) for i, j in up]
     half = stem.shape[0] // 2
@@ -266,19 +268,20 @@
     w2a = across(stem_a)
     w2b = far(stem_b)
     w1 = other_core(stem)
-    before = lax.ppermute(letters[bins - HALO :], "seq", up)
-    after = lax.ppermute(letters[:HALO], "seq", down)
+    before = lax.ppermute(letters[bins - HALO :].astype(bf16), "seq", up)
+    after = lax.ppermute(letters[:HALO].astype(bf16), "seq", down)
+    letters = lax.optimization_barrier(letters.astype(bf16))
     w2a, before, after = lax.optimization_barrier((w2a, before, after))
     w3a = other_core(w2a)
     w3b = other_core(w2b)
-    layer_weights = jax.ShapeDtypeStruct((3, 4 * width, width), bf16)
-    weight_sems = pltpu.SemaphoreType.DMA((3, 4))
-    onehot, weights = call(
+    tap = jax.ShapeDtypeStruct((4 * width, width), bf16)
+    tap_sems = pltpu.SemaphoreType.DMA((3, 4))
+    onehot, *weights = call(
         "one_hot",
         functools.partial(one_hot, bins, count),
-        [jax.ShapeDtypeStruct((rows, 4 * PATCH), bf16), layer_weights],
+        [jax.ShapeDtypeStruct((rows, 4 * PATCH), bf16)] + [tap] * 3,
         [SMEM] + [VMEM] * 3 + [HBM],
-        [weight_sems],
+        [tap_sems],
         flops=10**9,
     )(ids, before, letters, after, conv_weight)
 
@@ -300,46 +303,49 @@
         return own, beside, remote, other_core(remote)
 
     cut = bins // 2 + 3 * HALO
-    inputs = (onehot, stem_a, stem_b, w1, w2a, w2b, w3a, w3b, gains, weights)
-    part = call(
+    inputs = (onehot, stem_a, stem_b, w1, w2a, w2b, w3a, w3b, gains, *weights)
+    part, tap0 = call(
         "zero_front",
-        functools.partial(first_layer, (0, cut), bins, count),
-        shape(cut),
-        [SMEM] + [VMEM] * 10,
-        [normed(cut + HALO), pltpu.VMEM((cut + HALO, 4 * width), bf16)],
+        fetching(functools.partial(first_layer, (0, cut), bins, count), 12, 1, 1, (0,)),
+        [shape(cut), tap],
+        [SMEM] + [VMEM] * 12 + [HBM],
+        [normed(cut + HALO), pltpu.VMEM((cut + HALO, 4 * width), bf16), tap_sems],
         flops=work(cut),
-    )(ids, *inputs)
+    )(ids, *inputs, conv_weight)
     sent_front = exchange(part)
-    part, weights = call(
+    part, *taps = call(
         "zero_back",
-        functools.partial(first_layer, (cut, rows), bins, count),
-        [shape(rows - cut), layer_weights],
-        [SMEM] + [VMEM] * 10 + [HBM],
-        [normed(rows - cut + HALO), pltpu.VMEM((rows - cut + HALO, 4 * width), bf16), weight_sems],
+        fetching(functools.partial(first_layer, (cut, rows), bins, count), 12, 1, 1, (1, 2)),
+        [shape(rows - cut), tap, tap],
+        [SMEM] + [VMEM] * 12 + [HBM],
+        [normed(rows - cut + HALO), pltpu.VMEM((rows - cut + HALO, 4 * width), bf16), tap_sems],
         flops=work(rows - cut),
     )(ids, *inputs, conv_weight)
+    weights = (tap0, *taps)
     sent_back = exchange(part)
     fronts = finish(sent_front, part)
 
     cut = cut - HALO
-    part = call(
+    layer = (1, 2 * FIRST_DILATION0)
+    part, tap0 = call(
         "one_front",
-        functools.partial(front, 1, 2 * FIRST_DILATION0, (0, cut), bins, count),
-        shape(cut),
-        [SMEM] + [VMEM] * 6,
-        [normed(cut + HALO)],
+        fetching(functools.partial(front, *layer, (0, cut), bins, count), 8, 1, 2, (0,)),
+        [shape(cut), tap],
+        [SMEM] + [VMEM] * 8 + [HBM],
+        [normed(cut + HALO), tap_sems],
         flops=work(cut),
-    )(ids, *fronts, gains, weights)
+    )(ids, *fronts, gains, *weights, conv_weight)
     sent_front = exchange(part)
     backs = finish(sent_back, part)
-    part, weights = call(
+    part, *taps = call(
         "one_back",
-        functools.partial(back, 1, 2 * FIRST_DILATION0, (cut, rows), bins, count),
-        [shape(rows - cut), layer_weights],
-        [SMEM] + [VMEM] * 10 + [HBM],
-        [normed(rows - cut + HALO), weight_sems],
+        fetching(functools.partial(back, *layer, (cut, rows), bins, count), 12, 1, 2, (1, 2)),
+        [shape(rows - cut), tap, tap],
+        [SMEM] + [VMEM] * 12 + [HBM],
+        [normed(rows - cut + HALO), tap_sems],
         flops=work(rows - cut),
-    )(ids, *fronts, *backs, gains, weights, conv_weight)
+    )(ids, *fronts, *backs, gains, *weights, conv_weight)
+    weights = (tap0, *taps)
     sent_back = exchange(part)
     fronts = finish(sent_front, part)
 
@@ -348,20 +354,20 @@
         "two_front",
         functools.partial(last_front, (HALO, cut), bins),
         [shape(cut - HALO), jax.ShapeDtypeStruct((width, width), f32)],
-        [SMEM] + [VMEM] * 7,
+        [SMEM] + [VMEM] * 9,
         [normed(cut + HALO)],
         flops=work(cut - HALO),
-    )(ids, *fronts, gains, weights, upstream[0])
+    )(ids, *fronts, gains, *weights, upstream[0])
     backs = finish(sent_back, front_rows)
     back_rows, g0, g1, g2, g3 = call(
         "two_back",
         functools.partial(last_back, (cut, rows - HALO), bins),
         [shape(rows - HALO - cut), jax.ShapeDtypeStruct((width // 4, width), f32)]
         + [shape(width // 4)] * 3,
-        [SMEM] + [VMEM] * 12,
+        [SMEM] + [VMEM] * 14,
         [normed(rows - cut + HALO), pltpu.VMEM((width, width), f32)],
         flops=work(rows - HALO - cut),
-    )(ids, *fronts, *backs, gains, weights, upstream[0], front_grad)
+    )(ids, *fronts, *backs, gains, *weights, upstream[0], front_grad)
     decoded = call(
         "decode",
         decode,
@@ -371,11 +377,6 @@
         megabytes=8,
     )(front_rows, back_rows, dec_weight)
 
-    def over(fx, fz):
-        def partner(i):
-            return fx(i // zs) * zs + fz(i % zs)
-
-        return functools.partial(lax.ppermute, axis_name="seq", perm=pairs(seq_count, partner))
 
     def same(i):
         return i
@@ -392,23 +393,35 @@
     def zs_far(i):
         return {0: 3, 3: 0, 1: 6, 6: 1, 2: 5, 5: 2, 4: 7, 7: 4}[i]
 
-    r2 = over(flip, same)(g2)
-    r1 = over(same, flip)(g1)
-    r3 = over(flip, flip)(g3)
-    total = (g0 + r2.astype(f32)) + (r1.astype(f32) + r3.astype(f32))
+    def swap(own, *moves):
+        def partner(i):
+            pair, lane = divmod(i, 4)
+            section, spot = divmod(pair, seq_count)
+            fs, fx, fz = moves[lane % len(moves)]
+            spot = fx(spot // zs) * zs + fz(spot % zs)
+            return (fs(section) * seq_count + spot) * 4 + lane
+
+        perm = pairs(2 * seq_count * 4, partner)
+        return lax.ppermute(own, ("section", "seq", "chan"), perm)
+
+    def swap_three(fx, fz, a, b, c):
+        both = swap(c, (same, fx, fz))
+        along_x, along_z = (same, fx, same), (same, same, fz)
+        return swap(a, along_x, along_z), swap(b, along_z, along_x), both
+
+    def add(a, b):
+        return (a.astype(f32) + b.astype(f32)).astype(bf16)
+
+    r1, r2, r3 = swap_three(flip, flip, g1, g2, g3)
+    total = (g0 + r1.astype(f32)) + (r2.astype(f32) + r3.astype(f32))
     own = total.astype(bf16)
-    rx = over(xs_near, same)(own)
-    rz = over(same, zs_near)(own)
-    rxz = over(xs_near, zs_near)(own)
-    total = (own.astype(f32) + rx.astype(f32)) + (rz.astype(f32) + rxz.astype(f32))
+    r1, r2, r3 = swap_three(xs_near, zs_near, own, own, own)
+    total = (own.astype(f32) + r1.astype(f32)) + (r2.astype(f32) + r3.astype(f32))
     own = total.astype(bf16)
-    other = lax.ppermute(own, "section", [(0, 1), (1, 0)])
-    own = (own.astype(f32) + other.astype(f32)).astype(bf16)
-    other = over(same, zs_far)(own)
-    own = (own.astype(f32) + other.astype(f32)).astype(bf16)
-    r2 = over(flip, same)(own)
-    r1 = over(same, flip)(own)
-    r3 = over(flip, flip)(own)
+    sections, far_z = (flip, same, same), (same, same, zs_far)
+    own = add(own, swap(own, sections, far_z))
+    own = add(own, swap(own, far_z, sections))
+    r1, r2, r3 = swap_three(flip, flip, own, own, own)
     weight_grad = call(
         "assemble",
         assemble,

time: 103 us -> 102 us (level)
  waiting for transfers between devices: 39.9 us -> 37.1 us
  Pallas kernels: 25.8 us -> 27.5 us
  starting transfers between devices: 33.5 us -> 32.1 us
    ppermute x13, waiting for transfers between devices: 26.4 us -> 24.1 us  [the longest x11 20.8 us: swap(): return lax.ppermute(own, ('section', 'seq', 'chan'), perm)]
    another operation x1 -> x2, other arithmetic: 0.08 us -> 1.88 us  [body(): ids = jnp.stack([chan, seq, x_half * 2 + z_half]).astype(jnp.int32)]
    pallas_call x4, Pallas kernels: 15.1 us -> 16.8 us  [the longest x1 4.55 us: body(): call('zero_front', fetching(functools.partial(first_layer, (0, cut), bins...]
    convert_element_type x3 -> x2, other arithmetic: 1.69 us -> 0.04 us  [add(): return (a.astype(f32) + b.astype(f32)).astype(bf16)]
    ppermute x13, starting transfers between devices: 25.6 us -> 24.3 us  [the longest x11 18.4 us: swap(): return lax.ppermute(own, ('section', 'seq', 'chan'), perm)]
  transfers between devices with their start and end apart: 30 -> 30, of which waited for: 19 -> 19; matrix products, arithmetic and copies ran while one was open for 3% -> 2% of each run, Pallas kernels for 18% -> 19%
where the time goes in v4:
time: 102 us; the launch traced here: 101 us
  waiting for transfers between devices  37.1 us (36%)
  starting transfers between devices  32.1 us (31%)
  Pallas kernels  27.5 us (27%)
  other arithmetic  2.01 us (2%)
  local copies, waits for them, and re-layouts  1.27 us (1%)
    ppermute x11, waiting for transfers between devices, swap(): return lax.ppermute(own, ('section', 'seq', 'chan'), perm)  20.8 us
    ppermute x11, starting transfers between devices, swap(): return lax.ppermute(own, ('section', 'seq', 'chan'), perm)  18.4 us
    ppermute x8, waiting for transfers between devices, exchange(): return (own, other_core(own), across(own))  9.86 us
    pallas_call x1, Pallas kernels, body(): call('zero_front', fetching(functools.partial(first_layer, (0, cut), bins...  4.55 us
    pallas_call x1, Pallas kernels, body(): call('zero_back', fetching(functools.partial(first_layer, (cut, rows), bi...  4.32 us
    pallas_call x1, Pallas kernels, body(): call('one_back', fetching(functools.partial(back, *layer, (cut, rows), bi...  4.05 us
    pallas_call x1, Pallas kernels, body(): call('one_front', fetching(functools.partial(front, *layer, (0, cut), bin...  3.84 us
    ppermute x1, starting transfers between devices, body(): before = lax.ppermute(letters[bins - HALO:].astype(bf16), 'seq', up)  3.82 us
  transfers between devices with their start and end apart: 30, of which 19 were waited for; matrix products, arithmetic and copies ran while one was open for 2% of the time, Pallas kernels for 19%

profile of v4, /device:TPU:32, one launch (start us, length us, event | category | flops | bytes accessed | tf_op | source)
XLA Modules:
  0.0 101.0 jit_solution(18174327346253169318)
XLA Ops:
  0.6 1.1 %fusion = (bf16[256,384]{1,0:T(8,128)(2,1)S(1)}, bf16[256,384]{1,0:T(8,128)(2,1)S(1)}) fusion(bf16[512,384]{1,0:T(8,128)(2,1)} %param.7), kind=kLoop, calls=%fused_computation.7 | loop fusion | bytes 786432 | tf_op jit(solution)/shard_map/slice | solution.py:267
  1.8 1.7 %collective-permute-start = (bf16[256,384]{1,0:T(8,128)(2,1)S(1)}, bf16[256,384]{1,0:T(8,128)(2,1)S(1)}, u32[]{:S(2)}, u32[]{:S(2)}) collective-permute-start(bf16[256,384]{1,0:T(8,128)(2,1)S(1)} %get-tuple-element.32.refs_1_), channel_id=1, source_target_pairs={{0,2},{1,3},{2,0},{3,1},{4,6},{5,7},{6,4},{7,5},{8,10},{9,11},{10,... | collective-permute-start | bytes 589832 | tf_op jit(solution)/shard_map/ppermute | solution.py:268
  3.4 2.2 %collective-permute-start.4 = (bf16[256,384]{1,0:T(8,128)(2,1)S(1)}, bf16[256,384]{1,0:T(8,128)(2,1)S(1)}, u32[]{:S(2)}, u32[]{:S(2)}) collective-permute-start(bf16[256,384]{1,0:T(8,128)(2,1)S(1)} %get-tuple-element.36.refs_2_), channel_id=1, source_target_pairs={{0,130},{1,131},{2,128},{3,129},{128,2},{129,3},{130,0},{131,1},{4... | collective-permute-start | bytes 589832 | tf_op jit(solution)/shard_map/ppermute | solution.py:269
  5.6 1.1 %convert.4 = bf16[1,65536]{1,0:T(2,128)(2,1)S(1)} convert(s32[1,65536]{1,0:T(1,128)} %param.6) | non-fusion elementwise | flops 65536 | bytes 393216 | tf_op jit(solution)/shard_map/convert.1
  6.8 3.8 %collective-permute-start.1 = (bf16[16,128]{1,0:T(8,128)(2,1)S(1)}, bf16[16,128]{1,0:T(8,128)(2,1)S(1)}, u32[]{:S(2)}, u32[]{:S(2)}) collective-permute-start(bf16[16,128]{1,0:T(8,128)(2,1)S(1)} %bitcast.15), channel_id=1, source_target_pairs={{0,4},{4,8},{8,12},{12,16},{16,20},{20,24},{24,28},{28,32},{32,36}... | collective-permute-start | bytes 12296 | tf_op jit(solution)/shard_map/ppermute | solution.py:271
  10.6 2.0 %collective-permute-start.2 = (bf16[16,128]{1,0:T(8,128)(2,1)S(1)}, bf16[16,128]{1,0:T(8,128)(2,1)S(1)}, u32[]{:S(2)}, u32[]{:S(2)}) collective-permute-start(bf16[16,128]{1,0:T(8,128)(2,1)S(1)} %bitcast.14), channel_id=1, source_target_pairs={{4,0},{8,4},{12,8},{16,12},{20,16},{24,20},{28,24},{32,28},{36,32}... | collective-permute-start | bytes 12296 | tf_op jit(solution)/shard_map/ppermute | solution.py:272
  12.8 3.4 %collective-permute-done.2.after = bf16[16,128]{1,0:T(8,128)(2,1)S(1)} collective-permute-done((bf16[16,128]{1,0:T(8,128)(2,1)S(1)}, bf16[16,128]{1,0:T(8,128)(2,1)S(1)}, u32[]{:S(2)}, u32[]{:S(2)}) %collective-permute-start.2) | collective-permute-done | bytes 4128 | tf_op jit(solution)/shard_map/ppermute | solution.py:272
  16.1 0.5 collective-permute-start.6
  16.6 0.7 convert_reduce_fusion
  17.5 2.7 %one_hot.1 = (bf16[544,512]{1,0:T(8,128)(2,1)S(1)}, bf16[1536,384]{1,0:T(8,128)(2,1)S(1)}, bf16[1536,384]{1,0:T(8,128)(2,1)S(1)}, bf16[1536,384]{1,0:T(8,128)(2,1)S(1)}) custom-call(s32[6]{0:T(128)S(1)} %stack.23.ids, bf16[16,128]{1,0:T(8,128)(2,1)S(1)} %collective-permute-done.1.before, bf16[512,128]{1,0:T(8,128)(2,1)S(1)} %bitcast.12, ...), custom_call_target="tpu_custom_call" | custom-call | flops 1000000000 | bytes 1048576 | tf_op jit(solution)/shard_map/one_hot/pallas_call | solution.py:279
  20.3 4.6 %zero_front.1 = (bf16[304,384]{1,0:T(8,128)(2,1)S(1)}, bf16[1536,384]{1,0:T(8,128)(2,1)S(1)}) custom-call(s32[6]{0:T(128)S(1)} %stack.23.ids, bf16[544,512]{1,0:T(8,128)(2,1)S(1)} %get-tuple-element.35.refs_0_, bf16[256,384]{1,0:T(8,128)(2,1)S(1)} %get-tuple-element.32.refs_1_, bf16[256,384]{1,0:T(8,128)(2,1)S(1)} %get-tuple-element.36.refs_2_, ...), custom_call_target="tpu_custom_call" | custom-call | flops 1075838976 | bytes 1048576 | tf_op jit(solution)/shard_map/zero_front/pallas_call | solution.py:307
  24.9 0.8 collective-permute-start.8
  25.6 4.3 %zero_back.1 = (bf16[240,384]{1,0:T(8,128)(2,1)S(1)}, bf16[1536,384]{1,0:T(8,128)(2,1)S(1)}, bf16[1536,384]{1,0:T(8,128)(2,1)S(1)}) custom-call(s32[6]{0:T(128)S(1)} %stack.23.ids, bf16[544,512]{1,0:T(8,128)(2,1)S(1)} %get-tuple-element.35.refs_0_, bf16[256,384]{1,0:T(8,128)(2,1)S(1)} %get-tuple-element.32.refs_1_, ...), custom_call_target="tpu_custom_call" | custom-call | flops 849346560 | bytes 1048576 | tf_op jit(solution)/shard_map/zero_back/pallas_call | solution.py:316
  30.0 2.7 %collective-permute-done.8.refs_2_ = bf16[304,384]{1,0:T(8,128)(2,1)S(1)} collective-permute-done((bf16[304,384]{1,0:T(8,128)(2,1)S(1)}, bf16[304,384]{1,0:T(8,128)(2,1)S(1)}, u32[]{:S(2)}, u32[]{:S(2)}) %collective-permute-start.8) | collective-permute-done | bytes 233504 | tf_op jit(solution)/shard_map/ppermute | solution.py:298
  32.6 0.7 collective-permute-start.13
  33.6 0.6 collective-permute-done.9.refs_3_
  34.1 3.8 %one_front.1 = (bf16[288,384]{1,0:T(8,128)(2,1)S(1)}, bf16[1536,384]{1,0:T(8,128)(2,1)S(1)}) custom-call(s32[6]{0:T(128)S(1)} %stack.23.ids, bf16[304,384]{1,0:T(8,128)(2,1)S(1)} %get-tuple-element.41.refs_0_, bf16[304,384]{1,0:T(8,128)(2,1)S(1)} %collective-permute-done.7.refs_1_, bf16[304,384]{1,0:T(8,128)(2,1)S(1)} %collective-permute-done.8.refs_2_, ...), custom_call_target="tpu_custom_call" | custom-call | flops 1019215872 | bytes 1048576 | tf_op jit(solution)/shard_map/one_front/pallas_call | solution.py:330
  38.0 1.7 %collective-permute-done.13.refs_6_ = bf16[240,384]{1,0:T(8,128)(2,1)S(1)} collective-permute-done((bf16[240,384]{1,0:T(8,128)(2,1)S(1)}, bf16[240,384]{1,0:T(8,128)(2,1)S(1)}, u32[]{:S(2)}, u32[]{:S(2)}) %collective-permute-start.13) | collective-permute-done | bytes 184352 | tf_op jit(solution)/shard_map/ppermute | solution.py:298
  39.7 0.7 collective-permute-start.11
  40.6 0.5 collective-permute-done.14.refs_7_
  41.1 4.0 %one_back.1 = (bf16[256,384]{1,0:T(8,128)(2,1)S(1)}, bf16[1536,384]{1,0:T(8,128)(2,1)S(1)}, bf16[1536,384]{1,0:T(8,128)(2,1)S(1)}) custom-call(s32[6]{0:T(128)S(1)} %stack.23.ids, bf16[304,384]{1,0:T(8,128)(2,1)S(1)} %get-tuple-element.41.refs_0_, bf16[304,384]{1,0:T(8,128)(2,1)S(1)} %collective-permute-done.7.refs_1_, ...), custom_call_target="tpu_custom_call" | custom-call | flops 905969664 | bytes 1048576 | tf_op jit(solution)/shard_map/one_back/pallas_call | solution.py:340
  45.2 2.4 %collective-permute-done.11.refs_2_ = bf16[288,384]{1,0:T(8,128)(2,1)S(1)} collective-permute-done((bf16[288,384]{1,0:T(8,128)(2,1)S(1)}, bf16[288,384]{1,0:T(8,128)(2,1)S(1)}, u32[]{:S(2)}, u32[]{:S(2)}) %collective-permute-start.11) | collective-permute-done | bytes 221216 | tf_op jit(solution)/shard_map/ppermute | solution.py:298
  47.5 0.7 collective-permute-start.17
  48.5 0.6 collective-permute-done.15.refs_3_
  49.0 2.7 %two_front.1 = (bf16[256,384]{1,0:T(8,128)(2,1)S(1)}, f32[384,384]{1,0:T(8,128)S(1)}) custom-call(s32[6]{0:T(128)S(1)} %stack.23.ids, bf16[288,384]{1,0:T(8,128)(2,1)S(1)} %get-tuple-element.47.refs_0_, bf16[288,384]{1,0:T(8,128)(2,1)S(1)} %collective-permute-done.10.refs_1_, bf16[288,384]{1,0:T(8,128)(2,1)S(1)} %collective-permute-done.11.refs_2_, ...), custom_call_target="tpu_custom_call" | custom-call | flops 905969664 | bytes 1048576 | tf_op jit(solution)/shard_map/two_front/pallas_call | solution.py:353
  51.8 3.1 %collective-permute-done.17.refs_6_ = bf16[256,384]{1,0:T(8,128)(2,1)S(1)} collective-permute-done((bf16[256,384]{1,0:T(8,128)(2,1)S(1)}, bf16[256,384]{1,0:T(8,128)(2,1)S(1)}, u32[]{:S(2)}, u32[]{:S(2)}) %collective-permute-start.17) | collective-permute-done | bytes 196640 | tf_op jit(solution)/shard_map/ppermute | solution.py:298
  54.9 1.4 %collective-permute-done.18.refs_7_ = bf16[256,384]{1,0:T(8,128)(2,1)S(1)} collective-permute-done((bf16[256,384]{1,0:T(8,128)(2,1)S(1)}, bf16[256,384]{1,0:T(8,128)(2,1)S(1)}, u32[]{:S(2)}, u32[]{:S(2)}) %collective-permute-start.18) | collective-permute-done | bytes 196640 | tf_op jit(solution)/shard_map/ppermute | solution.py:303
  56.3 2.8 %two_back.1 = (bf16[256,384]{1,0:T(8,128)(2,1)S(1)}, f32[96,384]{1,0:T(8,128)S(1)}, bf16[96,384]{1,0:T(8,128)(2,1)S(1)}, bf16[96,384]{1,0:T(8,128)(2,1)S(1)}, bf16[96,384]{1,0:T(8,128)(2,1)S(1)}) custom-call(s32[6]{0:T(128)S(1)} %stack.23.ids, bf16[288,384]{1,0:T(8,128)(2,1)S(1)} %get-tuple-element.47.refs_0_, ...), custom_call_target="tpu_custom_call" | custom-call | flops 905969664 | bytes 1048576 | tf_op jit(solution)/shard_map/two_back/pallas_call | solution.py:362
  59.1 1.8 %collective-permute-start.19 = (bf16[96,384]{1,0:T(8,128)(2,1)S(1)}, bf16[96,384]{1,0:T(8,128)(2,1)S(1)}, u32[]{:S(2)}, u32[]{:S(2)}) collective-permute-start(bf16[96,384]{1,0:T(8,128)(2,1)S(1)} %get-tuple-element.59), channel_id=1, source_target_pairs={{0,32},{1,5},{2,34},{3,7},{4,36},{5,1},{6,38},{7,3},{8,40},{9,13},... | collective-permute-start | bytes 221192 | tf_op jit(solution)/shard_map/ppermute | solution.py:405
  60.9 1.7 %collective-permute-start.20 = (bf16[96,384]{1,0:T(8,128)(2,1)S(1)}, bf16[96,384]{1,0:T(8,128)(2,1)S(1)}, u32[]{:S(2)}, u32[]{:S(2)}) collective-permute-start(bf16[96,384]{1,0:T(8,128)(2,1)S(1)} %get-tuple-element.60), channel_id=1, source_target_pairs={{0,4},{1,33},{2,6},{3,35},{4,0},{5,37},{6,2},{7,39},{8,12},{9,41},... | collective-permute-start | bytes 221192 | tf_op jit(solution)/shard_map/ppermute | solution.py:405
  62.9 1.4 %collective-permute-done.19 = bf16[96,384]{1,0:T(8,128)(2,1)S(1)} collective-permute-done((bf16[96,384]{1,0:T(8,128)(2,1)S(1)}, bf16[96,384]{1,0:T(8,128)(2,1)S(1)}, u32[]{:S(2)}, u32[]{:S(2)}) %collective-permute-start.19) | collective-permute-done | bytes 73760 | tf_op jit(solution)/shard_map/ppermute | solution.py:405
  64.2 1.7 %collective-permute-done.20 = bf16[96,384]{1,0:T(8,128)(2,1)S(1)} collective-permute-done((bf16[96,384]{1,0:T(8,128)(2,1)S(1)}, bf16[96,384]{1,0:T(8,128)(2,1)S(1)}, u32[]{:S(2)}, u32[]{:S(2)}) %collective-permute-start.20) | collective-permute-done | bytes 73760 | tf_op jit(solution)/shard_map/ppermute | solution.py:405
  65.9 1.9 %collective-permute-done.21 = bf16[96,384]{1,0:T(8,128)(2,1)S(1)} collective-permute-done((bf16[96,384]{1,0:T(8,128)(2,1)S(1)}, bf16[96,384]{1,0:T(8,128)(2,1)S(1)}, u32[]{:S(2)}, u32[]{:S(2)}) %collective-permute-start.21) | collective-permute-done | bytes 73760 | tf_op jit(solution)/shard_map/ppermute | solution.py:405
  67.9 6.1 %collective-permute-start.24 = (bf16[96,384]{1,0:T(8,128)(2,1)S(1)}, bf16[96,384]{1,0:T(8,128)(2,1)S(1)}, u32[]{:S(2)}, u32[]{:S(2)}) collective-permute-start(bf16[96,384]{1,0:T(8,128)(2,1)S(1)} %add_convert_fusion.3), channel_id=1, source_target_pairs={{0,124},{1,125},{2,126},{3,127},{4,104},{5,105},{6,106},{7,107},{8... | collective-permute-start | bytes 221192 | tf_op jit(solution)/shard_map/ppermute | solution.py:405
  74.0 1.2 %collective-permute-start.22 = (bf16[96,384]{1,0:T(8,128)(2,1)S(1)}, bf16[96,384]{1,0:T(8,128)(2,1)S(1)}, u32[]{:S(2)}, u32[]{:S(2)}) collective-permute-start(bf16[96,384]{1,0:T(8,128)(2,1)S(1)} %add_convert_fusion.3), channel_id=1, source_target_pairs={{0,96},{1,29},{2,98},{3,31},{4,100},{5,9},{6,102},{7,11},{8,104},{... | collective-permute-start | bytes 221192 | tf_op jit(solution)/shard_map/ppermute | solution.py:405
  75.2 1.2 %collective-permute-done.24 = bf16[96,384]{1,0:T(8,128)(2,1)S(1)} collective-permute-done((bf16[96,384]{1,0:T(8,128)(2,1)S(1)}, bf16[96,384]{1,0:T(8,128)(2,1)S(1)}, u32[]{:S(2)}, u32[]{:S(2)}) %collective-permute-start.24) | collective-permute-done | bytes 73760 | tf_op jit(solution)/shard_map/ppermute | solution.py:405
  76.4 2.0 %collective-permute-done.23 = bf16[96,384]{1,0:T(8,128)(2,1)S(1)} collective-permute-done((bf16[96,384]{1,0:T(8,128)(2,1)S(1)}, bf16[96,384]{1,0:T(8,128)(2,1)S(1)}, u32[]{:S(2)}, u32[]{:S(2)}) %collective-permute-start.23) | collective-permute-done | bytes 73760 | tf_op jit(solution)/shard_map/ppermute | solution.py:405
  78.4 1.2 %collective-permute-done.22 = bf16[96,384]{1,0:T(8,128)(2,1)S(1)} collective-permute-done((bf16[96,384]{1,0:T(8,128)(2,1)S(1)}, bf16[96,384]{1,0:T(8,128)(2,1)S(1)}, u32[]{:S(2)}, u32[]{:S(2)}) %collective-permute-start.22) | collective-permute-done | bytes 73760 | tf_op jit(solution)/shard_map/ppermute | solution.py:405
  79.7 0.9 collective-permute-start.25
  80.5 5.1 %collective-permute-done.25 = bf16[96,384]{1,0:T(8,128)(2,1)S(1)} collective-permute-done((bf16[96,384]{1,0:T(8,128)(2,1)S(1)}, bf16[96,384]{1,0:T(8,128)(2,1)S(1)}, u32[]{:S(2)}, u32[]{:S(2)}) %collective-permute-start.25) | collective-permute-done | bytes 73760 | tf_op jit(solution)/shard_map/ppermute | solution.py:405
  85.6 2.9 %collective-permute-start.26 = (bf16[96,384]{1,0:T(8,128)(2,1)S(1)}, bf16[96,384]{1,0:T(8,128)(2,1)S(1)}, u32[]{:S(2)}, u32[]{:S(2)}) collective-permute-start(bf16[96,384]{1,0:T(8,128)(2,1)S(1)} %add_convert_fusion.1), channel_id=1, source_target_pairs={{0,12},{1,129},{2,14},{3,131},{4,24},{5,133},{6,26},{7,135},{8,20}... | collective-permute-start | bytes 221192 | tf_op jit(solution)/shard_map/ppermute | solution.py:405
  88.6 4.9 %collective-permute-done.26 = bf16[96,384]{1,0:T(8,128)(2,1)S(1)} collective-permute-done((bf16[96,384]{1,0:T(8,128)(2,1)S(1)}, bf16[96,384]{1,0:T(8,128)(2,1)S(1)}, u32[]{:S(2)}, u32[]{:S(2)}) %collective-permute-start.26) | collective-permute-done | bytes 73760 | tf_op jit(solution)/shard_map/ppermute | solution.py:405
  93.6 0.8 collective-permute-start.28
  94.4 2.7 %collective-permute-start.27 = (bf16[96,384]{1,0:T(8,128)(2,1)S(1)}, bf16[96,384]{1,0:T(8,128)(2,1)S(1)}, u32[]{:S(2)}, u32[]{:S(2)}) collective-permute-start(bf16[96,384]{1,0:T(8,128)(2,1)S(1)} %add_convert_fusion.p0), channel_id=1, source_target_pairs={{0,32},{1,5},{2,34},{3,7},{4,36},{5,1},{6,38},{7,3},{8,40},{9,13},... | collective-permute-start | bytes 221192 | tf_op jit(solution)/shard_map/ppermute | solution.py:405
  97.0 1.1 %decode.1 = bf16[512,384]{1,0:T(8,128)(2,1)} custom-call(bf16[256,384]{1,0:T(8,128)(2,1)S(1)} %get-tuple-element.54.front_rows, bf16[256,384]{1,0:T(8,128)(2,1)S(1)} %get-tuple-element.57.back_rows, bf16[384,384]{1,0:T(8,128)(2,1)S(1)} %copy-done.2), custom_call_target="tpu_custom_call" | custom-call | flops 150994944 | bytes 1048576 | tf_op jit(solution)/shard_map/decode/pallas_call | solution.py:371
  98.2 0.6 collective-permute-done.29.p3
  98.8 0.8 collective-permute-done.27.p1
  99.6 1.4 %assemble.1 = f32[384,384]{1,0:T(8,128)} custom-call(s32[6]{0:T(128)S(1)} %stack.23.ids, bf16[96,384]{1,0:T(8,128)(2,1)S(1)} %add_convert_fusion.p0, bf16[96,384]{1,0:T(8,128)(2,1)S(1)} %collective-permute-done.27.p1, bf16[96,384]{1,0:T(8,128)(2,1)S(1)} %collective-permute-done.28.p2, bf16[96,384]{1,0:T(8,128)(2,1)S(1)} %collective-permute-done.29.p3), custom_call_target="tpu_custom_call" | custom-call | bytes 1048576 | tf_op jit(solution)/shard_map/assemble/pallas_call | solution.py:425
  (38 shorter events, 1.4 us)
Async XLA Ops:
  0.6 16.0 %copy-start.3 = (s32[1,65536]{1,0:T(1,128)S(1)}, s32[1,65536]{1,0:T(1,128)}, u32[]{:S(2)}) copy-start(s32[1,65536]{1,0:T(1,128)} %param.6) | copy-start | bytes 786436
  1.8 14.4 %collective-permute-start = (bf16[256,384]{1,0:T(8,128)(2,1)S(1)}, bf16[256,384]{1,0:T(8,128)(2,1)S(1)}, u32[]{:S(2)}, u32[]{:S(2)}) collective-permute-start(bf16[256,384]{1,0:T(8,128)(2,1)S(1)} %get-tuple-element.32.refs_1_), channel_id=1, source_target_pairs={{0,2},{1,3},{2,0},{3,1},{4,6},{5,7},{6,4},{7,5},{8,10},{9,11},{10,... | collective-permute-start | bytes 589832 | tf_op jit(solution)/shard_map/ppermute | solution.py:268
  3.4 12.7 %collective-permute-start.4 = (bf16[256,384]{1,0:T(8,128)(2,1)S(1)}, bf16[256,384]{1,0:T(8,128)(2,1)S(1)}, u32[]{:S(2)}, u32[]{:S(2)}) collective-permute-start(bf16[256,384]{1,0:T(8,128)(2,1)S(1)} %get-tuple-element.36.refs_2_), channel_id=1, source_target_pairs={{0,130},{1,131},{2,128},{3,129},{128,2},{129,3},{130,0},{131,1},{4... | collective-permute-start | bytes 589832 | tf_op jit(solution)/shard_map/ppermute | solution.py:269
  5.6 14.7 %collective-permute-start.3 = (bf16[512,384]{1,0:T(8,128)(2,1)}, bf16[512,384]{1,0:T(8,128)(2,1)S(1)}, u32[]{:S(2)}, u32[]{:S(2)}) collective-permute-start(bf16[512,384]{1,0:T(8,128)(2,1)} %param.7), channel_id=1, source_target_pairs={{0,1},{1,0},{2,3},{3,2},{4,5},{5,4},{6,7},{7,6},{8,9},{9,8},{10,11... | collective-permute-start | bytes 1179656 | tf_op jit(solution)/shard_map/ppermute | solution.py:270
  6.8 6.0 %collective-permute-start.1 = (bf16[16,128]{1,0:T(8,128)(2,1)S(1)}, bf16[16,128]{1,0:T(8,128)(2,1)S(1)}, u32[]{:S(2)}, u32[]{:S(2)}) collective-permute-start(bf16[16,128]{1,0:T(8,128)(2,1)S(1)} %bitcast.15), channel_id=1, source_target_pairs={{0,4},{4,8},{8,12},{12,16},{16,20},{20,24},{24,28},{28,32},{32,36}... | collective-permute-start | bytes 12296 | tf_op jit(solution)/shard_map/ppermute | solution.py:271
  10.6 5.5 %collective-permute-start.2 = (bf16[16,128]{1,0:T(8,128)(2,1)S(1)}, bf16[16,128]{1,0:T(8,128)(2,1)S(1)}, u32[]{:S(2)}, u32[]{:S(2)}) collective-permute-start(bf16[16,128]{1,0:T(8,128)(2,1)S(1)} %bitcast.14), channel_id=1, source_target_pairs={{4,0},{8,4},{12,8},{16,12},{20,16},{24,20},{28,24},{32,28},{36,32}... | collective-permute-start | bytes 12296 | tf_op jit(solution)/shard_map/ppermute | solution.py:272
  16.1 4.1 %collective-permute-start.5 = (bf16[256,384]{1,0:T(8,128)(2,1)S(1)}, bf16[256,384]{1,0:T(8,128)(2,1)S(1)}, u32[]{:S(2)}, u32[]{:S(2)}) collective-permute-start(bf16[256,384]{1,0:T(8,128)(2,1)S(1)} %collective-permute-done.refs_4_), channel_id=1, source_target_pairs={{0,1},{1,0},{2,3},{3,2},{4,5},{5,4},{6,7},{7,6},{8,9},{9,8},{10,11... | collective-permute-start | bytes 589832 | tf_op jit(solution)/shard_map/ppermute | solution.py:275
  16.1 4.1 %collective-permute-start.6 = (bf16[256,384]{1,0:T(8,128)(2,1)S(1)}, bf16[256,384]{1,0:T(8,128)(2,1)S(1)}, u32[]{:S(2)}, u32[]{:S(2)}) collective-permute-start(bf16[256,384]{1,0:T(8,128)(2,1)S(1)} %collective-permute-done.4.refs_5_), channel_id=1, source_target_pairs={{0,1},{1,0},{2,3},{3,2},{4,5},{5,4},{6,7},{7,6},{8,9},{9,8},{10,11... | collective-permute-start | bytes 589832 | tf_op jit(solution)/shard_map/ppermute | solution.py:276
  17.5 2.8 %copy-start.1 = (f32[3,1536]{1,0:T(4,128)S(1)}, f32[3,1536]{1,0:T(4,128)}, u32[]{:S(2)}) copy-start(f32[3,1536]{1,0:T(4,128)} %refs_8_.9) | copy-start | bytes 55300
  24.9 7.8 %collective-permute-start.8 = (bf16[304,384]{1,0:T(8,128)(2,1)S(1)}, bf16[304,384]{1,0:T(8,128)(2,1)S(1)}, u32[]{:S(2)}, u32[]{:S(2)}) collective-permute-start(bf16[304,384]{1,0:T(8,128)(2,1)S(1)} %get-tuple-element.41.refs_0_), channel_id=1, source_target_pairs={{0,2},{1,3},{2,0},{3,1},{4,6},{5,7},{6,4},{7,5},{8,10},{9,11},{10,... | collective-permute-start | bytes 700424 | tf_op jit(solution)/shard_map/ppermute | solution.py:298
  25.6 7.9 %collective-permute-start.7 = (bf16[304,384]{1,0:T(8,128)(2,1)S(1)}, bf16[304,384]{1,0:T(8,128)(2,1)S(1)}, u32[]{:S(2)}, u32[]{:S(2)}) collective-permute-start(bf16[304,384]{1,0:T(8,128)(2,1)S(1)} %get-tuple-element.41.refs_0_), channel_id=1, source_target_pairs={{0,1},{1,0},{2,3},{3,2},{4,5},{5,4},{6,7},{7,6},{8,9},{9,8},{10,11... | collective-permute-start | bytes 700424 | tf_op jit(solution)/shard_map/ppermute | solution.py:298
  32.6 1.5 %collective-permute-start.9 = (bf16[304,384]{1,0:T(8,128)(2,1)S(1)}, bf16[304,384]{1,0:T(8,128)(2,1)S(1)}, u32[]{:S(2)}, u32[]{:S(2)}) collective-permute-start(bf16[304,384]{1,0:T(8,128)(2,1)S(1)} %collective-permute-done.8.refs_2_), channel_id=1, source_target_pairs={{0,1},{1,0},{2,3},{3,2},{4,5},{5,4},{6,7},{7,6},{8,9},{9,8},{10,11... | collective-permute-start | bytes 700424 | tf_op jit(solution)/shard_map/ppermute | solution.py:303
  32.6 7.1 %collective-permute-start.13 = (bf16[240,384]{1,0:T(8,128)(2,1)S(1)}, bf16[240,384]{1,0:T(8,128)(2,1)S(1)}, u32[]{:S(2)}, u32[]{:S(2)}) collective-permute-start(bf16[240,384]{1,0:T(8,128)(2,1)S(1)} %get-tuple-element.42.refs_4_), channel_id=1, source_target_pairs={{0,2},{1,3},{2,0},{3,1},{4,6},{5,7},{6,4},{7,5},{8,10},{9,11},{10,... | collective-permute-start | bytes 552968 | tf_op jit(solution)/shard_map/ppermute | solution.py:298
  33.3 7.3 %collective-permute-start.12 = (bf16[240,384]{1,0:T(8,128)(2,1)S(1)}, bf16[240,384]{1,0:T(8,128)(2,1)S(1)}, u32[]{:S(2)}, u32[]{:S(2)}) collective-permute-start(bf16[240,384]{1,0:T(8,128)(2,1)S(1)} %get-tuple-element.42.refs_4_), channel_id=1, source_target_pairs={{0,1},{1,0},{2,3},{3,2},{4,5},{5,4},{6,7},{7,6},{8,9},{9,8},{10,11... | collective-permute-start | bytes 552968 | tf_op jit(solution)/shard_map/ppermute | solution.py:298
  39.7 9.3 %copy-start = (bf16[1,512,384]{2,1,0:T(8,128)(2,1)S(1)}, bf16[1,512,384]{2,1,0:T(8,128)(2,1)}, u32[]{:S(2)}) copy-start(bf16[1,512,384]{2,1,0:T(8,128)(2,1)} %param.11) | copy-start | bytes 1179652
  39.7 1.4 %collective-permute-start.14 = (bf16[240,384]{1,0:T(8,128)(2,1)S(1)}, bf16[240,384]{1,0:T(8,128)(2,1)S(1)}, u32[]{:S(2)}, u32[]{:S(2)}) collective-permute-start(bf16[240,384]{1,0:T(8,128)(2,1)S(1)} %collective-permute-done.13.refs_6_), channel_id=1, source_target_pairs={{0,1},{1,0},{2,3},{3,2},{4,5},{5,4},{6,7},{7,6},{8,9},{9,8},{10,11... | collective-permute-start | bytes 552968 | tf_op jit(solution)/shard_map/ppermute | solution.py:303
  39.7 7.8 %collective-permute-start.11 = (bf16[288,384]{1,0:T(8,128)(2,1)S(1)}, bf16[288,384]{1,0:T(8,128)(2,1)S(1)}, u32[]{:S(2)}, u32[]{:S(2)}) collective-permute-start(bf16[288,384]{1,0:T(8,128)(2,1)S(1)} %get-tuple-element.47.refs_0_), channel_id=1, source_target_pairs={{0,2},{1,3},{2,0},{3,1},{4,6},{5,7},{6,4},{7,5},{8,10},{9,11},{10,... | collective-permute-start | bytes 663560 | tf_op jit(solution)/shard_map/ppermute | solution.py:298
  40.4 8.1 %collective-permute-start.10 = (bf16[288,384]{1,0:T(8,128)(2,1)S(1)}, bf16[288,384]{1,0:T(8,128)(2,1)S(1)}, u32[]{:S(2)}, u32[]{:S(2)}) collective-permute-start(bf16[288,384]{1,0:T(8,128)(2,1)S(1)} %get-tuple-element.47.refs_0_), channel_id=1, source_target_pairs={{0,1},{1,0},{2,3},{3,2},{4,5},{5,4},{6,7},{7,6},{8,9},{9,8},{10,11... | collective-permute-start | bytes 663560 | tf_op jit(solution)/shard_map/ppermute | solution.py:298
  47.5 1.5 %collective-permute-start.15 = (bf16[288,384]{1,0:T(8,128)(2,1)S(1)}, bf16[288,384]{1,0:T(8,128)(2,1)S(1)}, u32[]{:S(2)}, u32[]{:S(2)}) collective-permute-start(bf16[288,384]{1,0:T(8,128)(2,1)S(1)} %collective-permute-done.11.refs_2_), channel_id=1, source_target_pairs={{0,1},{1,0},{2,3},{3,2},{4,5},{5,4},{6,7},{7,6},{8,9},{9,8},{10,11... | collective-permute-start | bytes 663560 | tf_op jit(solution)/shard_map/ppermute | solution.py:303
  47.5 7.3 %collective-permute-start.17 = (bf16[256,384]{1,0:T(8,128)(2,1)S(1)}, bf16[256,384]{1,0:T(8,128)(2,1)S(1)}, u32[]{:S(2)}, u32[]{:S(2)}) collective-permute-start(bf16[256,384]{1,0:T(8,128)(2,1)S(1)} %get-tuple-element.49.refs_4_), channel_id=1, source_target_pairs={{0,2},{1,3},{2,0},{3,1},{4,6},{5,7},{6,4},{7,5},{8,10},{9,11},{10,... | collective-permute-start | bytes 589832 | tf_op jit(solution)/shard_map/ppermute | solution.py:298
  48.2 6.6 %collective-permute-start.16 = (bf16[256,384]{1,0:T(8,128)(2,1)S(1)}, bf16[256,384]{1,0:T(8,128)(2,1)S(1)}, u32[]{:S(2)}, u32[]{:S(2)}) collective-permute-start(bf16[256,384]{1,0:T(8,128)(2,1)S(1)} %get-tuple-element.49.refs_4_), channel_id=1, source_target_pairs={{0,1},{1,0},{2,3},{3,2},{4,5},{5,4},{6,7},{7,6},{8,9},{9,8},{10,11... | collective-permute-start | bytes 589832 | tf_op jit(solution)/shard_map/ppermute | solution.py:298
  54.9 1.4 %collective-permute-start.18 = (bf16[256,384]{1,0:T(8,128)(2,1)S(1)}, bf16[256,384]{1,0:T(8,128)(2,1)S(1)}, u32[]{:S(2)}, u32[]{:S(2)}) collective-permute-start(bf16[256,384]{1,0:T(8,128)(2,1)S(1)} %collective-permute-done.17.refs_6_), channel_id=1, source_target_pairs={{0,1},{1,0},{2,3},{3,2},{4,5},{5,4},{6,7},{7,6},{8,9},{9,8},{10,11... | collective-permute-start | bytes 589832 | tf_op jit(solution)/shard_map/ppermute | solution.py:303
  59.1 38.0 %copy-start.2 = (bf16[384,384]{1,0:T(8,128)(2,1)S(1)}, bf16[384,384]{1,0:T(8,128)(2,1)}, u32[]{:S(2)}) copy-start(bf16[384,384]{1,0:T(8,128)(2,1)} %weights.1) | copy-start | bytes 884740
  59.1 5.1 %collective-permute-start.19 = (bf16[96,384]{1,0:T(8,128)(2,1)S(1)}, bf16[96,384]{1,0:T(8,128)(2,1)S(1)}, u32[]{:S(2)}, u32[]{:S(2)}) collective-permute-start(bf16[96,384]{1,0:T(8,128)(2,1)S(1)} %get-tuple-element.59), channel_id=1, source_target_pairs={{0,32},{1,5},{2,34},{3,7},{4,36},{5,1},{6,38},{7,3},{8,40},{9,13},... | collective-permute-start | bytes 221192 | tf_op jit(solution)/shard_map/ppermute | solution.py:405
  60.9 5.1 %collective-permute-start.20 = (bf16[96,384]{1,0:T(8,128)(2,1)S(1)}, bf16[96,384]{1,0:T(8,128)(2,1)S(1)}, u32[]{:S(2)}, u32[]{:S(2)}) collective-permute-start(bf16[96,384]{1,0:T(8,128)(2,1)S(1)} %get-tuple-element.60), channel_id=1, source_target_pairs={{0,4},{1,33},{2,6},{3,35},{4,0},{5,37},{6,2},{7,39},{8,12},{9,41},... | collective-permute-start | bytes 221192 | tf_op jit(solution)/shard_map/ppermute | solution.py:405
  62.6 5.3 %collective-permute-start.21 = (bf16[96,384]{1,0:T(8,128)(2,1)S(1)}, bf16[96,384]{1,0:T(8,128)(2,1)S(1)}, u32[]{:S(2)}, u32[]{:S(2)}) collective-permute-start(bf16[96,384]{1,0:T(8,128)(2,1)S(1)} %get-tuple-element.61), channel_id=1, source_target_pairs={{0,36},{1,37},{2,38},{3,39},{4,32},{5,33},{6,34},{7,35},{8,44},{9,... | collective-permute-start | bytes 221192 | tf_op jit(solution)/shard_map/ppermute | solution.py:405
  67.9 8.5 %collective-permute-start.24 = (bf16[96,384]{1,0:T(8,128)(2,1)S(1)}, bf16[96,384]{1,0:T(8,128)(2,1)S(1)}, u32[]{:S(2)}, u32[]{:S(2)}) collective-permute-start(bf16[96,384]{1,0:T(8,128)(2,1)S(1)} %add_convert_fusion.3), channel_id=1, source_target_pairs={{0,124},{1,125},{2,126},{3,127},{4,104},{5,105},{6,106},{7,107},{8... | collective-permute-start | bytes 221192 | tf_op jit(solution)/shard_map/ppermute | solution.py:405
  74.0 4.4 %collective-permute-start.23 = (bf16[96,384]{1,0:T(8,128)(2,1)S(1)}, bf16[96,384]{1,0:T(8,128)(2,1)S(1)}, u32[]{:S(2)}, u32[]{:S(2)}) collective-permute-start(bf16[96,384]{1,0:T(8,128)(2,1)S(1)} %add_convert_fusion.3), channel_id=1, source_target_pairs={{0,28},{1,97},{2,30},{3,99},{4,8},{5,101},{6,10},{7,103},{8,4},{9,... | collective-permute-start | bytes 221192 | tf_op jit(solution)/shard_map/ppermute | solution.py:405
  74.0 5.6 %collective-permute-start.22 = (bf16[96,384]{1,0:T(8,128)(2,1)S(1)}, bf16[96,384]{1,0:T(8,128)(2,1)S(1)}, u32[]{:S(2)}, u32[]{:S(2)}) collective-permute-start(bf16[96,384]{1,0:T(8,128)(2,1)S(1)} %add_convert_fusion.3), channel_id=1, source_target_pairs={{0,96},{1,29},{2,98},{3,31},{4,100},{5,9},{6,102},{7,11},{8,104},{... | collective-permute-start | bytes 221192 | tf_op jit(solution)/shard_map/ppermute | solution.py:405
  79.7 5.9 %collective-permute-start.25 = (bf16[96,384]{1,0:T(8,128)(2,1)S(1)}, bf16[96,384]{1,0:T(8,128)(2,1)S(1)}, u32[]{:S(2)}, u32[]{:S(2)}) collective-permute-start(bf16[96,384]{1,0:T(8,128)(2,1)S(1)} %add_convert_fusion.2), channel_id=1, source_target_pairs={{0,128},{1,13},{2,130},{3,15},{4,132},{5,25},{6,134},{7,27},{8,136... | collective-permute-start | bytes 221192 | tf_op jit(solution)/shard_map/ppermute | solution.py:405
  85.6 7.8 %collective-permute-start.26 = (bf16[96,384]{1,0:T(8,128)(2,1)S(1)}, bf16[96,384]{1,0:T(8,128)(2,1)S(1)}, u32[]{:S(2)}, u32[]{:S(2)}) collective-permute-start(bf16[96,384]{1,0:T(8,128)(2,1)S(1)} %add_convert_fusion.1), channel_id=1, source_target_pairs={{0,12},{1,129},{2,14},{3,131},{4,24},{5,133},{6,26},{7,135},{8,20}... | collective-permute-start | bytes 221192 | tf_op jit(solution)/shard_map/ppermute | solution.py:405
  93.5 5.4 %collective-permute-start.29 = (bf16[96,384]{1,0:T(8,128)(2,1)S(1)}, bf16[96,384]{1,0:T(8,128)(2,1)S(1)}, u32[]{:S(2)}, u32[]{:S(2)}) collective-permute-start(bf16[96,384]{1,0:T(8,128)(2,1)S(1)} %add_convert_fusion.p0), channel_id=1, source_target_pairs={{0,36},{1,37},{2,38},{3,39},{4,32},{5,33},{6,34},{7,35},{8,44},{9,... | collective-permute-start | bytes 221192 | tf_op jit(solution)/shard_map/ppermute | solution.py:405
  93.6 5.3 %collective-permute-start.28 = (bf16[96,384]{1,0:T(8,128)(2,1)S(1)}, bf16[96,384]{1,0:T(8,128)(2,1)S(1)}, u32[]{:S(2)}, u32[]{:S(2)}) collective-permute-start(bf16[96,384]{1,0:T(8,128)(2,1)S(1)} %add_convert_fusion.p0), channel_id=1, source_target_pairs={{0,4},{1,33},{2,6},{3,35},{4,0},{5,37},{6,2},{7,39},{8,12},{9,41},... | collective-permute-start | bytes 221192 | tf_op jit(solution)/shard_map/ppermute | solution.py:405
  94.4 5.2 %collective-permute-start.27 = (bf16[96,384]{1,0:T(8,128)(2,1)S(1)}, bf16[96,384]{1,0:T(8,128)(2,1)S(1)}, u32[]{:S(2)}, u32[]{:S(2)}) collective-permute-start(bf16[96,384]{1,0:T(8,128)(2,1)S(1)} %add_convert_fusion.p0), channel_id=1, source_target_pairs={{0,32},{1,5},{2,34},{3,7},{4,36},{5,1},{6,38},{7,3},{8,40},{9,13},... | collective-permute-start | bytes 221192 | tf_op jit(solution)/shard_map/ppermute | solution.py:405

commit v5 on v4

--- a/solution.py
+++ b/solution.py
@@ -53,7 +53,7 @@
     for t in range(3):
         first = at + (t - 1) * dilation
         part = jnp.dot(
-            normed[first : first + rows, :], weights[t][...], preferred_element_type=jnp.float32
+            normed[first : first + rows, :], weights[t], preferred_element_type=jnp.float32
         )
         update = part if update is None else update + part
     return update
@@ -63,54 +63,39 @@
     ref[first : first + rows, :] = jnp.zeros((rows, ref.shape[1]), ref.dtype)
 
 
-def start_weights(ids, layer, taps, w_hbm, outs, sems):
-    copies = []
-    for n, (t, out) in enumerate(zip(taps, outs)):
-        width = out.shape[1]
-        for k in range(4):
-            copies.append(
-                pltpu.make_async_copy(
-                    w_hbm.at[layer, t, pl.ds((ids[0] ^ k) * width, width), :],
-                    out.at[pl.ds(k * width, width), :],
-                    sems.at[n, k],
-                )
-            )
-            copies[-1].start()
-    return copies
-
-
-def wait_all(copies):
-    for copy in copies:
-        copy.wait()
-
-
-def one_hot(bins, count, ids, before, own, after, w_hbm, onehot, *refs):
-    copies = start_weights(ids, 0, range(3), w_hbm, refs[:3], refs[3])
-    letters = jnp.concatenate([before[...], own[...], after[...]], axis=0)
+def one_hot(letters):
+    letters = letters.astype(jnp.float32).astype(jnp.bfloat16)
     lane = lax.broadcasted_iota(jnp.int32, (PATCH, 4 * PATCH), 1)
     row = lax.broadcasted_iota(jnp.int32, (PATCH, 4 * PATCH), 0)
     spread = jnp.where(lane // 4 == row, 1.0, 0.0).astype(jnp.bfloat16)
     repeated = jnp.dot(letters, spread, preferred_element_type=jnp.float32)
     base = (lax.broadcasted_iota(jnp.int32, (1, 4 * PATCH), 1) % 4).astype(jnp.float32)
-    inside = in_sequence(ids, 0, bins + 2 * HALO, bins, count)
-    onehot[...] = (jnp.where(repeated == base, 1.0, 0.0) * inside).astype(jnp.bfloat16)
-    wait_all(copies)
-
-
-def fetching(kernel, inputs, results, layer, taps):
-    def run(ids, *refs):
-        ins, (w_hbm, *refs) = refs[:inputs], refs[inputs:]
-        outs, later, refs = refs[:results], refs[results : results + len(taps)], refs[results + len(taps) :]
-        copies = start_weights(ids, layer, taps, w_hbm, later, refs[-1])
-        kernel(ids, *ins, *outs, *refs[:-1])
-        wait_all(copies)
-
-    return run
-
-
-def first_layer(span, bins, count, ids, onehot, own_a, own_b, w1, w2a, w2b, w3a, w3b, gains, *refs):
+    return jnp.where(repeated == base, 1.0, 0.0).astype(jnp.bfloat16)
+
+
+def fetch(layer, ids, w_hbm, weights, sems):
+    width = weights.shape[2]
+    copies = []
+    for t in range(3):
+        for k in range(4):
+            copies.append(
+                pltpu.make_async_copy(
+                    w_hbm.at[layer, t, pl.ds((ids[0] ^ k) * width, width), :],
+                    weights.at[t, pl.ds(k * width, width), :],
+                    sems.at[t, k],
+                )
+            )
+            copies[-1].start()
+    for copy in copies:
+        copy.wait()
+
+
+def prepare(letters, onehot):
+    onehot[...] = one_hot(letters[...])
+
+
+def first_layer(span, bins, count, ids, onehot, halo, own_a, own_b, w1, w2a, w2b, w3a, w3b, gains, weights, out, normed, stream):
     low, high = span
-    weights, (out, normed, stream) = refs[:3], refs[3:]
     width = out.shape[1]
     first, last = max(low - HALO, 0), min(high + HALO, bins + 2 * HALO)
     rows = last - first
@@ -125,9 +110,14 @@
         ],
         axis=1,
     )
-    stream[...] = jnp.dot(
-        onehot[first:last, :], stem, preferred_element_type=jnp.float32
-    ).astype(jnp.bfloat16)
+    beyond = one_hot(halo[...])
+    if low == 0:
+        beyond = jnp.where(ids[1] > 0, beyond, jnp.zeros_like(beyond))
+        lines = jnp.concatenate([beyond, onehot[0 : last - HALO, :]], axis=0)
+    else:
+        beyond = jnp.where((ids[1] + 1) * bins < count, beyond, jnp.zeros_like(beyond))
+        lines = jnp.concatenate([onehot[first - HALO : bins, :], beyond], axis=0)
+    stream[...] = jnp.dot(lines, stem, preferred_element_type=jnp.float32).astype(jnp.bfloat16)
 
     def read(at, n):
         return [stream[at : at + n, k * width : (k + 1) * width] for k in range(4)]
@@ -140,7 +130,7 @@
 
 
 def front(layer, dilation, span, bins, count, ids, *refs):
-    pieces, gains, weights, (out, normed) = refs[:4], refs[4], refs[5:8], refs[8:]
+    pieces, (gains, weights, out, normed) = refs[:4], refs[4:]
     low, high = span
     rows = high + HALO
     clear(normed, 0, PAD)
@@ -157,7 +147,7 @@
 
 
 def back(layer, dilation, span, bins, count, ids, *refs):
-    fronts, backs, gains, weights, (out, normed) = refs[:4], refs[4:8], refs[8], refs[9:12], refs[12:]
+    fronts, backs, (gains, weights, out, normed) = refs[:4], refs[4:8], refs[8:]
     low, high = span
     first = low - HALO
     joint = fronts[0].shape[0]
@@ -187,14 +177,14 @@
 
 
 def last_front(span, bins, ids, *refs):
-    refs, (upstream, out, grad, normed) = refs[:8], refs[8:]
+    refs, (upstream, out, grad, normed) = refs[:6], refs[6:]
     front(2, 4 * FIRST_DILATION0, span, bins, 0, ids, *refs, out, normed)
     low, high = span
     grad[...] = gradient(out[...], upstream[low - HALO : high - HALO, :])
 
 
 def last_back(span, bins, ids, *refs):
-    refs, (upstream, before, out, g0, g1, g2, g3, normed, grad) = refs[:12], refs[12:]
+    refs, (upstream, before, out, g0, g1, g2, g3, normed, grad) = refs[:10], refs[10:]
     back(2, 4 * FIRST_DILATION0, span, bins, 0, ids, *refs, out, normed)
     low, high = span
     grad[...] = before[...] + gradient(out[...], upstream[low - HALO : high - HALO, :])
@@ -228,7 +218,7 @@
     return [(i, partner(i)) for i in range(size)]
 
 
-def call(name, kernel, outs, in_specs, scratch=(), flops=0, megabytes=40):
+def call(name, kernel, outs, in_specs, scratch=(), flops=0, megabytes=46):
     many = isinstance(outs, (list, tuple))
     return pl.pallas_call(
         kernel,
@@ -268,22 +258,29 @@
     w2a = across(stem_a)
     w2b = far(stem_b)
     w1 = other_core(stem)
-    before = lax.ppermute(letters[bins - HALO :].astype(bf16), "seq", up)
-    after = lax.ppermute(letters[:HALO].astype(bf16), "seq", down)
-    letters = lax.optimization_barrier(letters.astype(bf16))
-    w2a, before, after = lax.optimization_barrier((w2a, before, after))
+    before = lax.ppermute(letters[bins - HALO :], "seq", up)
+    def fetched(layer, *done):
+        return call(
+            "fetch",
+            functools.partial(fetch, layer),
+            jax.ShapeDtypeStruct(conv_weight.shape[1:], bf16),
+            [SMEM, HBM],
+            [pltpu.SemaphoreType.DMA((3, 4))],
+            flops=10**9,
+        )(tie(ids, *done) if done else ids, conv_weight)
+
+    onehot = call(
+        "prepare",
+        prepare,
+        jax.ShapeDtypeStruct((bins, 4 * PATCH), bf16),
+        [VMEM],
+        flops=10**9,
+    )(letters)
+    after = lax.ppermute(letters[:HALO], "seq", down)
+    weights = fetched(0)
+    w2a = tie(w2a, before, after, onehot, weights)
     w3a = other_core(w2a)
     w3b = other_core(w2b)
-    tap = jax.ShapeDtypeStruct((4 * width, width), bf16)
-    tap_sems = pltpu.SemaphoreType.DMA((3, 4))
-    onehot, *weights = call(
-        "one_hot",
-        functools.partial(one_hot, bins, count),
-        [jax.ShapeDtypeStruct((rows, 4 * PATCH), bf16)] + [tap] * 3,
-        [SMEM] + [VMEM] * 3 + [HBM],
-        [tap_sems],
-        flops=10**9,
-    )(ids, before, letters, after, conv_weight)
 
     def shape(n):
         return jax.ShapeDtypeStruct((n, width), bf16)
@@ -303,71 +300,71 @@
         return own, beside, remote, other_core(remote)
 
     cut = bins // 2 + 3 * HALO
-    inputs = (onehot, stem_a, stem_b, w1, w2a, w2b, w3a, w3b, gains, *weights)
-    part, tap0 = call(
+    inputs = (stem_a, stem_b, w1, w2a, w2b, w3a, w3b, gains, weights)
+    part = call(
         "zero_front",
-        fetching(functools.partial(first_layer, (0, cut), bins, count), 12, 1, 1, (0,)),
-        [shape(cut), tap],
-        [SMEM] + [VMEM] * 12 + [HBM],
-        [normed(cut + HALO), pltpu.VMEM((cut + HALO, 4 * width), bf16), tap_sems],
+        functools.partial(first_layer, (0, cut), bins, count),
+        shape(cut),
+        [SMEM] + [VMEM] * 11,
+        [normed(cut + HALO), pltpu.VMEM((cut + HALO, 4 * width), bf16)],
         flops=work(cut),
-    )(ids, *inputs, conv_weight)
+    )(ids, onehot, before, *inputs)
     sent_front = exchange(part)
-    part, *taps = call(
+    part = call(
         "zero_back",
-        fetching(functools.partial(first_layer, (cut, rows), bins, count), 12, 1, 1, (1, 2)),
-        [shape(rows - cut), tap, tap],
-        [SMEM] + [VMEM] * 12 + [HBM],
-        [normed(rows - cut + HALO), pltpu.VMEM((rows - cut + HALO, 4 * width), bf16), tap_sems],
+        functools.partial(first_layer, (cut, rows), bins, count),
+        shape(rows - cut),
+        [SMEM] + [VMEM] * 11,
+        [normed(rows - cut + HALO), pltpu.VMEM((rows - cut + HALO, 4 * width), bf16)],
         flops=work(rows - cut),
-    )(ids, *inputs, conv_weight)
-    weights = (tap0, *taps)
+    )(ids, onehot, after, *inputs)
     sent_back = exchange(part)
-    fronts = finish(sent_front, part)
+    weights = fetched(1, part)
+    fronts = finish(sent_front, part, weights)
 
     cut = cut - HALO
     layer = (1, 2 * FIRST_DILATION0)
-    part, tap0 = call(
+    part = call(
         "one_front",
-        fetching(functools.partial(front, *layer, (0, cut), bins, count), 8, 1, 2, (0,)),
-        [shape(cut), tap],
-        [SMEM] + [VMEM] * 8 + [HBM],
-        [normed(cut + HALO), tap_sems],
+        functools.partial(front, *layer, (0, cut), bins, count),
+        shape(cut),
+        [SMEM] + [VMEM] * 6,
+        [normed(cut + HALO)],
         flops=work(cut),
-    )(ids, *fronts, gains, *weights, conv_weight)
+    )(ids, *fronts, gains, weights)
     sent_front = exchange(part)
     backs = finish(sent_back, part)
-    part, *taps = call(
+    part = call(
         "one_back",
-        fetching(functools.partial(back, *layer, (cut, rows), bins, count), 12, 1, 2, (1, 2)),
-        [shape(rows - cut), tap, tap],
-        [SMEM] + [VMEM] * 12 + [HBM],
-        [normed(rows - cut + HALO), tap_sems],
+        functools.partial(back, *layer, (cut, rows), bins, count),
+        shape(rows - cut),
+        [SMEM] + [VMEM] * 10,
+        [normed(rows - cut + HALO)],
         flops=work(rows - cut),
-    )(ids, *fronts, *backs, gains, *weights, conv_weight)
-    weights = (tap0, *taps)
+    )(ids, *fronts, *backs, gains, weights)
     sent_back = exchange(part)
-    fronts = finish(sent_front, part)
+    weights = fetched(2, part)
+    fronts = finish(sent_front, part, weights)
 
     cut = cut - HALO
     front_rows, front_grad = call(
         "two_front",
         functools.partial(last_front, (HALO, cut), bins),
         [shape(cut - HALO), jax.ShapeDtypeStruct((width, width), f32)],
-        [SMEM] + [VMEM] * 9,
+        [SMEM] + [VMEM] * 7,
         [normed(cut + HALO)],
         flops=work(cut - HALO),
-    )(ids, *fronts, gains, *weights, upstream[0])
+    )(ids, *fronts, gains, weights, upstream[0])
     backs = finish(sent_back, front_rows)
     back_rows, g0, g1, g2, g3 = call(
         "two_back",
         functools.partial(last_back, (cut, rows - HALO), bins),
         [shape(rows - HALO - cut), jax.ShapeDtypeStruct((width // 4, width), f32)]
         + [shape(width // 4)] * 3,
-        [SMEM] + [VMEM] * 14,
+        [SMEM] + [VMEM] * 12,
         [normed(rows - cut + HALO), pltpu.VMEM((width, width), f32)],
         flops=work(rows - HALO - cut),
-    )(ids, *fronts, *backs, gains, *weights, upstream[0], front_grad)
+    )(ids, *fronts, *backs, gains, weights, upstream[0], front_grad)
     decoded = call(
         "decode",
         decode,

time: 102 us -> 98.9 us (0.970)
  waiting for transfers between devices: 37.1 us -> 34.2 us
  other arithmetic: 2.01 us -> 0.12 us
  local copies, waits for them, and re-layouts: 1.27 us -> 2.83 us
    ppermute x2, waiting for transfers between devices: 3.37 us -> 0.01 us  [the longest x1 0.01 us: body(): before = lax.ppermute(letters[bins - HALO:], 'seq', up)]
    another operation x2 -> x0, other arithmetic: 1.88 us -> none
    pallas_call x5 -> x8, Pallas kernels: 19.5 us -> 19.5 us  [the longest x3 7.77 us: fetched(): call('fetch', functools.partial(fetch, layer), jax.ShapeDtypeStruct(conv_...]
  transfers between devices with their start and end apart: 30 -> 30, of which waited for: 19 -> 19; matrix products, arithmetic and copies ran while one was open for 2% -> 2% of each run, Pallas kernels for 19% -> 20%
where the time goes in v5:
time: 98.9 us; the launch traced here: 97.6 us
  waiting for transfers between devices  34.2 us (35%)
  starting transfers between devices  32 us (32%)
  Pallas kernels  27.5 us (28%)
  local copies, waits for them, and re-layouts  2.83 us (3%)
    ppermute x11, waiting for transfers between devices, swap(): return lax.ppermute(own, ('section', 'seq', 'chan'), perm)  20.8 us
    ppermute x11, starting transfers between devices, swap(): return lax.ppermute(own, ('section', 'seq', 'chan'), perm)  18.2 us
    ppermute x8, waiting for transfers between devices, exchange(): return (own, other_core(own), across(own))  9.05 us
    pallas_call x3, Pallas kernels, fetched(): call('fetch', functools.partial(fetch, layer), jax.ShapeDtypeStruct(conv_...  7.77 us
    ppermute x1, starting transfers between devices, body(): before = lax.ppermute(letters[bins - HALO:], 'seq', up)  3.81 us
    ppermute x8, starting transfers between devices, exchange(): return (own, other_core(own), across(own))  3.48 us
    pallas_call x1, Pallas kernels, body(): call('zero_front', functools.partial(first_layer, (0, cut), bins, count),...  3.43 us
    ppermute x4, waiting for transfers between devices, finish(): return (own, beside, remote, other_core(remote))  3.1 us
  transfers between devices with their start and end apart: 30, of which 19 were waited for; matrix products, arithmetic and copies ran while one was open for 2% of the time, Pallas kernels for 20%

profile of v5, /device:TPU:32, one launch (start us, length us, event | category | flops | bytes accessed | tf_op | source)
XLA Modules:
  0.0 97.6 jit_solution(16081804194433675717)
XLA Ops:
  0.7 1.1 %fusion = (bf16[256,384]{1,0:T(8,128)(2,1)S(1)}, bf16[256,384]{1,0:T(8,128)(2,1)S(1)}) fusion(bf16[512,384]{1,0:T(8,128)(2,1)} %param.7), kind=kLoop, calls=%fused_computation.4 | loop fusion | bytes 786432 | tf_op jit(solution)/shard_map/slice | solution.py:257
  1.8 1.7 %collective-permute-start.2 = (bf16[256,384]{1,0:T(8,128)(2,1)S(1)}, bf16[256,384]{1,0:T(8,128)(2,1)S(1)}, u32[]{:S(2)}, u32[]{:S(2)}) collective-permute-start(bf16[256,384]{1,0:T(8,128)(2,1)S(1)} %get-tuple-element.18.own_a), channel_id=1, source_target_pairs={{0,2},{1,3},{2,0},{3,1},{4,6},{5,7},{6,4},{7,5},{8,10},{9,11},{10,... | collective-permute-start | bytes 589832 | tf_op jit(solution)/shard_map/ppermute | solution.py:258
  3.5 2.2 %collective-permute-start.4 = (bf16[256,384]{1,0:T(8,128)(2,1)S(1)}, bf16[256,384]{1,0:T(8,128)(2,1)S(1)}, u32[]{:S(2)}, u32[]{:S(2)}) collective-permute-start(bf16[256,384]{1,0:T(8,128)(2,1)S(1)} %get-tuple-element.19.own_b), channel_id=1, source_target_pairs={{0,130},{1,131},{2,128},{3,129},{128,2},{129,3},{130,0},{131,1},{4... | collective-permute-start | bytes 589832 | tf_op jit(solution)/shard_map/ppermute | solution.py:259
  5.6 0.7 fusion.1
  6.4 3.8 %collective-permute-start = (s32[16,128]{1,0:T(8,128)S(1)}, s32[16,128]{1,0:T(8,128)S(1)}, u32[]{:S(2)}, u32[]{:S(2)}) collective-permute-start(s32[16,128]{1,0:T(8,128)S(1)} %bitcast.15), channel_id=1, source_target_pairs={{0,4},{4,8},{8,12},{12,16},{16,20},{20,24},{24,28},{28,32},{32,36}... | collective-permute-start | bytes 24584 | tf_op jit(solution)/shard_map/ppermute | solution.py:261
  10.2 2.0 %collective-permute-start.3 = (s32[16,128]{1,0:T(8,128)S(1)}, s32[16,128]{1,0:T(8,128)S(1)}, u32[]{:S(2)}, u32[]{:S(2)}) collective-permute-start(s32[16,128]{1,0:T(8,128)S(1)} %bitcast.14), channel_id=1, source_target_pairs={{4,0},{8,4},{12,8},{16,12},{20,16},{24,20},{28,24},{32,28},{36,32}... | collective-permute-start | bytes 24584 | tf_op jit(solution)/shard_map/ppermute | solution.py:279
  12.4 1.0 copy-done.3
  13.6 2.6 %fetch.3.weights = bf16[3,1536,384]{2,1,0:T(8,128)(2,1)S(1)} custom-call(s32[6]{0:T(128)S(1)} %stack.23.ids, bf16[3,3,1536,384]{3,2,1,0:T(8,128)(2,1)} %w_hbm.5), custom_call_target="tpu_custom_call" | custom-call | flops 1000000000 | bytes 1048576 | tf_op jit(solution)/shard_map/fetch/pallas_call | solution.py:263
  16.9 0.9 collective-permute-done.6.w3b
  18.1 3.4 %zero_front.1.refs_0_ = bf16[304,384]{1,0:T(8,128)(2,1)S(1)} custom-call(s32[6]{0:T(128)S(1)} %stack.23.ids, bf16[512,512]{1,0:T(8,128)(2,1)S(1)} %prepare.1.onehot, s32[16,128]{1,0:T(8,128)S(1)} %collective-permute-done.halo, bf16[256,384]{1,0:T(8,128)(2,1)S(1)} %get-tuple-element.18.own_a, bf16[256,384]{1,0:T(8,128)(2,1)S(1)} %get-tuple-element.19.own_b, ...), custom_call_target="tpu_custom_call" | custom-call | flops 1075838976 | bytes 1048576 | tf_op jit(solution)/shard_map/zero_front/pallas_call | solution.py:304
  21.5 0.8 collective-permute-start.8
  22.3 2.9 %zero_back.1.refs_4_ = bf16[240,384]{1,0:T(8,128)(2,1)S(1)} custom-call(s32[6]{0:T(128)S(1)} %stack.23.ids, bf16[512,512]{1,0:T(8,128)(2,1)S(1)} %prepare.1.onehot, s32[16,128]{1,0:T(8,128)S(1)} %collective-permute-done.3.halo, bf16[256,384]{1,0:T(8,128)(2,1)S(1)} %get-tuple-element.18.own_a, bf16[256,384]{1,0:T(8,128)(2,1)S(1)} %get-tuple-element.19.own_b, ...), custom_call_target="tpu_custom_call" | custom-call | flops 849346560 | bytes 1048576 | tf_op jit(solution)/shard_map/zero_back/pallas_call | solution.py:313
  25.2 2.6 %fetch.4.refs_5_.refs_9_ = bf16[3,1536,384]{2,1,0:T(8,128)(2,1)S(1)} custom-call(s32[6]{0:T(128)S(1)} %stack.23.ids, bf16[3,3,1536,384]{3,2,1,0:T(8,128)(2,1)} %w_hbm.5), custom_call_target="tpu_custom_call" | custom-call | flops 1000000000 | bytes 1048576 | tf_op jit(solution)/shard_map/fetch/pallas_call | solution.py:263
  27.8 1.6 %collective-permute-done.8.refs_2_ = bf16[304,384]{1,0:T(8,128)(2,1)S(1)} collective-permute-done((bf16[304,384]{1,0:T(8,128)(2,1)S(1)}, bf16[304,384]{1,0:T(8,128)(2,1)S(1)}, u32[]{:S(2)}, u32[]{:S(2)}) %collective-permute-start.8) | collective-permute-done | bytes 233504 | tf_op jit(solution)/shard_map/ppermute | solution.py:295
  29.5 0.7 collective-permute-start.13
  30.4 0.6 collective-permute-done.9.refs_3_
  30.9 2.6 %one_front.1.refs_0_ = bf16[288,384]{1,0:T(8,128)(2,1)S(1)} custom-call(s32[6]{0:T(128)S(1)} %stack.23.ids, bf16[304,384]{1,0:T(8,128)(2,1)S(1)} %zero_front.1.refs_0_, bf16[304,384]{1,0:T(8,128)(2,1)S(1)} %collective-permute-done.7.refs_1_, bf16[304,384]{1,0:T(8,128)(2,1)S(1)} %collective-permute-done.8.refs_2_, ...), custom_call_target="tpu_custom_call" | custom-call | flops 1019215872 | bytes 1048576 | tf_op jit(solution)/shard_map/one_front/pallas_call | solution.py:327
  33.6 2.9 %collective-permute-done.13.refs_6_ = bf16[240,384]{1,0:T(8,128)(2,1)S(1)} collective-permute-done((bf16[240,384]{1,0:T(8,128)(2,1)S(1)}, bf16[240,384]{1,0:T(8,128)(2,1)S(1)}, u32[]{:S(2)}, u32[]{:S(2)}) %collective-permute-start.13) | collective-permute-done | bytes 184352 | tf_op jit(solution)/shard_map/ppermute | solution.py:295
  36.5 0.7 collective-permute-start.11
  37.4 0.5 collective-permute-done.14.refs_7_
  37.9 2.4 %one_back.1.refs_4_ = bf16[256,384]{1,0:T(8,128)(2,1)S(1)} custom-call(s32[6]{0:T(128)S(1)} %stack.23.ids, bf16[304,384]{1,0:T(8,128)(2,1)S(1)} %zero_front.1.refs_0_, bf16[304,384]{1,0:T(8,128)(2,1)S(1)} %collective-permute-done.7.refs_1_, bf16[304,384]{1,0:T(8,128)(2,1)S(1)} %collective-permute-done.8.refs_2_, ...), custom_call_target="tpu_custom_call" | custom-call | flops 905969664 | bytes 1048576 | tf_op jit(solution)/shard_map/one_back/pallas_call | solution.py:337
  40.4 2.6 %fetch.5.refs_5_.refs_9_ = bf16[3,1536,384]{2,1,0:T(8,128)(2,1)S(1)} custom-call(s32[6]{0:T(128)S(1)} %stack.23.ids, bf16[3,3,1536,384]{3,2,1,0:T(8,128)(2,1)} %w_hbm.5), custom_call_target="tpu_custom_call" | custom-call | flops 1000000000 | bytes 1048576 | tf_op jit(solution)/shard_map/fetch/pallas_call | solution.py:263
  43.0 1.4 %collective-permute-done.11.refs_2_ = bf16[288,384]{1,0:T(8,128)(2,1)S(1)} collective-permute-done((bf16[288,384]{1,0:T(8,128)(2,1)S(1)}, bf16[288,384]{1,0:T(8,128)(2,1)S(1)}, u32[]{:S(2)}, u32[]{:S(2)}) %collective-permute-start.11) | collective-permute-done | bytes 221216 | tf_op jit(solution)/shard_map/ppermute | solution.py:295
  44.4 0.7 collective-permute-start.17
  45.3 0.6 collective-permute-done.15.refs_3_
  45.8 2.7 %two_front.1 = (bf16[256,384]{1,0:T(8,128)(2,1)S(1)}, f32[384,384]{1,0:T(8,128)S(1)}) custom-call(s32[6]{0:T(128)S(1)} %stack.23.ids, bf16[288,384]{1,0:T(8,128)(2,1)S(1)} %one_front.1.refs_0_, bf16[288,384]{1,0:T(8,128)(2,1)S(1)} %collective-permute-done.10.refs_1_, bf16[288,384]{1,0:T(8,128)(2,1)S(1)} %collective-permute-done.11.refs_2_, ...), custom_call_target="tpu_custom_call" | custom-call | flops 905969664 | bytes 1048576 | tf_op jit(solution)/shard_map/two_front/pallas_call | solution.py:350
  48.5 3.1 %collective-permute-done.17.refs_6_ = bf16[256,384]{1,0:T(8,128)(2,1)S(1)} collective-permute-done((bf16[256,384]{1,0:T(8,128)(2,1)S(1)}, bf16[256,384]{1,0:T(8,128)(2,1)S(1)}, u32[]{:S(2)}, u32[]{:S(2)}) %collective-permute-start.17) | collective-permute-done | bytes 196640 | tf_op jit(solution)/shard_map/ppermute | solution.py:295
  51.7 1.4 %collective-permute-done.18.refs_7_ = bf16[256,384]{1,0:T(8,128)(2,1)S(1)} collective-permute-done((bf16[256,384]{1,0:T(8,128)(2,1)S(1)}, bf16[256,384]{1,0:T(8,128)(2,1)S(1)}, u32[]{:S(2)}, u32[]{:S(2)}) %collective-permute-start.18) | collective-permute-done | bytes 196640 | tf_op jit(solution)/shard_map/ppermute | solution.py:300
  53.1 2.8 %two_back.1 = (bf16[256,384]{1,0:T(8,128)(2,1)S(1)}, f32[96,384]{1,0:T(8,128)S(1)}, bf16[96,384]{1,0:T(8,128)(2,1)S(1)}, bf16[96,384]{1,0:T(8,128)(2,1)S(1)}, bf16[96,384]{1,0:T(8,128)(2,1)S(1)}) custom-call(s32[6]{0:T(128)S(1)} %stack.23.ids, bf16[288,384]{1,0:T(8,128)(2,1)S(1)} %one_front.1.refs_0_, bf16[288,384]{1,0:T(8,128)(2,1)S(1)} %collective-permute-done.10.refs_1_, ...), custom_call_target="tpu_custom_call" | custom-call | flops 905969664 | bytes 1048576 | tf_op jit(solution)/shard_map/two_back/pallas_call | solution.py:359
  55.9 1.8 %collective-permute-start.19 = (bf16[96,384]{1,0:T(8,128)(2,1)S(1)}, bf16[96,384]{1,0:T(8,128)(2,1)S(1)}, u32[]{:S(2)}, u32[]{:S(2)}) collective-permute-start(bf16[96,384]{1,0:T(8,128)(2,1)S(1)} %get-tuple-element.31), channel_id=1, source_target_pairs={{0,32},{1,5},{2,34},{3,7},{4,36},{5,1},{6,38},{7,3},{8,40},{9,13},... | collective-permute-start | bytes 221192 | tf_op jit(solution)/shard_map/ppermute | solution.py:402
  57.7 3.9 %collective-permute-start.20 = (bf16[96,384]{1,0:T(8,128)(2,1)S(1)}, bf16[96,384]{1,0:T(8,128)(2,1)S(1)}, u32[]{:S(2)}, u32[]{:S(2)}) collective-permute-start(bf16[96,384]{1,0:T(8,128)(2,1)S(1)} %get-tuple-element.32), channel_id=1, source_target_pairs={{0,4},{1,33},{2,6},{3,35},{4,0},{5,37},{6,2},{7,39},{8,12},{9,41},... | collective-permute-start | bytes 221192 | tf_op jit(solution)/shard_map/ppermute | solution.py:402
  61.6 2.8 %collective-permute-done.20 = bf16[96,384]{1,0:T(8,128)(2,1)S(1)} collective-permute-done((bf16[96,384]{1,0:T(8,128)(2,1)S(1)}, bf16[96,384]{1,0:T(8,128)(2,1)S(1)}, u32[]{:S(2)}, u32[]{:S(2)}) %collective-permute-start.20) | collective-permute-done | bytes 73760 | tf_op jit(solution)/shard_map/ppermute | solution.py:402
  64.5 2.4 %collective-permute-done.21 = bf16[96,384]{1,0:T(8,128)(2,1)S(1)} collective-permute-done((bf16[96,384]{1,0:T(8,128)(2,1)S(1)}, bf16[96,384]{1,0:T(8,128)(2,1)S(1)}, u32[]{:S(2)}, u32[]{:S(2)}) %collective-permute-start.21) | collective-permute-done | bytes 73760 | tf_op jit(solution)/shard_map/ppermute | solution.py:402
  66.9 3.3 %collective-permute-start.24 = (bf16[96,384]{1,0:T(8,128)(2,1)S(1)}, bf16[96,384]{1,0:T(8,128)(2,1)S(1)}, u32[]{:S(2)}, u32[]{:S(2)}) collective-permute-start(bf16[96,384]{1,0:T(8,128)(2,1)S(1)} %add_convert_fusion.3), channel_id=1, source_target_pairs={{0,124},{1,125},{2,126},{3,127},{4,104},{5,105},{6,106},{7,107},{8... | collective-permute-start | bytes 221192 | tf_op jit(solution)/shard_map/ppermute | solution.py:402
  70.5 1.1 %collective-permute-start.22 = (bf16[96,384]{1,0:T(8,128)(2,1)S(1)}, bf16[96,384]{1,0:T(8,128)(2,1)S(1)}, u32[]{:S(2)}, u32[]{:S(2)}) collective-permute-start(bf16[96,384]{1,0:T(8,128)(2,1)S(1)} %add_convert_fusion.3), channel_id=1, source_target_pairs={{0,96},{1,29},{2,98},{3,31},{4,100},{5,9},{6,102},{7,11},{8,104},{... | collective-permute-start | bytes 221192 | tf_op jit(solution)/shard_map/ppermute | solution.py:402
  71.7 1.9 %collective-permute-done.24 = bf16[96,384]{1,0:T(8,128)(2,1)S(1)} collective-permute-done((bf16[96,384]{1,0:T(8,128)(2,1)S(1)}, bf16[96,384]{1,0:T(8,128)(2,1)S(1)}, u32[]{:S(2)}, u32[]{:S(2)}) %collective-permute-start.24) | collective-permute-done | bytes 73760 | tf_op jit(solution)/shard_map/ppermute | solution.py:402
  73.6 1.0 collective-permute-done.23
  74.6 1.5 %collective-permute-done.22 = bf16[96,384]{1,0:T(8,128)(2,1)S(1)} collective-permute-done((bf16[96,384]{1,0:T(8,128)(2,1)S(1)}, bf16[96,384]{1,0:T(8,128)(2,1)S(1)}, u32[]{:S(2)}, u32[]{:S(2)}) %collective-permute-start.22) | collective-permute-done | bytes 73760 | tf_op jit(solution)/shard_map/ppermute | solution.py:402
  76.2 0.9 collective-permute-start.25
  77.0 5.1 %collective-permute-done.25 = bf16[96,384]{1,0:T(8,128)(2,1)S(1)} collective-permute-done((bf16[96,384]{1,0:T(8,128)(2,1)S(1)}, bf16[96,384]{1,0:T(8,128)(2,1)S(1)}, u32[]{:S(2)}, u32[]{:S(2)}) %collective-permute-start.25) | collective-permute-done | bytes 73760 | tf_op jit(solution)/shard_map/ppermute | solution.py:402
  82.1 3.2 %collective-permute-start.26 = (bf16[96,384]{1,0:T(8,128)(2,1)S(1)}, bf16[96,384]{1,0:T(8,128)(2,1)S(1)}, u32[]{:S(2)}, u32[]{:S(2)}) collective-permute-start(bf16[96,384]{1,0:T(8,128)(2,1)S(1)} %add_convert_fusion.1), channel_id=1, source_target_pairs={{0,12},{1,129},{2,14},{3,131},{4,24},{5,133},{6,26},{7,135},{8,20}... | collective-permute-start | bytes 221192 | tf_op jit(solution)/shard_map/ppermute | solution.py:402
  85.3 4.7 %collective-permute-done.26 = bf16[96,384]{1,0:T(8,128)(2,1)S(1)} collective-permute-done((bf16[96,384]{1,0:T(8,128)(2,1)S(1)}, bf16[96,384]{1,0:T(8,128)(2,1)S(1)}, u32[]{:S(2)}, u32[]{:S(2)}) %collective-permute-start.26) | collective-permute-done | bytes 73760 | tf_op jit(solution)/shard_map/ppermute | solution.py:402
  90.2 1.0 collective-permute-start.28
  91.1 2.5 %collective-permute-start.27 = (bf16[96,384]{1,0:T(8,128)(2,1)S(1)}, bf16[96,384]{1,0:T(8,128)(2,1)S(1)}, u32[]{:S(2)}, u32[]{:S(2)}) collective-permute-start(bf16[96,384]{1,0:T(8,128)(2,1)S(1)} %add_convert_fusion.p0), channel_id=1, source_target_pairs={{0,32},{1,5},{2,34},{3,7},{4,36},{5,1},{6,38},{7,3},{8,40},{9,13},... | collective-permute-start | bytes 221192 | tf_op jit(solution)/shard_map/ppermute | solution.py:402
  93.6 1.1 %decode.1 = bf16[512,384]{1,0:T(8,128)(2,1)} custom-call(bf16[256,384]{1,0:T(8,128)(2,1)S(1)} %get-tuple-element.26.front_rows, bf16[256,384]{1,0:T(8,128)(2,1)S(1)} %get-tuple-element.29.back_rows, bf16[384,384]{1,0:T(8,128)(2,1)S(1)} %copy-done.2), custom_call_target="tpu_custom_call" | custom-call | flops 150994944 | bytes 1048576 | tf_op jit(solution)/shard_map/decode/pallas_call | solution.py:368
  94.8 0.6 collective-permute-done.29.p3
  95.4 0.8 collective-permute-done.27.p1
  96.2 1.4 %assemble.1 = f32[384,384]{1,0:T(8,128)} custom-call(s32[6]{0:T(128)S(1)} %stack.23.ids, bf16[96,384]{1,0:T(8,128)(2,1)S(1)} %add_convert_fusion.p0, bf16[96,384]{1,0:T(8,128)(2,1)S(1)} %collective-permute-done.27.p1, bf16[96,384]{1,0:T(8,128)(2,1)S(1)} %collective-permute-done.28.p2, bf16[96,384]{1,0:T(8,128)(2,1)S(1)} %collective-permute-done.29.p3), custom_call_target="tpu_custom_call" | custom-call | bytes 1048576 | tf_op jit(solution)/shard_map/assemble/pallas_call | solution.py:422
  (39 shorter events, 2.6 us)
Async XLA Ops:
  0.6 17.2 %collective-permute-start.1 = (bf16[512,384]{1,0:T(8,128)(2,1)}, bf16[512,384]{1,0:T(8,128)(2,1)S(1)}, u32[]{:S(2)}, u32[]{:S(2)}) collective-permute-start(bf16[512,384]{1,0:T(8,128)(2,1)} %param.7), channel_id=1, source_target_pairs={{0,1},{1,0},{2,3},{3,2},{4,5},{5,4},{6,7},{7,6},{8,9},{9,8},{10,11... | collective-permute-start | bytes 1179656 | tf_op jit(solution)/shard_map/ppermute | solution.py:260
  1.8 14.5 %collective-permute-start.2 = (bf16[256,384]{1,0:T(8,128)(2,1)S(1)}, bf16[256,384]{1,0:T(8,128)(2,1)S(1)}, u32[]{:S(2)}, u32[]{:S(2)}) collective-permute-start(bf16[256,384]{1,0:T(8,128)(2,1)S(1)} %get-tuple-element.18.own_a), channel_id=1, source_target_pairs={{0,2},{1,3},{2,0},{3,1},{4,6},{5,7},{6,4},{7,5},{8,10},{9,11},{10,... | collective-permute-start | bytes 589832 | tf_op jit(solution)/shard_map/ppermute | solution.py:258
  3.5 12.8 %collective-permute-start.4 = (bf16[256,384]{1,0:T(8,128)(2,1)S(1)}, bf16[256,384]{1,0:T(8,128)(2,1)S(1)}, u32[]{:S(2)}, u32[]{:S(2)}) collective-permute-start(bf16[256,384]{1,0:T(8,128)(2,1)S(1)} %get-tuple-element.19.own_b), channel_id=1, source_target_pairs={{0,130},{1,131},{2,128},{3,129},{128,2},{129,3},{130,0},{131,1},{4... | collective-permute-start | bytes 589832 | tf_op jit(solution)/shard_map/ppermute | solution.py:259
  6.4 9.9 %collective-permute-start = (s32[16,128]{1,0:T(8,128)S(1)}, s32[16,128]{1,0:T(8,128)S(1)}, u32[]{:S(2)}, u32[]{:S(2)}) collective-permute-start(s32[16,128]{1,0:T(8,128)S(1)} %bitcast.15), channel_id=1, source_target_pairs={{0,4},{4,8},{8,12},{12,16},{16,20},{20,24},{24,28},{28,32},{32,36}... | collective-permute-start | bytes 24584 | tf_op jit(solution)/shard_map/ppermute | solution.py:261
  10.2 6.1 %collective-permute-start.3 = (s32[16,128]{1,0:T(8,128)S(1)}, s32[16,128]{1,0:T(8,128)S(1)}, u32[]{:S(2)}, u32[]{:S(2)}) collective-permute-start(s32[16,128]{1,0:T(8,128)S(1)} %bitcast.14), channel_id=1, source_target_pairs={{4,0},{8,4},{12,8},{16,12},{20,16},{24,20},{28,24},{32,28},{36,32}... | collective-permute-start | bytes 24584 | tf_op jit(solution)/shard_map/ppermute | solution.py:279
  12.4 1.0 copy-start.3
  13.6 4.5 %copy-start.1 = (f32[3,1536]{1,0:T(4,128)S(1)}, f32[3,1536]{1,0:T(4,128)}, u32[]{:S(2)}) copy-start(f32[3,1536]{1,0:T(4,128)} %refs_8_.3) | copy-start | bytes 55300
  16.3 1.5 %collective-permute-start.6 = (bf16[256,384]{1,0:T(8,128)(2,1)S(1)}, bf16[256,384]{1,0:T(8,128)(2,1)S(1)}, u32[]{:S(2)}, u32[]{:S(2)}) collective-permute-start(bf16[256,384]{1,0:T(8,128)(2,1)S(1)} %collective-permute-done.4.w2b), channel_id=1, source_target_pairs={{0,1},{1,0},{2,3},{3,2},{4,5},{5,4},{6,7},{7,6},{8,9},{9,8},{10,11... | collective-permute-start | bytes 589832 | tf_op jit(solution)/shard_map/ppermute | solution.py:283
  16.4 1.7 %collective-permute-start.5 = (bf16[256,384]{1,0:T(8,128)(2,1)S(1)}, bf16[256,384]{1,0:T(8,128)(2,1)S(1)}, u32[]{:S(2)}, u32[]{:S(2)}) collective-permute-start(bf16[256,384]{1,0:T(8,128)(2,1)S(1)} %collective-permute-done.2.w2a), channel_id=1, source_target_pairs={{0,1},{1,0},{2,3},{3,2},{4,5},{5,4},{6,7},{7,6},{8,9},{9,8},{10,11... | collective-permute-start | bytes 589832 | tf_op jit(solution)/shard_map/ppermute | solution.py:282
  21.5 7.9 %collective-permute-start.8 = (bf16[304,384]{1,0:T(8,128)(2,1)S(1)}, bf16[304,384]{1,0:T(8,128)(2,1)S(1)}, u32[]{:S(2)}, u32[]{:S(2)}) collective-permute-start(bf16[304,384]{1,0:T(8,128)(2,1)S(1)} %zero_front.1.refs_0_), channel_id=1, source_target_pairs={{0,2},{1,3},{2,0},{3,1},{4,6},{5,7},{6,4},{7,5},{8,10},{9,11},{10,... | collective-permute-start | bytes 700424 | tf_op jit(solution)/shard_map/ppermute | solution.py:295
  22.3 8.1 %collective-permute-start.7 = (bf16[304,384]{1,0:T(8,128)(2,1)S(1)}, bf16[304,384]{1,0:T(8,128)(2,1)S(1)}, u32[]{:S(2)}, u32[]{:S(2)}) collective-permute-start(bf16[304,384]{1,0:T(8,128)(2,1)S(1)} %zero_front.1.refs_0_), channel_id=1, source_target_pairs={{0,1},{1,0},{2,3},{3,2},{4,5},{5,4},{6,7},{7,6},{8,9},{9,8},{10,11... | collective-permute-start | bytes 700424 | tf_op jit(solution)/shard_map/ppermute | solution.py:295
  29.4 1.5 %collective-permute-start.9 = (bf16[304,384]{1,0:T(8,128)(2,1)S(1)}, bf16[304,384]{1,0:T(8,128)(2,1)S(1)}, u32[]{:S(2)}, u32[]{:S(2)}) collective-permute-start(bf16[304,384]{1,0:T(8,128)(2,1)S(1)} %collective-permute-done.8.refs_2_), channel_id=1, source_target_pairs={{0,1},{1,0},{2,3},{3,2},{4,5},{5,4},{6,7},{7,6},{8,9},{9,8},{10,11... | collective-permute-start | bytes 700424 | tf_op jit(solution)/shard_map/ppermute | solution.py:300
  29.5 7.1 %collective-permute-start.13 = (bf16[240,384]{1,0:T(8,128)(2,1)S(1)}, bf16[240,384]{1,0:T(8,128)(2,1)S(1)}, u32[]{:S(2)}, u32[]{:S(2)}) collective-permute-start(bf16[240,384]{1,0:T(8,128)(2,1)S(1)} %zero_back.1.refs_4_), channel_id=1, source_target_pairs={{0,2},{1,3},{2,0},{3,1},{4,6},{5,7},{6,4},{7,5},{8,10},{9,11},{10,... | collective-permute-start | bytes 552968 | tf_op jit(solution)/shard_map/ppermute | solution.py:295
  30.1 7.3 %collective-permute-start.12 = (bf16[240,384]{1,0:T(8,128)(2,1)S(1)}, bf16[240,384]{1,0:T(8,128)(2,1)S(1)}, u32[]{:S(2)}, u32[]{:S(2)}) collective-permute-start(bf16[240,384]{1,0:T(8,128)(2,1)S(1)} %zero_back.1.refs_4_), channel_id=1, source_target_pairs={{0,1},{1,0},{2,3},{3,2},{4,5},{5,4},{6,7},{7,6},{8,9},{9,8},{10,11... | collective-permute-start | bytes 552968 | tf_op jit(solution)/shard_map/ppermute | solution.py:295
  36.5 1.4 %collective-permute-start.14 = (bf16[240,384]{1,0:T(8,128)(2,1)S(1)}, bf16[240,384]{1,0:T(8,128)(2,1)S(1)}, u32[]{:S(2)}, u32[]{:S(2)}) collective-permute-start(bf16[240,384]{1,0:T(8,128)(2,1)S(1)} %collective-permute-done.13.refs_6_), channel_id=1, source_target_pairs={{0,1},{1,0},{2,3},{3,2},{4,5},{5,4},{6,7},{7,6},{8,9},{9,8},{10,11... | collective-permute-start | bytes 552968 | tf_op jit(solution)/shard_map/ppermute | solution.py:300
  36.5 7.8 %collective-permute-start.11 = (bf16[288,384]{1,0:T(8,128)(2,1)S(1)}, bf16[288,384]{1,0:T(8,128)(2,1)S(1)}, u32[]{:S(2)}, u32[]{:S(2)}) collective-permute-start(bf16[288,384]{1,0:T(8,128)(2,1)S(1)} %one_front.1.refs_0_), channel_id=1, source_target_pairs={{0,2},{1,3},{2,0},{3,1},{4,6},{5,7},{6,4},{7,5},{8,10},{9,11},{10,... | collective-permute-start | bytes 663560 | tf_op jit(solution)/shard_map/ppermute | solution.py:295
  37.2 8.1 %collective-permute-start.10 = (bf16[288,384]{1,0:T(8,128)(2,1)S(1)}, bf16[288,384]{1,0:T(8,128)(2,1)S(1)}, u32[]{:S(2)}, u32[]{:S(2)}) collective-permute-start(bf16[288,384]{1,0:T(8,128)(2,1)S(1)} %one_front.1.refs_0_), channel_id=1, source_target_pairs={{0,1},{1,0},{2,3},{3,2},{4,5},{5,4},{6,7},{7,6},{8,9},{9,8},{10,11... | collective-permute-start | bytes 663560 | tf_op jit(solution)/shard_map/ppermute | solution.py:295
  40.4 5.5 %copy-start = (bf16[1,512,384]{2,1,0:T(8,128)(2,1)S(1)}, bf16[1,512,384]{2,1,0:T(8,128)(2,1)}, u32[]{:S(2)}) copy-start(bf16[1,512,384]{2,1,0:T(8,128)(2,1)} %param.11) | copy-start | bytes 1179652
  44.3 1.5 %collective-permute-start.15 = (bf16[288,384]{1,0:T(8,128)(2,1)S(1)}, bf16[288,384]{1,0:T(8,128)(2,1)S(1)}, u32[]{:S(2)}, u32[]{:S(2)}) collective-permute-start(bf16[288,384]{1,0:T(8,128)(2,1)S(1)} %collective-permute-done.11.refs_2_), channel_id=1, source_target_pairs={{0,1},{1,0},{2,3},{3,2},{4,5},{5,4},{6,7},{7,6},{8,9},{9,8},{10,11... | collective-permute-start | bytes 663560 | tf_op jit(solution)/shard_map/ppermute | solution.py:300
  44.4 7.3 %collective-permute-start.17 = (bf16[256,384]{1,0:T(8,128)(2,1)S(1)}, bf16[256,384]{1,0:T(8,128)(2,1)S(1)}, u32[]{:S(2)}, u32[]{:S(2)}) collective-permute-start(bf16[256,384]{1,0:T(8,128)(2,1)S(1)} %one_back.1.refs_4_), channel_id=1, source_target_pairs={{0,2},{1,3},{2,0},{3,1},{4,6},{5,7},{6,4},{7,5},{8,10},{9,11},{10,... | collective-permute-start | bytes 589832 | tf_op jit(solution)/shard_map/ppermute | solution.py:295
  45.0 6.6 %collective-permute-start.16 = (bf16[256,384]{1,0:T(8,128)(2,1)S(1)}, bf16[256,384]{1,0:T(8,128)(2,1)S(1)}, u32[]{:S(2)}, u32[]{:S(2)}) collective-permute-start(bf16[256,384]{1,0:T(8,128)(2,1)S(1)} %one_back.1.refs_4_), channel_id=1, source_target_pairs={{0,1},{1,0},{2,3},{3,2},{4,5},{5,4},{6,7},{7,6},{8,9},{9,8},{10,11... | collective-permute-start | bytes 589832 | tf_op jit(solution)/shard_map/ppermute | solution.py:295
  51.7 1.4 %collective-permute-start.18 = (bf16[256,384]{1,0:T(8,128)(2,1)S(1)}, bf16[256,384]{1,0:T(8,128)(2,1)S(1)}, u32[]{:S(2)}, u32[]{:S(2)}) collective-permute-start(bf16[256,384]{1,0:T(8,128)(2,1)S(1)} %collective-permute-done.17.refs_6_), channel_id=1, source_target_pairs={{0,1},{1,0},{2,3},{3,2},{4,5},{5,4},{6,7},{7,6},{8,9},{9,8},{10,11... | collective-permute-start | bytes 589832 | tf_op jit(solution)/shard_map/ppermute | solution.py:300
  53.1 40.5 %copy-start.2 = (bf16[384,384]{1,0:T(8,128)(2,1)S(1)}, bf16[384,384]{1,0:T(8,128)(2,1)}, u32[]{:S(2)}) copy-start(bf16[384,384]{1,0:T(8,128)(2,1)} %weights.1) | copy-start | bytes 884740
  55.9 5.7 %collective-permute-start.19 = (bf16[96,384]{1,0:T(8,128)(2,1)S(1)}, bf16[96,384]{1,0:T(8,128)(2,1)S(1)}, u32[]{:S(2)}, u32[]{:S(2)}) collective-permute-start(bf16[96,384]{1,0:T(8,128)(2,1)S(1)} %get-tuple-element.31), channel_id=1, source_target_pairs={{0,32},{1,5},{2,34},{3,7},{4,36},{5,1},{6,38},{7,3},{8,40},{9,13},... | collective-permute-start | bytes 221192 | tf_op jit(solution)/shard_map/ppermute | solution.py:402
  57.7 6.8 %collective-permute-start.20 = (bf16[96,384]{1,0:T(8,128)(2,1)S(1)}, bf16[96,384]{1,0:T(8,128)(2,1)S(1)}, u32[]{:S(2)}, u32[]{:S(2)}) collective-permute-start(bf16[96,384]{1,0:T(8,128)(2,1)S(1)} %get-tuple-element.32), channel_id=1, source_target_pairs={{0,4},{1,33},{2,6},{3,35},{4,0},{5,37},{6,2},{7,39},{8,12},{9,41},... | collective-permute-start | bytes 221192 | tf_op jit(solution)/shard_map/ppermute | solution.py:402
  61.6 5.3 %collective-permute-start.21 = (bf16[96,384]{1,0:T(8,128)(2,1)S(1)}, bf16[96,384]{1,0:T(8,128)(2,1)S(1)}, u32[]{:S(2)}, u32[]{:S(2)}) collective-permute-start(bf16[96,384]{1,0:T(8,128)(2,1)S(1)} %get-tuple-element.33), channel_id=1, source_target_pairs={{0,36},{1,37},{2,38},{3,39},{4,32},{5,33},{6,34},{7,35},{8,44},{9,... | collective-permute-start | bytes 221192 | tf_op jit(solution)/shard_map/ppermute | solution.py:402
  66.9 6.7 %collective-permute-start.24 = (bf16[96,384]{1,0:T(8,128)(2,1)S(1)}, bf16[96,384]{1,0:T(8,128)(2,1)S(1)}, u32[]{:S(2)}, u32[]{:S(2)}) collective-permute-start(bf16[96,384]{1,0:T(8,128)(2,1)S(1)} %add_convert_fusion.3), channel_id=1, source_target_pairs={{0,124},{1,125},{2,126},{3,127},{4,104},{5,105},{6,106},{7,107},{8... | collective-permute-start | bytes 221192 | tf_op jit(solution)/shard_map/ppermute | solution.py:402
  70.2 4.4 %collective-permute-start.23 = (bf16[96,384]{1,0:T(8,128)(2,1)S(1)}, bf16[96,384]{1,0:T(8,128)(2,1)S(1)}, u32[]{:S(2)}, u32[]{:S(2)}) collective-permute-start(bf16[96,384]{1,0:T(8,128)(2,1)S(1)} %add_convert_fusion.3), channel_id=1, source_target_pairs={{0,28},{1,97},{2,30},{3,99},{4,8},{5,101},{6,10},{7,103},{8,4},{9,... | collective-permute-start | bytes 221192 | tf_op jit(solution)/shard_map/ppermute | solution.py:402
  70.5 5.6 %collective-permute-start.22 = (bf16[96,384]{1,0:T(8,128)(2,1)S(1)}, bf16[96,384]{1,0:T(8,128)(2,1)S(1)}, u32[]{:S(2)}, u32[]{:S(2)}) collective-permute-start(bf16[96,384]{1,0:T(8,128)(2,1)S(1)} %add_convert_fusion.3), channel_id=1, source_target_pairs={{0,96},{1,29},{2,98},{3,31},{4,100},{5,9},{6,102},{7,11},{8,104},{... | collective-permute-start | bytes 221192 | tf_op jit(solution)/shard_map/ppermute | solution.py:402
  76.2 5.9 %collective-permute-start.25 = (bf16[96,384]{1,0:T(8,128)(2,1)S(1)}, bf16[96,384]{1,0:T(8,128)(2,1)S(1)}, u32[]{:S(2)}, u32[]{:S(2)}) collective-permute-start(bf16[96,384]{1,0:T(8,128)(2,1)S(1)} %add_convert_fusion.2), channel_id=1, source_target_pairs={{0,128},{1,13},{2,130},{3,15},{4,132},{5,25},{6,134},{7,27},{8,136... | collective-permute-start | bytes 221192 | tf_op jit(solution)/shard_map/ppermute | solution.py:402
  82.1 7.9 %collective-permute-start.26 = (bf16[96,384]{1,0:T(8,128)(2,1)S(1)}, bf16[96,384]{1,0:T(8,128)(2,1)S(1)}, u32[]{:S(2)}, u32[]{:S(2)}) collective-permute-start(bf16[96,384]{1,0:T(8,128)(2,1)S(1)} %add_convert_fusion.1), channel_id=1, source_target_pairs={{0,12},{1,129},{2,14},{3,131},{4,24},{5,133},{6,26},{7,135},{8,20}... | collective-permute-start | bytes 221192 | tf_op jit(solution)/shard_map/ppermute | solution.py:402
  90.1 5.4 %collective-permute-start.29 = (bf16[96,384]{1,0:T(8,128)(2,1)S(1)}, bf16[96,384]{1,0:T(8,128)(2,1)S(1)}, u32[]{:S(2)}, u32[]{:S(2)}) collective-permute-start(bf16[96,384]{1,0:T(8,128)(2,1)S(1)} %add_convert_fusion.p0), channel_id=1, source_target_pairs={{0,36},{1,37},{2,38},{3,39},{4,32},{5,33},{6,34},{7,35},{8,44},{9,... | collective-permute-start | bytes 221192 | tf_op jit(solution)/shard_map/ppermute | solution.py:402
  90.2 5.3 %collective-permute-start.28 = (bf16[96,384]{1,0:T(8,128)(2,1)S(1)}, bf16[96,384]{1,0:T(8,128)(2,1)S(1)}, u32[]{:S(2)}, u32[]{:S(2)}) collective-permute-start(bf16[96,384]{1,0:T(8,128)(2,1)S(1)} %add_convert_fusion.p0), channel_id=1, source_target_pairs={{0,4},{1,33},{2,6},{3,35},{4,0},{5,37},{6,2},{7,39},{8,12},{9,41},... | collective-permute-start | bytes 221192 | tf_op jit(solution)/shard_map/ppermute | solution.py:402
  91.1 5.1 %collective-permute-start.27 = (bf16[96,384]{1,0:T(8,128)(2,1)S(1)}, bf16[96,384]{1,0:T(8,128)(2,1)S(1)}, u32[]{:S(2)}, u32[]{:S(2)}) collective-permute-start(bf16[96,384]{1,0:T(8,128)(2,1)S(1)} %add_convert_fusion.p0), channel_id=1, source_target_pairs={{0,32},{1,5},{2,34},{3,7},{4,36},{5,1},{6,38},{7,3},{8,40},{9,13},... | collective-permute-start | bytes 221192 | tf_op jit(solution)/shard_map/ppermute | solution.py:402

commit v6 on v5

--- a/solution.py
+++ b/solution.py
@@ -227,7 +227,7 @@
         out_specs=(VMEM,) * len(outs) if many else VMEM,
         scratch_shapes=list(scratch),
         compiler_params=pltpu.CompilerParams(vmem_limit_bytes=megabytes * 2**20),
-        cost_estimate=pl.CostEstimate(flops=flops, bytes_accessed=2**20, transcendentals=0),
+        cost_estimate=pl.CostEstimate(flops=flops // 1000 if name != 'fetch' else flops, bytes_accessed=1024, transcendentals=0),
         name=name,
     )
 
@@ -299,7 +299,7 @@
         remote = tie(remote, *done)
         return own, beside, remote, other_core(remote)
 
-    cut = bins // 2 + 3 * HALO
+    cut = bins // 2 + (0) * HALO
     inputs = (stem_a, stem_b, w1, w2a, w2b, w3a, w3b, gains, weights)
     part = call(
         "zero_front",

time: 98.9 us -> 92.4 us (0.934)
  waiting for transfers between devices: 34.2 us -> 25.6 us
  starting transfers between devices: 32 us -> 35.7 us
    ppermute x8, waiting for transfers between devices: 9.05 us -> 0.15 us  [exchange(): return (own, other_core(own), across(own))]
    ppermute x8, starting transfers between devices: 3.48 us -> 5.59 us  [exchange(): return (own, other_core(own), across(own))]
  transfers between devices with their start and end apart: 30 -> 30, of which waited for: 19 -> 16; matrix products, arithmetic and copies ran while one was open for 2% -> 2% of each run, Pallas kernels for 20% -> 22%
where the time goes in v6:
time: 92.4 us; the launch traced here: 91.8 us
  starting transfers between devices  35.7 us (39%)
  Pallas kernels  27.6 us (30%)
  waiting for transfers between devices  25.6 us (28%)
  local copies, waits for them, and re-layouts  1.88 us (2%)
  between operations  0.94 us (1%)
    ppermute x11, waiting for transfers between devices, swap(): return lax.ppermute(own, ('section', 'seq', 'chan'), perm)  20.6 us
    ppermute x11, starting transfers between devices, swap(): return lax.ppermute(own, ('section', 'seq', 'chan'), perm)  19 us
    pallas_call x3, Pallas kernels, fetched(): call('fetch', functools.partial(fetch, layer), jax.ShapeDtypeStruct(conv_...  7.77 us
    ppermute x8, starting transfers between devices, exchange(): return (own, other_core(own), across(own))  5.59 us
    ppermute x1, starting transfers between devices, body(): before = lax.ppermute(letters[bins - HALO:], 'seq', up)  3.81 us
    pallas_call x1, Pallas kernels, body(): call('zero_back', functools.partial(first_layer, (cut, rows), bins, count...  3.28 us
    ppermute x4, waiting for transfers between devices, finish(): return (own, beside, remote, other_core(remote))  3.2 us
    pallas_call x1, Pallas kernels, body(): call('two_back', functools.partial(last_back, (cut, rows - HALO), bins),...  3.14 us
  transfers between devices with their start and end apart: 30, of which 16 were waited for; matrix products, arithmetic and copies ran while one was open for 2% of the time, Pallas kernels for 22%

profile of v6, /device:TPU:32, one launch (start us, length us, event | category | flops | bytes accessed | tf_op | source)
XLA Modules:
  0.0 91.8 jit_solution(14141787971288873305)
XLA Ops:
  0.7 1.1 %fusion = (bf16[256,384]{1,0:T(8,128)(2,1)S(1)}, bf16[256,384]{1,0:T(8,128)(2,1)S(1)}) fusion(bf16[512,384]{1,0:T(8,128)(2,1)} %param.7), kind=kLoop, calls=%fused_computation.4 | loop fusion | bytes 786432 | tf_op jit(solution)/shard_map/slice | solution.py:257
  1.8 1.7 %collective-permute-start.2 = (bf16[256,384]{1,0:T(8,128)(2,1)S(1)}, bf16[256,384]{1,0:T(8,128)(2,1)S(1)}, u32[]{:S(2)}, u32[]{:S(2)}) collective-permute-start(bf16[256,384]{1,0:T(8,128)(2,1)S(1)} %get-tuple-element.18.own_a), channel_id=1, source_target_pairs={{0,2},{1,3},{2,0},{3,1},{4,6},{5,7},{6,4},{7,5},{8,10},{9,11},{10,... | collective-permute-start | bytes 589832 | tf_op jit(solution)/shard_map/ppermute | solution.py:258
  3.5 2.2 %collective-permute-start.4 = (bf16[256,384]{1,0:T(8,128)(2,1)S(1)}, bf16[256,384]{1,0:T(8,128)(2,1)S(1)}, u32[]{:S(2)}, u32[]{:S(2)}) collective-permute-start(bf16[256,384]{1,0:T(8,128)(2,1)S(1)} %get-tuple-element.19.own_b), channel_id=1, source_target_pairs={{0,130},{1,131},{2,128},{3,129},{128,2},{129,3},{130,0},{131,1},{4... | collective-permute-start | bytes 589832 | tf_op jit(solution)/shard_map/ppermute | solution.py:259
  5.6 0.7 fusion.1
  6.4 3.8 %collective-permute-start = (s32[16,128]{1,0:T(8,128)S(1)}, s32[16,128]{1,0:T(8,128)S(1)}, u32[]{:S(2)}, u32[]{:S(2)}) collective-permute-start(s32[16,128]{1,0:T(8,128)S(1)} %bitcast.15), channel_id=1, source_target_pairs={{0,4},{4,8},{8,12},{12,16},{16,20},{20,24},{24,28},{28,32},{32,36}... | collective-permute-start | bytes 24584 | tf_op jit(solution)/shard_map/ppermute | solution.py:261
  10.2 2.0 %collective-permute-start.3 = (s32[16,128]{1,0:T(8,128)S(1)}, s32[16,128]{1,0:T(8,128)S(1)}, u32[]{:S(2)}, u32[]{:S(2)}) collective-permute-start(s32[16,128]{1,0:T(8,128)S(1)} %bitcast.14), channel_id=1, source_target_pairs={{4,0},{8,4},{12,8},{16,12},{20,16},{24,20},{28,24},{32,28},{36,32}... | collective-permute-start | bytes 24584 | tf_op jit(solution)/shard_map/ppermute | solution.py:279
  12.4 2.6 %fetch.3.weights = bf16[3,1536,384]{2,1,0:T(8,128)(2,1)S(1)} custom-call(s32[6]{0:T(128)S(1)} %stack.23.ids, bf16[3,3,1536,384]{3,2,1,0:T(8,128)(2,1)} %w_hbm.5), custom_call_target="tpu_custom_call" | custom-call | flops 1000000000 | bytes 1024 | tf_op jit(solution)/shard_map/fetch/pallas_call | solution.py:263
  15.0 0.3 prepare.1.onehot
  15.3 0.4 collective-permute-done.3.halo
  15.7 0.5 collective-permute-start.5
  16.2 0.9 %collective-permute-done.6.w3b = bf16[256,384]{1,0:T(8,128)(2,1)S(1)} collective-permute-done((bf16[256,384]{1,0:T(8,128)(2,1)S(1)}, bf16[256,384]{1,0:T(8,128)(2,1)S(1)}, u32[]{:S(2)}, u32[]{:S(2)}) %collective-permute-start.6) | collective-permute-done | bytes 196640 | tf_op jit(solution)/shard_map/ppermute | solution.py:283
  17.5 3.1 %zero_front.1.refs_0_ = bf16[256,384]{1,0:T(8,128)(2,1)S(1)} custom-call(s32[6]{0:T(128)S(1)} %stack.23.ids, bf16[512,512]{1,0:T(8,128)(2,1)S(1)} %prepare.1.onehot, s32[16,128]{1,0:T(8,128)S(1)} %collective-permute-done.halo, bf16[256,384]{1,0:T(8,128)(2,1)S(1)} %get-tuple-element.18.own_a, bf16[256,384]{1,0:T(8,128)(2,1)S(1)} %get-tuple-element.19.own_b, ...), custom_call_target="tpu_custom_call" | custom-call | flops 905969 | bytes 1024 | tf_op jit(solution)/shard_map/zero_front/pallas_call | solution.py:304
  20.6 0.8 collective-permute-start.8
  21.3 3.3 %zero_back.1.refs_4_ = bf16[288,384]{1,0:T(8,128)(2,1)S(1)} custom-call(s32[6]{0:T(128)S(1)} %stack.23.ids, bf16[512,512]{1,0:T(8,128)(2,1)S(1)} %prepare.1.onehot, s32[16,128]{1,0:T(8,128)S(1)} %collective-permute-done.3.halo, bf16[256,384]{1,0:T(8,128)(2,1)S(1)} %get-tuple-element.18.own_a, bf16[256,384]{1,0:T(8,128)(2,1)S(1)} %get-tuple-element.19.own_b, ...), custom_call_target="tpu_custom_call" | custom-call | flops 1019215 | bytes 1024 | tf_op jit(solution)/shard_map/zero_back/pallas_call | solution.py:313
  24.6 1.4 %collective-permute-start.13 = (bf16[288,384]{1,0:T(8,128)(2,1)S(1)}, bf16[288,384]{1,0:T(8,128)(2,1)S(1)}, u32[]{:S(2)}, u32[]{:S(2)}) collective-permute-start(bf16[288,384]{1,0:T(8,128)(2,1)S(1)} %zero_back.1.refs_4_), channel_id=1, source_target_pairs={{0,2},{1,3},{2,0},{3,1},{4,6},{5,7},{6,4},{7,5},{8,10},{9,11},{10,... | collective-permute-start | bytes 663560 | tf_op jit(solution)/shard_map/ppermute | solution.py:295
  26.1 2.6 %fetch.4.refs_5_.refs_9_ = bf16[3,1536,384]{2,1,0:T(8,128)(2,1)S(1)} custom-call(s32[6]{0:T(128)S(1)} %stack.23.ids, bf16[3,3,1536,384]{3,2,1,0:T(8,128)(2,1)} %w_hbm.5), custom_call_target="tpu_custom_call" | custom-call | flops 1000000000 | bytes 1024 | tf_op jit(solution)/shard_map/fetch/pallas_call | solution.py:263
  28.7 0.3 collective-permute-start.9
  29.0 0.3 collective-permute-start.12
  29.3 0.9 %collective-permute-done.9.refs_3_ = bf16[256,384]{1,0:T(8,128)(2,1)S(1)} collective-permute-done((bf16[256,384]{1,0:T(8,128)(2,1)S(1)}, bf16[256,384]{1,0:T(8,128)(2,1)S(1)}, u32[]{:S(2)}, u32[]{:S(2)}) %collective-permute-start.9) | collective-permute-done | bytes 196640 | tf_op jit(solution)/shard_map/ppermute | solution.py:300
  30.2 2.3 %one_front.1.refs_0_ = bf16[240,384]{1,0:T(8,128)(2,1)S(1)} custom-call(s32[6]{0:T(128)S(1)} %stack.23.ids, bf16[256,384]{1,0:T(8,128)(2,1)S(1)} %zero_front.1.refs_0_, bf16[256,384]{1,0:T(8,128)(2,1)S(1)} %collective-permute-done.7.refs_1_, bf16[256,384]{1,0:T(8,128)(2,1)S(1)} %collective-permute-done.8.refs_2_, ...), custom_call_target="tpu_custom_call" | custom-call | flops 849346 | bytes 1024 | tf_op jit(solution)/shard_map/one_front/pallas_call | solution.py:327
  32.5 0.3 collective-permute-start.14
  32.8 1.1 %collective-permute-start.11 = (bf16[240,384]{1,0:T(8,128)(2,1)S(1)}, bf16[240,384]{1,0:T(8,128)(2,1)S(1)}, u32[]{:S(2)}, u32[]{:S(2)}) collective-permute-start(bf16[240,384]{1,0:T(8,128)(2,1)S(1)} %one_front.1.refs_0_), channel_id=1, source_target_pairs={{0,2},{1,3},{2,0},{3,1},{4,6},{5,7},{6,4},{7,5},{8,10},{9,11},{10,... | collective-permute-start | bytes 552968 | tf_op jit(solution)/shard_map/ppermute | solution.py:295
  34.1 2.7 %one_back.1.refs_4_ = bf16[304,384]{1,0:T(8,128)(2,1)S(1)} custom-call(s32[6]{0:T(128)S(1)} %stack.23.ids, bf16[256,384]{1,0:T(8,128)(2,1)S(1)} %zero_front.1.refs_0_, bf16[256,384]{1,0:T(8,128)(2,1)S(1)} %collective-permute-done.7.refs_1_, bf16[256,384]{1,0:T(8,128)(2,1)S(1)} %collective-permute-done.8.refs_2_, ...), custom_call_target="tpu_custom_call" | custom-call | flops 1075838 | bytes 1024 | tf_op jit(solution)/shard_map/one_back/pallas_call | solution.py:337
  36.9 1.3 %collective-permute-start.17 = (bf16[304,384]{1,0:T(8,128)(2,1)S(1)}, bf16[304,384]{1,0:T(8,128)(2,1)S(1)}, u32[]{:S(2)}, u32[]{:S(2)}) collective-permute-start(bf16[304,384]{1,0:T(8,128)(2,1)S(1)} %one_back.1.refs_4_), channel_id=1, source_target_pairs={{0,2},{1,3},{2,0},{3,1},{4,6},{5,7},{6,4},{7,5},{8,10},{9,11},{10,... | collective-permute-start | bytes 700424 | tf_op jit(solution)/shard_map/ppermute | solution.py:295
  38.2 2.6 %fetch.5.refs_5_.refs_9_ = bf16[3,1536,384]{2,1,0:T(8,128)(2,1)S(1)} custom-call(s32[6]{0:T(128)S(1)} %stack.23.ids, bf16[3,3,1536,384]{3,2,1,0:T(8,128)(2,1)} %w_hbm.5), custom_call_target="tpu_custom_call" | custom-call | flops 1000000000 | bytes 1024 | tf_op jit(solution)/shard_map/fetch/pallas_call | solution.py:263
  40.9 0.5 collective-permute-start.16
  41.4 0.9 collective-permute-done.15.refs_3_
  42.3 2.4 %two_front.1 = (bf16[208,384]{1,0:T(8,128)(2,1)S(1)}, f32[384,384]{1,0:T(8,128)S(1)}) custom-call(s32[6]{0:T(128)S(1)} %stack.23.ids, bf16[240,384]{1,0:T(8,128)(2,1)S(1)} %one_front.1.refs_0_, bf16[240,384]{1,0:T(8,128)(2,1)S(1)} %collective-permute-done.10.refs_1_, bf16[240,384]{1,0:T(8,128)(2,1)S(1)} %collective-permute-done.11.refs_2_, ...), custom_call_target="tpu_custom_call" | custom-call | flops 736100 | bytes 1024 | tf_op jit(solution)/shard_map/two_front/pallas_call | solution.py:350
  45.0 1.4 %collective-permute-done.18.refs_7_ = bf16[304,384]{1,0:T(8,128)(2,1)S(1)} collective-permute-done((bf16[304,384]{1,0:T(8,128)(2,1)S(1)}, bf16[304,384]{1,0:T(8,128)(2,1)S(1)}, u32[]{:S(2)}, u32[]{:S(2)}) %collective-permute-start.18) | collective-permute-done | bytes 233504 | tf_op jit(solution)/shard_map/ppermute | solution.py:300
  46.3 3.1 %two_back.1 = (bf16[304,384]{1,0:T(8,128)(2,1)S(1)}, f32[96,384]{1,0:T(8,128)S(1)}, bf16[96,384]{1,0:T(8,128)(2,1)S(1)}, bf16[96,384]{1,0:T(8,128)(2,1)S(1)}, bf16[96,384]{1,0:T(8,128)(2,1)S(1)}) custom-call(s32[6]{0:T(128)S(1)} %stack.23.ids, bf16[240,384]{1,0:T(8,128)(2,1)S(1)} %one_front.1.refs_0_, bf16[240,384]{1,0:T(8,128)(2,1)S(1)} %collective-permute-done.10.refs_1_, ...), custom_call_target="tpu_custom_call" | custom-call | flops 1075838 | bytes 1024 | tf_op jit(solution)/shard_map/two_back/pallas_call | solution.py:359
  49.5 1.8 %collective-permute-start.19 = (bf16[96,384]{1,0:T(8,128)(2,1)S(1)}, bf16[96,384]{1,0:T(8,128)(2,1)S(1)}, u32[]{:S(2)}, u32[]{:S(2)}) collective-permute-start(bf16[96,384]{1,0:T(8,128)(2,1)S(1)} %get-tuple-element.31), channel_id=1, source_target_pairs={{0,32},{1,5},{2,34},{3,7},{4,36},{5,1},{6,38},{7,3},{8,40},{9,13},... | collective-permute-start | bytes 221192 | tf_op jit(solution)/shard_map/ppermute | solution.py:402
  51.3 3.6 %collective-permute-start.20 = (bf16[96,384]{1,0:T(8,128)(2,1)S(1)}, bf16[96,384]{1,0:T(8,128)(2,1)S(1)}, u32[]{:S(2)}, u32[]{:S(2)}) collective-permute-start(bf16[96,384]{1,0:T(8,128)(2,1)S(1)} %get-tuple-element.32), channel_id=1, source_target_pairs={{0,4},{1,33},{2,6},{3,35},{4,0},{5,37},{6,2},{7,39},{8,12},{9,41},... | collective-permute-start | bytes 221192 | tf_op jit(solution)/shard_map/ppermute | solution.py:402
  54.9 2.8 %collective-permute-done.20 = bf16[96,384]{1,0:T(8,128)(2,1)S(1)} collective-permute-done((bf16[96,384]{1,0:T(8,128)(2,1)S(1)}, bf16[96,384]{1,0:T(8,128)(2,1)S(1)}, u32[]{:S(2)}, u32[]{:S(2)}) %collective-permute-start.20) | collective-permute-done | bytes 73760 | tf_op jit(solution)/shard_map/ppermute | solution.py:402
  57.7 2.4 %collective-permute-done.21 = bf16[96,384]{1,0:T(8,128)(2,1)S(1)} collective-permute-done((bf16[96,384]{1,0:T(8,128)(2,1)S(1)}, bf16[96,384]{1,0:T(8,128)(2,1)S(1)}, u32[]{:S(2)}, u32[]{:S(2)}) %collective-permute-start.21) | collective-permute-done | bytes 73760 | tf_op jit(solution)/shard_map/ppermute | solution.py:402
  60.2 4.3 %collective-permute-start.24 = (bf16[96,384]{1,0:T(8,128)(2,1)S(1)}, bf16[96,384]{1,0:T(8,128)(2,1)S(1)}, u32[]{:S(2)}, u32[]{:S(2)}) collective-permute-start(bf16[96,384]{1,0:T(8,128)(2,1)S(1)} %add_convert_fusion.3), channel_id=1, source_target_pairs={{0,124},{1,125},{2,126},{3,127},{4,104},{5,105},{6,106},{7,107},{8... | collective-permute-start | bytes 221192 | tf_op jit(solution)/shard_map/ppermute | solution.py:402
  64.4 1.1 %collective-permute-start.22 = (bf16[96,384]{1,0:T(8,128)(2,1)S(1)}, bf16[96,384]{1,0:T(8,128)(2,1)S(1)}, u32[]{:S(2)}, u32[]{:S(2)}) collective-permute-start(bf16[96,384]{1,0:T(8,128)(2,1)S(1)} %add_convert_fusion.3), channel_id=1, source_target_pairs={{0,96},{1,29},{2,98},{3,31},{4,100},{5,9},{6,102},{7,11},{8,104},{... | collective-permute-start | bytes 221192 | tf_op jit(solution)/shard_map/ppermute | solution.py:402
  65.6 1.2 %collective-permute-done.24 = bf16[96,384]{1,0:T(8,128)(2,1)S(1)} collective-permute-done((bf16[96,384]{1,0:T(8,128)(2,1)S(1)}, bf16[96,384]{1,0:T(8,128)(2,1)S(1)}, u32[]{:S(2)}, u32[]{:S(2)}) %collective-permute-start.24) | collective-permute-done | bytes 73760 | tf_op jit(solution)/shard_map/ppermute | solution.py:402
  66.8 2.0 %collective-permute-done.23 = bf16[96,384]{1,0:T(8,128)(2,1)S(1)} collective-permute-done((bf16[96,384]{1,0:T(8,128)(2,1)S(1)}, bf16[96,384]{1,0:T(8,128)(2,1)S(1)}, u32[]{:S(2)}, u32[]{:S(2)}) %collective-permute-start.23) | collective-permute-done | bytes 73760 | tf_op jit(solution)/shard_map/ppermute | solution.py:402
  68.8 1.2 %collective-permute-done.22 = bf16[96,384]{1,0:T(8,128)(2,1)S(1)} collective-permute-done((bf16[96,384]{1,0:T(8,128)(2,1)S(1)}, bf16[96,384]{1,0:T(8,128)(2,1)S(1)}, u32[]{:S(2)}, u32[]{:S(2)}) %collective-permute-start.22) | collective-permute-done | bytes 73760 | tf_op jit(solution)/shard_map/ppermute | solution.py:402
  70.1 1.7 %collective-permute-start.25 = (bf16[96,384]{1,0:T(8,128)(2,1)S(1)}, bf16[96,384]{1,0:T(8,128)(2,1)S(1)}, u32[]{:S(2)}, u32[]{:S(2)}) collective-permute-start(bf16[96,384]{1,0:T(8,128)(2,1)S(1)} %add_convert_fusion.2), channel_id=1, source_target_pairs={{0,128},{1,13},{2,130},{3,15},{4,132},{5,25},{6,134},{7,27},{8,136... | collective-permute-start | bytes 221192 | tf_op jit(solution)/shard_map/ppermute | solution.py:402
  71.7 4.2 %collective-permute-done.25 = bf16[96,384]{1,0:T(8,128)(2,1)S(1)} collective-permute-done((bf16[96,384]{1,0:T(8,128)(2,1)S(1)}, bf16[96,384]{1,0:T(8,128)(2,1)S(1)}, u32[]{:S(2)}, u32[]{:S(2)}) %collective-permute-start.25) | collective-permute-done | bytes 73760 | tf_op jit(solution)/shard_map/ppermute | solution.py:402
  76.0 2.9 %collective-permute-start.26 = (bf16[96,384]{1,0:T(8,128)(2,1)S(1)}, bf16[96,384]{1,0:T(8,128)(2,1)S(1)}, u32[]{:S(2)}, u32[]{:S(2)}) collective-permute-start(bf16[96,384]{1,0:T(8,128)(2,1)S(1)} %add_convert_fusion.1), channel_id=1, source_target_pairs={{0,12},{1,129},{2,14},{3,131},{4,24},{5,133},{6,26},{7,135},{8,20}... | collective-permute-start | bytes 221192 | tf_op jit(solution)/shard_map/ppermute | solution.py:402
  79.0 5.3 %collective-permute-done.26 = bf16[96,384]{1,0:T(8,128)(2,1)S(1)} collective-permute-done((bf16[96,384]{1,0:T(8,128)(2,1)S(1)}, bf16[96,384]{1,0:T(8,128)(2,1)S(1)}, u32[]{:S(2)}, u32[]{:S(2)}) %collective-permute-start.26) | collective-permute-done | bytes 73760 | tf_op jit(solution)/shard_map/ppermute | solution.py:402
  84.5 3.3 %collective-permute-start.27 = (bf16[96,384]{1,0:T(8,128)(2,1)S(1)}, bf16[96,384]{1,0:T(8,128)(2,1)S(1)}, u32[]{:S(2)}, u32[]{:S(2)}) collective-permute-start(bf16[96,384]{1,0:T(8,128)(2,1)S(1)} %add_convert_fusion.p0), channel_id=1, source_target_pairs={{0,32},{1,5},{2,34},{3,7},{4,36},{5,1},{6,38},{7,3},{8,40},{9,13},... | collective-permute-start | bytes 221192 | tf_op jit(solution)/shard_map/ppermute | solution.py:402
  87.9 1.2 %decode.1 = bf16[512,384]{1,0:T(8,128)(2,1)} custom-call(bf16[208,384]{1,0:T(8,128)(2,1)S(1)} %get-tuple-element.26.front_rows, bf16[304,384]{1,0:T(8,128)(2,1)S(1)} %get-tuple-element.29.back_rows, bf16[384,384]{1,0:T(8,128)(2,1)S(1)} %copy-done.3), custom_call_target="tpu_custom_call" | custom-call | flops 150994 | bytes 1024 | tf_op jit(solution)/shard_map/decode/pallas_call | solution.py:368
  89.0 0.6 collective-permute-done.29.p3
  89.7 0.8 collective-permute-done.27.p1
  90.4 1.4 %assemble.1 = f32[384,384]{1,0:T(8,128)} custom-call(s32[6]{0:T(128)S(1)} %stack.23.ids, bf16[96,384]{1,0:T(8,128)(2,1)S(1)} %add_convert_fusion.p0, bf16[96,384]{1,0:T(8,128)(2,1)S(1)} %collective-permute-done.27.p1, bf16[96,384]{1,0:T(8,128)(2,1)S(1)} %collective-permute-done.28.p2, bf16[96,384]{1,0:T(8,128)(2,1)S(1)} %collective-permute-done.29.p3), custom_call_target="tpu_custom_call" | custom-call | bytes 1024 | tf_op jit(solution)/shard_map/assemble/pallas_call | solution.py:422
  (39 shorter events, 1.5 us)
Async XLA Ops:
  0.6 16.5 %collective-permute-start.1 = (bf16[512,384]{1,0:T(8,128)(2,1)}, bf16[512,384]{1,0:T(8,128)(2,1)S(1)}, u32[]{:S(2)}, u32[]{:S(2)}) collective-permute-start(bf16[512,384]{1,0:T(8,128)(2,1)} %param.7), channel_id=1, source_target_pairs={{0,1},{1,0},{2,3},{3,2},{4,5},{5,4},{6,7},{7,6},{8,9},{9,8},{10,11... | collective-permute-start | bytes 1179656 | tf_op jit(solution)/shard_map/ppermute | solution.py:260
  1.8 13.9 %collective-permute-start.2 = (bf16[256,384]{1,0:T(8,128)(2,1)S(1)}, bf16[256,384]{1,0:T(8,128)(2,1)S(1)}, u32[]{:S(2)}, u32[]{:S(2)}) collective-permute-start(bf16[256,384]{1,0:T(8,128)(2,1)S(1)} %get-tuple-element.18.own_a), channel_id=1, source_target_pairs={{0,2},{1,3},{2,0},{3,1},{4,6},{5,7},{6,4},{7,5},{8,10},{9,11},{10,... | collective-permute-start | bytes 589832 | tf_op jit(solution)/shard_map/ppermute | solution.py:258
  3.5 12.3 %collective-permute-start.4 = (bf16[256,384]{1,0:T(8,128)(2,1)S(1)}, bf16[256,384]{1,0:T(8,128)(2,1)S(1)}, u32[]{:S(2)}, u32[]{:S(2)}) collective-permute-start(bf16[256,384]{1,0:T(8,128)(2,1)S(1)} %get-tuple-element.19.own_b), channel_id=1, source_target_pairs={{0,130},{1,131},{2,128},{3,129},{128,2},{129,3},{130,0},{131,1},{4... | collective-permute-start | bytes 589832 | tf_op jit(solution)/shard_map/ppermute | solution.py:259
  6.4 8.9 %collective-permute-start = (s32[16,128]{1,0:T(8,128)S(1)}, s32[16,128]{1,0:T(8,128)S(1)}, u32[]{:S(2)}, u32[]{:S(2)}) collective-permute-start(s32[16,128]{1,0:T(8,128)S(1)} %bitcast.15), channel_id=1, source_target_pairs={{0,4},{4,8},{8,12},{12,16},{16,20},{20,24},{24,28},{28,32},{32,36}... | collective-permute-start | bytes 24584 | tf_op jit(solution)/shard_map/ppermute | solution.py:261
  10.2 5.5 %collective-permute-start.3 = (s32[16,128]{1,0:T(8,128)S(1)}, s32[16,128]{1,0:T(8,128)S(1)}, u32[]{:S(2)}, u32[]{:S(2)}) collective-permute-start(s32[16,128]{1,0:T(8,128)S(1)} %bitcast.14), channel_id=1, source_target_pairs={{4,0},{8,4},{12,8},{16,12},{20,16},{24,20},{28,24},{32,28},{36,32}... | collective-permute-start | bytes 24584 | tf_op jit(solution)/shard_map/ppermute | solution.py:279
  12.4 2.6 %copy-start.2 = (s32[1,65536]{1,0:T(1,128)S(1)}, s32[1,65536]{1,0:T(1,128)}, u32[]{:S(2)}) copy-start(s32[1,65536]{1,0:T(1,128)} %param.6) | copy-start | bytes 786436
  12.4 5.1 %copy-start.1 = (f32[3,1536]{1,0:T(4,128)S(1)}, f32[3,1536]{1,0:T(4,128)}, u32[]{:S(2)}) copy-start(f32[3,1536]{1,0:T(4,128)} %refs_8_.3) | copy-start | bytes 55300
  15.7 1.4 %collective-permute-start.6 = (bf16[256,384]{1,0:T(8,128)(2,1)S(1)}, bf16[256,384]{1,0:T(8,128)(2,1)S(1)}, u32[]{:S(2)}, u32[]{:S(2)}) collective-permute-start(bf16[256,384]{1,0:T(8,128)(2,1)S(1)} %collective-permute-done.4.w2b), channel_id=1, source_target_pairs={{0,1},{1,0},{2,3},{3,2},{4,5},{5,4},{6,7},{7,6},{8,9},{9,8},{10,11... | collective-permute-start | bytes 589832 | tf_op jit(solution)/shard_map/ppermute | solution.py:283
  15.7 1.7 %collective-permute-start.5 = (bf16[256,384]{1,0:T(8,128)(2,1)S(1)}, bf16[256,384]{1,0:T(8,128)(2,1)S(1)}, u32[]{:S(2)}, u32[]{:S(2)}) collective-permute-start(bf16[256,384]{1,0:T(8,128)(2,1)S(1)} %collective-permute-done.2.w2a), channel_id=1, source_target_pairs={{0,1},{1,0},{2,3},{3,2},{4,5},{5,4},{6,7},{7,6},{8,9},{9,8},{10,11... | collective-permute-start | bytes 589832 | tf_op jit(solution)/shard_map/ppermute | solution.py:282
  20.6 8.1 %collective-permute-start.8 = (bf16[256,384]{1,0:T(8,128)(2,1)S(1)}, bf16[256,384]{1,0:T(8,128)(2,1)S(1)}, u32[]{:S(2)}, u32[]{:S(2)}) collective-permute-start(bf16[256,384]{1,0:T(8,128)(2,1)S(1)} %zero_front.1.refs_0_), channel_id=1, source_target_pairs={{0,2},{1,3},{2,0},{3,1},{4,6},{5,7},{6,4},{7,5},{8,10},{9,11},{10,... | collective-permute-start | bytes 589832 | tf_op jit(solution)/shard_map/ppermute | solution.py:295
  21.3 7.9 %collective-permute-start.7 = (bf16[256,384]{1,0:T(8,128)(2,1)S(1)}, bf16[256,384]{1,0:T(8,128)(2,1)S(1)}, u32[]{:S(2)}, u32[]{:S(2)}) collective-permute-start(bf16[256,384]{1,0:T(8,128)(2,1)S(1)} %zero_front.1.refs_0_), channel_id=1, source_target_pairs={{0,1},{1,0},{2,3},{3,2},{4,5},{5,4},{6,7},{7,6},{8,9},{9,8},{10,11... | collective-permute-start | bytes 589832 | tf_op jit(solution)/shard_map/ppermute | solution.py:295
  24.6 7.9 %collective-permute-start.13 = (bf16[288,384]{1,0:T(8,128)(2,1)S(1)}, bf16[288,384]{1,0:T(8,128)(2,1)S(1)}, u32[]{:S(2)}, u32[]{:S(2)}) collective-permute-start(bf16[288,384]{1,0:T(8,128)(2,1)S(1)} %zero_back.1.refs_4_), channel_id=1, source_target_pairs={{0,2},{1,3},{2,0},{3,1},{4,6},{5,7},{6,4},{7,5},{8,10},{9,11},{10,... | collective-permute-start | bytes 663560 | tf_op jit(solution)/shard_map/ppermute | solution.py:295
  28.7 1.5 %collective-permute-start.9 = (bf16[256,384]{1,0:T(8,128)(2,1)S(1)}, bf16[256,384]{1,0:T(8,128)(2,1)S(1)}, u32[]{:S(2)}, u32[]{:S(2)}) collective-permute-start(bf16[256,384]{1,0:T(8,128)(2,1)S(1)} %collective-permute-done.8.refs_2_), channel_id=1, source_target_pairs={{0,1},{1,0},{2,3},{3,2},{4,5},{5,4},{6,7},{7,6},{8,9},{9,8},{10,11... | collective-permute-start | bytes 589832 | tf_op jit(solution)/shard_map/ppermute | solution.py:300
  29.0 5.2 %collective-permute-start.12 = (bf16[288,384]{1,0:T(8,128)(2,1)S(1)}, bf16[288,384]{1,0:T(8,128)(2,1)S(1)}, u32[]{:S(2)}, u32[]{:S(2)}) collective-permute-start(bf16[288,384]{1,0:T(8,128)(2,1)S(1)} %zero_back.1.refs_4_), channel_id=1, source_target_pairs={{0,1},{1,0},{2,3},{3,2},{4,5},{5,4},{6,7},{7,6},{8,9},{9,8},{10,11... | collective-permute-start | bytes 663560 | tf_op jit(solution)/shard_map/ppermute | solution.py:295
  32.5 1.6 %collective-permute-start.14 = (bf16[288,384]{1,0:T(8,128)(2,1)S(1)}, bf16[288,384]{1,0:T(8,128)(2,1)S(1)}, u32[]{:S(2)}, u32[]{:S(2)}) collective-permute-start(bf16[288,384]{1,0:T(8,128)(2,1)S(1)} %collective-permute-done.13.refs_6_), channel_id=1, source_target_pairs={{0,1},{1,0},{2,3},{3,2},{4,5},{5,4},{6,7},{7,6},{8,9},{9,8},{10,11... | collective-permute-start | bytes 663560 | tf_op jit(solution)/shard_map/ppermute | solution.py:300
  32.8 7.9 %collective-permute-start.11 = (bf16[240,384]{1,0:T(8,128)(2,1)S(1)}, bf16[240,384]{1,0:T(8,128)(2,1)S(1)}, u32[]{:S(2)}, u32[]{:S(2)}) collective-permute-start(bf16[240,384]{1,0:T(8,128)(2,1)S(1)} %one_front.1.refs_0_), channel_id=1, source_target_pairs={{0,2},{1,3},{2,0},{3,1},{4,6},{5,7},{6,4},{7,5},{8,10},{9,11},{10,... | collective-permute-start | bytes 552968 | tf_op jit(solution)/shard_map/ppermute | solution.py:295
  33.9 7.5 %collective-permute-start.10 = (bf16[240,384]{1,0:T(8,128)(2,1)S(1)}, bf16[240,384]{1,0:T(8,128)(2,1)S(1)}, u32[]{:S(2)}, u32[]{:S(2)}) collective-permute-start(bf16[240,384]{1,0:T(8,128)(2,1)S(1)} %one_front.1.refs_0_), channel_id=1, source_target_pairs={{0,1},{1,0},{2,3},{3,2},{4,5},{5,4},{6,7},{7,6},{8,9},{9,8},{10,11... | collective-permute-start | bytes 552968 | tf_op jit(solution)/shard_map/ppermute | solution.py:295
  36.8 5.5 %copy-start = (bf16[1,512,384]{2,1,0:T(8,128)(2,1)S(1)}, bf16[1,512,384]{2,1,0:T(8,128)(2,1)}, u32[]{:S(2)}) copy-start(bf16[1,512,384]{2,1,0:T(8,128)(2,1)} %param.11) | copy-start | bytes 1179652
  36.9 8.0 %collective-permute-start.17 = (bf16[304,384]{1,0:T(8,128)(2,1)S(1)}, bf16[304,384]{1,0:T(8,128)(2,1)S(1)}, u32[]{:S(2)}, u32[]{:S(2)}) collective-permute-start(bf16[304,384]{1,0:T(8,128)(2,1)S(1)} %one_back.1.refs_4_), channel_id=1, source_target_pairs={{0,2},{1,3},{2,0},{3,1},{4,6},{5,7},{6,4},{7,5},{8,10},{9,11},{10,... | collective-permute-start | bytes 700424 | tf_op jit(solution)/shard_map/ppermute | solution.py:295
  40.8 1.5 %collective-permute-start.15 = (bf16[240,384]{1,0:T(8,128)(2,1)S(1)}, bf16[240,384]{1,0:T(8,128)(2,1)S(1)}, u32[]{:S(2)}, u32[]{:S(2)}) collective-permute-start(bf16[240,384]{1,0:T(8,128)(2,1)S(1)} %collective-permute-done.11.refs_2_), channel_id=1, source_target_pairs={{0,1},{1,0},{2,3},{3,2},{4,5},{5,4},{6,7},{7,6},{8,9},{9,8},{10,11... | collective-permute-start | bytes 552968 | tf_op jit(solution)/shard_map/ppermute | solution.py:300
  40.9 4.1 %collective-permute-start.16 = (bf16[304,384]{1,0:T(8,128)(2,1)S(1)}, bf16[304,384]{1,0:T(8,128)(2,1)S(1)}, u32[]{:S(2)}, u32[]{:S(2)}) collective-permute-start(bf16[304,384]{1,0:T(8,128)(2,1)S(1)} %one_back.1.refs_4_), channel_id=1, source_target_pairs={{0,1},{1,0},{2,3},{3,2},{4,5},{5,4},{6,7},{7,6},{8,9},{9,8},{10,11... | collective-permute-start | bytes 700424 | tf_op jit(solution)/shard_map/ppermute | solution.py:295
  44.8 1.5 %collective-permute-start.18 = (bf16[304,384]{1,0:T(8,128)(2,1)S(1)}, bf16[304,384]{1,0:T(8,128)(2,1)S(1)}, u32[]{:S(2)}, u32[]{:S(2)}) collective-permute-start(bf16[304,384]{1,0:T(8,128)(2,1)S(1)} %collective-permute-done.17.refs_6_), channel_id=1, source_target_pairs={{0,1},{1,0},{2,3},{3,2},{4,5},{5,4},{6,7},{7,6},{8,9},{9,8},{10,11... | collective-permute-start | bytes 700424 | tf_op jit(solution)/shard_map/ppermute | solution.py:300
  46.3 41.5 %copy-start.3 = (bf16[384,384]{1,0:T(8,128)(2,1)S(1)}, bf16[384,384]{1,0:T(8,128)(2,1)}, u32[]{:S(2)}) copy-start(bf16[384,384]{1,0:T(8,128)(2,1)} %weights.1) | copy-start | bytes 884740
  49.5 5.4 %collective-permute-start.19 = (bf16[96,384]{1,0:T(8,128)(2,1)S(1)}, bf16[96,384]{1,0:T(8,128)(2,1)S(1)}, u32[]{:S(2)}, u32[]{:S(2)}) collective-permute-start(bf16[96,384]{1,0:T(8,128)(2,1)S(1)} %get-tuple-element.31), channel_id=1, source_target_pairs={{0,32},{1,5},{2,34},{3,7},{4,36},{5,1},{6,38},{7,3},{8,40},{9,13},... | collective-permute-start | bytes 221192 | tf_op jit(solution)/shard_map/ppermute | solution.py:402
  51.3 6.5 %collective-permute-start.20 = (bf16[96,384]{1,0:T(8,128)(2,1)S(1)}, bf16[96,384]{1,0:T(8,128)(2,1)S(1)}, u32[]{:S(2)}, u32[]{:S(2)}) collective-permute-start(bf16[96,384]{1,0:T(8,128)(2,1)S(1)} %get-tuple-element.32), channel_id=1, source_target_pairs={{0,4},{1,33},{2,6},{3,35},{4,0},{5,37},{6,2},{7,39},{8,12},{9,41},... | collective-permute-start | bytes 221192 | tf_op jit(solution)/shard_map/ppermute | solution.py:402
  54.9 5.3 %collective-permute-start.21 = (bf16[96,384]{1,0:T(8,128)(2,1)S(1)}, bf16[96,384]{1,0:T(8,128)(2,1)S(1)}, u32[]{:S(2)}, u32[]{:S(2)}) collective-permute-start(bf16[96,384]{1,0:T(8,128)(2,1)S(1)} %get-tuple-element.33), channel_id=1, source_target_pairs={{0,36},{1,37},{2,38},{3,39},{4,32},{5,33},{6,34},{7,35},{8,44},{9,... | collective-permute-start | bytes 221192 | tf_op jit(solution)/shard_map/ppermute | solution.py:402
  60.2 6.6 %collective-permute-start.24 = (bf16[96,384]{1,0:T(8,128)(2,1)S(1)}, bf16[96,384]{1,0:T(8,128)(2,1)S(1)}, u32[]{:S(2)}, u32[]{:S(2)}) collective-permute-start(bf16[96,384]{1,0:T(8,128)(2,1)S(1)} %add_convert_fusion.3), channel_id=1, source_target_pairs={{0,124},{1,125},{2,126},{3,127},{4,104},{5,105},{6,106},{7,107},{8... | collective-permute-start | bytes 221192 | tf_op jit(solution)/shard_map/ppermute | solution.py:402
  64.4 4.4 %collective-permute-start.23 = (bf16[96,384]{1,0:T(8,128)(2,1)S(1)}, bf16[96,384]{1,0:T(8,128)(2,1)S(1)}, u32[]{:S(2)}, u32[]{:S(2)}) collective-permute-start(bf16[96,384]{1,0:T(8,128)(2,1)S(1)} %add_convert_fusion.3), channel_id=1, source_target_pairs={{0,28},{1,97},{2,30},{3,99},{4,8},{5,101},{6,10},{7,103},{8,4},{9,... | collective-permute-start | bytes 221192 | tf_op jit(solution)/shard_map/ppermute | solution.py:402
  64.4 5.6 %collective-permute-start.22 = (bf16[96,384]{1,0:T(8,128)(2,1)S(1)}, bf16[96,384]{1,0:T(8,128)(2,1)S(1)}, u32[]{:S(2)}, u32[]{:S(2)}) collective-permute-start(bf16[96,384]{1,0:T(8,128)(2,1)S(1)} %add_convert_fusion.3), channel_id=1, source_target_pairs={{0,96},{1,29},{2,98},{3,31},{4,100},{5,9},{6,102},{7,11},{8,104},{... | collective-permute-start | bytes 221192 | tf_op jit(solution)/shard_map/ppermute | solution.py:402
  70.1 5.9 %collective-permute-start.25 = (bf16[96,384]{1,0:T(8,128)(2,1)S(1)}, bf16[96,384]{1,0:T(8,128)(2,1)S(1)}, u32[]{:S(2)}, u32[]{:S(2)}) collective-permute-start(bf16[96,384]{1,0:T(8,128)(2,1)S(1)} %add_convert_fusion.2), channel_id=1, source_target_pairs={{0,128},{1,13},{2,130},{3,15},{4,132},{5,25},{6,134},{7,27},{8,136... | collective-permute-start | bytes 221192 | tf_op jit(solution)/shard_map/ppermute | solution.py:402
  76.0 8.2 %collective-permute-start.26 = (bf16[96,384]{1,0:T(8,128)(2,1)S(1)}, bf16[96,384]{1,0:T(8,128)(2,1)S(1)}, u32[]{:S(2)}, u32[]{:S(2)}) collective-permute-start(bf16[96,384]{1,0:T(8,128)(2,1)S(1)} %add_convert_fusion.1), channel_id=1, source_target_pairs={{0,12},{1,129},{2,14},{3,131},{4,24},{5,133},{6,26},{7,135},{8,20}... | collective-permute-start | bytes 221192 | tf_op jit(solution)/shard_map/ppermute | solution.py:402
  84.3 5.4 %collective-permute-start.29 = (bf16[96,384]{1,0:T(8,128)(2,1)S(1)}, bf16[96,384]{1,0:T(8,128)(2,1)S(1)}, u32[]{:S(2)}, u32[]{:S(2)}) collective-permute-start(bf16[96,384]{1,0:T(8,128)(2,1)S(1)} %add_convert_fusion.p0), channel_id=1, source_target_pairs={{0,36},{1,37},{2,38},{3,39},{4,32},{5,33},{6,34},{7,35},{8,44},{9,... | collective-permute-start | bytes 221192 | tf_op jit(solution)/shard_map/ppermute | solution.py:402
  84.4 5.3 %collective-permute-start.28 = (bf16[96,384]{1,0:T(8,128)(2,1)S(1)}, bf16[96,384]{1,0:T(8,128)(2,1)S(1)}, u32[]{:S(2)}, u32[]{:S(2)}) collective-permute-start(bf16[96,384]{1,0:T(8,128)(2,1)S(1)} %add_convert_fusion.p0), channel_id=1, source_target_pairs={{0,4},{1,33},{2,6},{3,35},{4,0},{5,37},{6,2},{7,39},{8,12},{9,41},... | collective-permute-start | bytes 221192 | tf_op jit(solution)/shard_map/ppermute | solution.py:402
  84.5 5.9 %collective-permute-start.27 = (bf16[96,384]{1,0:T(8,128)(2,1)S(1)}, bf16[96,384]{1,0:T(8,128)(2,1)S(1)}, u32[]{:S(2)}, u32[]{:S(2)}) collective-permute-start(bf16[96,384]{1,0:T(8,128)(2,1)S(1)} %add_convert_fusion.p0), channel_id=1, source_target_pairs={{0,32},{1,5},{2,34},{3,7},{4,36},{5,1},{6,38},{7,3},{8,40},{9,13},... | collective-permute-start | bytes 221192 | tf_op jit(solution)/shard_map/ppermute | solution.py:402

commit v7 on v6

--- a/solution.py
+++ b/solution.py
@@ -416,8 +416,8 @@
     total = (own.astype(f32) + r1.astype(f32)) + (r2.astype(f32) + r3.astype(f32))
     own = total.astype(bf16)
     sections, far_z = (flip, same, same), (same, same, zs_far)
+    own = add(own, swap(own, far_z, sections))
     own = add(own, swap(own, sections, far_z))
-    own = add(own, swap(own, far_z, sections))
     r1, r2, r3 = swap_three(flip, flip, own, own, own)
     weight_grad = call(
         "assemble",

time: 92.4 us -> 92.2 us (level)
  no operation moved by 1% of the time
where the time goes in v7:
time: 92.2 us; the launch traced here: 91.1 us
  starting transfers between devices  35.7 us (39%)
  Pallas kernels  27.6 us (30%)
  waiting for transfers between devices  24.9 us (27%)
  local copies, waits for them, and re-layouts  1.88 us (2%)
  between operations  0.94 us (1%)
    ppermute x11, waiting for transfers between devices, swap(): return lax.ppermute(own, ('section', 'seq', 'chan'), perm)  19.9 us
    ppermute x11, starting transfers between devices, swap(): return lax.ppermute(own, ('section', 'seq', 'chan'), perm)  19 us
    pallas_call x3, Pallas kernels, fetched(): call('fetch', functools.partial(fetch, layer), jax.ShapeDtypeStruct(conv_...  7.77 us
    ppermute x8, starting transfers between devices, exchange(): return (own, other_core(own), across(own))  5.59 us
    ppermute x1, starting transfers between devices, body(): before = lax.ppermute(letters[bins - HALO:], 'seq', up)  3.81 us
    pallas_call x1, Pallas kernels, body(): call('zero_back', functools.partial(first_layer, (cut, rows), bins, count...  3.28 us
    ppermute x4, waiting for transfers between devices, finish(): return (own, beside, remote, other_core(remote))  3.2 us
    pallas_call x1, Pallas kernels, body(): call('two_back', functools.partial(last_back, (cut, rows - HALO), bins),...  3.14 us
  transfers between devices with their start and end apart: 30, of which 16 were waited for; matrix products, arithmetic and copies ran while one was open for 2% of the time, Pallas kernels for 22%

profile of v7, /device:TPU:32, one launch (start us, length us, event | category | flops | bytes accessed | tf_op | source)
XLA Modules:
  0.0 91.1 jit_solution(2303192845943429517)
XLA Ops:
  0.7 1.1 %fusion = (bf16[256,384]{1,0:T(8,128)(2,1)S(1)}, bf16[256,384]{1,0:T(8,128)(2,1)S(1)}) fusion(bf16[512,384]{1,0:T(8,128)(2,1)} %param.7), kind=kLoop, calls=%fused_computation.4 | loop fusion | bytes 786432 | tf_op jit(solution)/shard_map/slice | solution.py:257
  1.8 1.7 %collective-permute-start.2 = (bf16[256,384]{1,0:T(8,128)(2,1)S(1)}, bf16[256,384]{1,0:T(8,128)(2,1)S(1)}, u32[]{:S(2)}, u32[]{:S(2)}) collective-permute-start(bf16[256,384]{1,0:T(8,128)(2,1)S(1)} %get-tuple-element.18.own_a), channel_id=1, source_target_pairs={{0,2},{1,3},{2,0},{3,1},{4,6},{5,7},{6,4},{7,5},{8,10},{9,11},{10,... | collective-permute-start | bytes 589832 | tf_op jit(solution)/shard_map/ppermute | solution.py:258
  3.5 2.2 %collective-permute-start.4 = (bf16[256,384]{1,0:T(8,128)(2,1)S(1)}, bf16[256,384]{1,0:T(8,128)(2,1)S(1)}, u32[]{:S(2)}, u32[]{:S(2)}) collective-permute-start(bf16[256,384]{1,0:T(8,128)(2,1)S(1)} %get-tuple-element.19.own_b), channel_id=1, source_target_pairs={{0,130},{1,131},{2,128},{3,129},{128,2},{129,3},{130,0},{131,1},{4... | collective-permute-start | bytes 589832 | tf_op jit(solution)/shard_map/ppermute | solution.py:259
  5.6 0.7 fusion.1
  6.4 3.8 %collective-permute-start = (s32[16,128]{1,0:T(8,128)S(1)}, s32[16,128]{1,0:T(8,128)S(1)}, u32[]{:S(2)}, u32[]{:S(2)}) collective-permute-start(s32[16,128]{1,0:T(8,128)S(1)} %bitcast.15), channel_id=1, source_target_pairs={{0,4},{4,8},{8,12},{12,16},{16,20},{20,24},{24,28},{28,32},{32,36}... | collective-permute-start | bytes 24584 | tf_op jit(solution)/shard_map/ppermute | solution.py:261
  10.2 2.0 %collective-permute-start.3 = (s32[16,128]{1,0:T(8,128)S(1)}, s32[16,128]{1,0:T(8,128)S(1)}, u32[]{:S(2)}, u32[]{:S(2)}) collective-permute-start(s32[16,128]{1,0:T(8,128)S(1)} %bitcast.14), channel_id=1, source_target_pairs={{4,0},{8,4},{12,8},{16,12},{20,16},{24,20},{28,24},{32,28},{36,32}... | collective-permute-start | bytes 24584 | tf_op jit(solution)/shard_map/ppermute | solution.py:279
  12.4 2.6 %fetch.3.weights = bf16[3,1536,384]{2,1,0:T(8,128)(2,1)S(1)} custom-call(s32[6]{0:T(128)S(1)} %stack.23.ids, bf16[3,3,1536,384]{3,2,1,0:T(8,128)(2,1)} %w_hbm.5), custom_call_target="tpu_custom_call" | custom-call | flops 1000000000 | bytes 1024 | tf_op jit(solution)/shard_map/fetch/pallas_call | solution.py:263
  15.3 0.4 collective-permute-done.3.halo
  15.7 0.5 collective-permute-start.5
  16.2 0.9 %collective-permute-done.6.w3b = bf16[256,384]{1,0:T(8,128)(2,1)S(1)} collective-permute-done((bf16[256,384]{1,0:T(8,128)(2,1)S(1)}, bf16[256,384]{1,0:T(8,128)(2,1)S(1)}, u32[]{:S(2)}, u32[]{:S(2)}) %collective-permute-start.6) | collective-permute-done | bytes 196640 | tf_op jit(solution)/shard_map/ppermute | solution.py:283
  17.5 3.1 %zero_front.1.refs_0_ = bf16[256,384]{1,0:T(8,128)(2,1)S(1)} custom-call(s32[6]{0:T(128)S(1)} %stack.23.ids, bf16[512,512]{1,0:T(8,128)(2,1)S(1)} %prepare.1.onehot, s32[16,128]{1,0:T(8,128)S(1)} %collective-permute-done.halo, bf16[256,384]{1,0:T(8,128)(2,1)S(1)} %get-tuple-element.18.own_a, bf16[256,384]{1,0:T(8,128)(2,1)S(1)} %get-tuple-element.19.own_b, ...), custom_call_target="tpu_custom_call" | custom-call | flops 905969 | bytes 1024 | tf_op jit(solution)/shard_map/zero_front/pallas_call | solution.py:304
  20.6 0.8 collective-permute-start.8
  21.3 3.3 %zero_back.1.refs_4_ = bf16[288,384]{1,0:T(8,128)(2,1)S(1)} custom-call(s32[6]{0:T(128)S(1)} %stack.23.ids, bf16[512,512]{1,0:T(8,128)(2,1)S(1)} %prepare.1.onehot, s32[16,128]{1,0:T(8,128)S(1)} %collective-permute-done.3.halo, bf16[256,384]{1,0:T(8,128)(2,1)S(1)} %get-tuple-element.18.own_a, bf16[256,384]{1,0:T(8,128)(2,1)S(1)} %get-tuple-element.19.own_b, ...), custom_call_target="tpu_custom_call" | custom-call | flops 1019215 | bytes 1024 | tf_op jit(solution)/shard_map/zero_back/pallas_call | solution.py:313
  24.6 1.4 %collective-permute-start.13 = (bf16[288,384]{1,0:T(8,128)(2,1)S(1)}, bf16[288,384]{1,0:T(8,128)(2,1)S(1)}, u32[]{:S(2)}, u32[]{:S(2)}) collective-permute-start(bf16[288,384]{1,0:T(8,128)(2,1)S(1)} %zero_back.1.refs_4_), channel_id=1, source_target_pairs={{0,2},{1,3},{2,0},{3,1},{4,6},{5,7},{6,4},{7,5},{8,10},{9,11},{10,... | collective-permute-start | bytes 663560 | tf_op jit(solution)/shard_map/ppermute | solution.py:295
  26.1 2.6 %fetch.4.refs_5_.refs_9_ = bf16[3,1536,384]{2,1,0:T(8,128)(2,1)S(1)} custom-call(s32[6]{0:T(128)S(1)} %stack.23.ids, bf16[3,3,1536,384]{3,2,1,0:T(8,128)(2,1)} %w_hbm.5), custom_call_target="tpu_custom_call" | custom-call | flops 1000000000 | bytes 1024 | tf_op jit(solution)/shard_map/fetch/pallas_call | solution.py:263
  28.7 0.3 collective-permute-start.9
  29.0 0.3 collective-permute-start.12
  29.3 0.9 %collective-permute-done.9.refs_3_ = bf16[256,384]{1,0:T(8,128)(2,1)S(1)} collective-permute-done((bf16[256,384]{1,0:T(8,128)(2,1)S(1)}, bf16[256,384]{1,0:T(8,128)(2,1)S(1)}, u32[]{:S(2)}, u32[]{:S(2)}) %collective-permute-start.9) | collective-permute-done | bytes 196640 | tf_op jit(solution)/shard_map/ppermute | solution.py:300
  30.2 2.3 %one_front.1.refs_0_ = bf16[240,384]{1,0:T(8,128)(2,1)S(1)} custom-call(s32[6]{0:T(128)S(1)} %stack.23.ids, bf16[256,384]{1,0:T(8,128)(2,1)S(1)} %zero_front.1.refs_0_, bf16[256,384]{1,0:T(8,128)(2,1)S(1)} %collective-permute-done.7.refs_1_, bf16[256,384]{1,0:T(8,128)(2,1)S(1)} %collective-permute-done.8.refs_2_, ...), custom_call_target="tpu_custom_call" | custom-call | flops 849346 | bytes 1024 | tf_op jit(solution)/shard_map/one_front/pallas_call | solution.py:327
  32.5 0.3 collective-permute-start.14
  32.8 1.1 %collective-permute-start.11 = (bf16[240,384]{1,0:T(8,128)(2,1)S(1)}, bf16[240,384]{1,0:T(8,128)(2,1)S(1)}, u32[]{:S(2)}, u32[]{:S(2)}) collective-permute-start(bf16[240,384]{1,0:T(8,128)(2,1)S(1)} %one_front.1.refs_0_), channel_id=1, source_target_pairs={{0,2},{1,3},{2,0},{3,1},{4,6},{5,7},{6,4},{7,5},{8,10},{9,11},{10,... | collective-permute-start | bytes 552968 | tf_op jit(solution)/shard_map/ppermute | solution.py:295
  34.1 2.7 %one_back.1.refs_4_ = bf16[304,384]{1,0:T(8,128)(2,1)S(1)} custom-call(s32[6]{0:T(128)S(1)} %stack.23.ids, bf16[256,384]{1,0:T(8,128)(2,1)S(1)} %zero_front.1.refs_0_, bf16[256,384]{1,0:T(8,128)(2,1)S(1)} %collective-permute-done.7.refs_1_, bf16[256,384]{1,0:T(8,128)(2,1)S(1)} %collective-permute-done.8.refs_2_, ...), custom_call_target="tpu_custom_call" | custom-call | flops 1075838 | bytes 1024 | tf_op jit(solution)/shard_map/one_back/pallas_call | solution.py:337
  36.9 1.3 %collective-permute-start.17 = (bf16[304,384]{1,0:T(8,128)(2,1)S(1)}, bf16[304,384]{1,0:T(8,128)(2,1)S(1)}, u32[]{:S(2)}, u32[]{:S(2)}) collective-permute-start(bf16[304,384]{1,0:T(8,128)(2,1)S(1)} %one_back.1.refs_4_), channel_id=1, source_target_pairs={{0,2},{1,3},{2,0},{3,1},{4,6},{5,7},{6,4},{7,5},{8,10},{9,11},{10,... | collective-permute-start | bytes 700424 | tf_op jit(solution)/shard_map/ppermute | solution.py:295
  38.2 2.6 %fetch.5.refs_5_.refs_9_ = bf16[3,1536,384]{2,1,0:T(8,128)(2,1)S(1)} custom-call(s32[6]{0:T(128)S(1)} %stack.23.ids, bf16[3,3,1536,384]{3,2,1,0:T(8,128)(2,1)} %w_hbm.5), custom_call_target="tpu_custom_call" | custom-call | flops 1000000000 | bytes 1024 | tf_op jit(solution)/shard_map/fetch/pallas_call | solution.py:263
  40.9 0.5 collective-permute-start.16
  41.4 0.9 collective-permute-done.15.refs_3_
  42.3 2.4 %two_front.1 = (bf16[208,384]{1,0:T(8,128)(2,1)S(1)}, f32[384,384]{1,0:T(8,128)S(1)}) custom-call(s32[6]{0:T(128)S(1)} %stack.23.ids, bf16[240,384]{1,0:T(8,128)(2,1)S(1)} %one_front.1.refs_0_, bf16[240,384]{1,0:T(8,128)(2,1)S(1)} %collective-permute-done.10.refs_1_, bf16[240,384]{1,0:T(8,128)(2,1)S(1)} %collective-permute-done.11.refs_2_, ...), custom_call_target="tpu_custom_call" | custom-call | flops 736100 | bytes 1024 | tf_op jit(solution)/shard_map/two_front/pallas_call | solution.py:350
  45.0 1.4 %collective-permute-done.18.refs_7_ = bf16[304,384]{1,0:T(8,128)(2,1)S(1)} collective-permute-done((bf16[304,384]{1,0:T(8,128)(2,1)S(1)}, bf16[304,384]{1,0:T(8,128)(2,1)S(1)}, u32[]{:S(2)}, u32[]{:S(2)}) %collective-permute-start.18) | collective-permute-done | bytes 233504 | tf_op jit(solution)/shard_map/ppermute | solution.py:300
  46.3 3.1 %two_back.1 = (bf16[304,384]{1,0:T(8,128)(2,1)S(1)}, f32[96,384]{1,0:T(8,128)S(1)}, bf16[96,384]{1,0:T(8,128)(2,1)S(1)}, bf16[96,384]{1,0:T(8,128)(2,1)S(1)}, bf16[96,384]{1,0:T(8,128)(2,1)S(1)}) custom-call(s32[6]{0:T(128)S(1)} %stack.23.ids, bf16[240,384]{1,0:T(8,128)(2,1)S(1)} %one_front.1.refs_0_, bf16[240,384]{1,0:T(8,128)(2,1)S(1)} %collective-permute-done.10.refs_1_, ...), custom_call_target="tpu_custom_call" | custom-call | flops 1075838 | bytes 1024 | tf_op jit(solution)/shard_map/two_back/pallas_call | solution.py:359
  49.5 1.8 %collective-permute-start.19 = (bf16[96,384]{1,0:T(8,128)(2,1)S(1)}, bf16[96,384]{1,0:T(8,128)(2,1)S(1)}, u32[]{:S(2)}, u32[]{:S(2)}) collective-permute-start(bf16[96,384]{1,0:T(8,128)(2,1)S(1)} %get-tuple-element.31), channel_id=1, source_target_pairs={{0,32},{1,5},{2,34},{3,7},{4,36},{5,1},{6,38},{7,3},{8,40},{9,13},... | collective-permute-start | bytes 221192 | tf_op jit(solution)/shard_map/ppermute | solution.py:402
  51.3 3.6 %collective-permute-start.20 = (bf16[96,384]{1,0:T(8,128)(2,1)S(1)}, bf16[96,384]{1,0:T(8,128)(2,1)S(1)}, u32[]{:S(2)}, u32[]{:S(2)}) collective-permute-start(bf16[96,384]{1,0:T(8,128)(2,1)S(1)} %get-tuple-element.32), channel_id=1, source_target_pairs={{0,4},{1,33},{2,6},{3,35},{4,0},{5,37},{6,2},{7,39},{8,12},{9,41},... | collective-permute-start | bytes 221192 | tf_op jit(solution)/shard_map/ppermute | solution.py:402
  54.9 2.8 %collective-permute-done.20 = bf16[96,384]{1,0:T(8,128)(2,1)S(1)} collective-permute-done((bf16[96,384]{1,0:T(8,128)(2,1)S(1)}, bf16[96,384]{1,0:T(8,128)(2,1)S(1)}, u32[]{:S(2)}, u32[]{:S(2)}) %collective-permute-start.20) | collective-permute-done | bytes 73760 | tf_op jit(solution)/shard_map/ppermute | solution.py:402
  57.7 2.4 %collective-permute-done.21 = bf16[96,384]{1,0:T(8,128)(2,1)S(1)} collective-permute-done((bf16[96,384]{1,0:T(8,128)(2,1)S(1)}, bf16[96,384]{1,0:T(8,128)(2,1)S(1)}, u32[]{:S(2)}, u32[]{:S(2)}) %collective-permute-start.21) | collective-permute-done | bytes 73760 | tf_op jit(solution)/shard_map/ppermute | solution.py:402
  60.2 4.3 %collective-permute-start.24 = (bf16[96,384]{1,0:T(8,128)(2,1)S(1)}, bf16[96,384]{1,0:T(8,128)(2,1)S(1)}, u32[]{:S(2)}, u32[]{:S(2)}) collective-permute-start(bf16[96,384]{1,0:T(8,128)(2,1)S(1)} %add_convert_fusion.3), channel_id=1, source_target_pairs={{0,124},{1,125},{2,126},{3,127},{4,104},{5,105},{6,106},{7,107},{8... | collective-permute-start | bytes 221192 | tf_op jit(solution)/shard_map/ppermute | solution.py:402
  64.4 1.1 %collective-permute-start.22 = (bf16[96,384]{1,0:T(8,128)(2,1)S(1)}, bf16[96,384]{1,0:T(8,128)(2,1)S(1)}, u32[]{:S(2)}, u32[]{:S(2)}) collective-permute-start(bf16[96,384]{1,0:T(8,128)(2,1)S(1)} %add_convert_fusion.3), channel_id=1, source_target_pairs={{0,96},{1,29},{2,98},{3,31},{4,100},{5,9},{6,102},{7,11},{8,104},{... | collective-permute-start | bytes 221192 | tf_op jit(solution)/shard_map/ppermute | solution.py:402
  65.6 1.2 %collective-permute-done.24 = bf16[96,384]{1,0:T(8,128)(2,1)S(1)} collective-permute-done((bf16[96,384]{1,0:T(8,128)(2,1)S(1)}, bf16[96,384]{1,0:T(8,128)(2,1)S(1)}, u32[]{:S(2)}, u32[]{:S(2)}) %collective-permute-start.24) | collective-permute-done | bytes 73760 | tf_op jit(solution)/shard_map/ppermute | solution.py:402
  66.8 2.0 %collective-permute-done.23 = bf16[96,384]{1,0:T(8,128)(2,1)S(1)} collective-permute-done((bf16[96,384]{1,0:T(8,128)(2,1)S(1)}, bf16[96,384]{1,0:T(8,128)(2,1)S(1)}, u32[]{:S(2)}, u32[]{:S(2)}) %collective-permute-start.23) | collective-permute-done | bytes 73760 | tf_op jit(solution)/shard_map/ppermute | solution.py:402
  68.8 1.2 %collective-permute-done.22 = bf16[96,384]{1,0:T(8,128)(2,1)S(1)} collective-permute-done((bf16[96,384]{1,0:T(8,128)(2,1)S(1)}, bf16[96,384]{1,0:T(8,128)(2,1)S(1)}, u32[]{:S(2)}, u32[]{:S(2)}) %collective-permute-start.22) | collective-permute-done | bytes 73760 | tf_op jit(solution)/shard_map/ppermute | solution.py:402
  70.1 2.9 %collective-permute-start.25 = (bf16[96,384]{1,0:T(8,128)(2,1)S(1)}, bf16[96,384]{1,0:T(8,128)(2,1)S(1)}, u32[]{:S(2)}, u32[]{:S(2)}) collective-permute-start(bf16[96,384]{1,0:T(8,128)(2,1)S(1)} %add_convert_fusion.2), channel_id=1, source_target_pairs={{0,12},{1,129},{2,14},{3,131},{4,24},{5,133},{6,26},{7,135},{8,20}... | collective-permute-start | bytes 221192 | tf_op jit(solution)/shard_map/ppermute | solution.py:402
  73.0 4.6 %collective-permute-done.25 = bf16[96,384]{1,0:T(8,128)(2,1)S(1)} collective-permute-done((bf16[96,384]{1,0:T(8,128)(2,1)S(1)}, bf16[96,384]{1,0:T(8,128)(2,1)S(1)}, u32[]{:S(2)}, u32[]{:S(2)}) %collective-permute-start.25) | collective-permute-done | bytes 73760 | tf_op jit(solution)/shard_map/ppermute | solution.py:402
  77.6 1.7 %collective-permute-start.26 = (bf16[96,384]{1,0:T(8,128)(2,1)S(1)}, bf16[96,384]{1,0:T(8,128)(2,1)S(1)}, u32[]{:S(2)}, u32[]{:S(2)}) collective-permute-start(bf16[96,384]{1,0:T(8,128)(2,1)S(1)} %add_convert_fusion.1), channel_id=1, source_target_pairs={{0,128},{1,13},{2,130},{3,15},{4,132},{5,25},{6,134},{7,27},{8,136... | collective-permute-start | bytes 221192 | tf_op jit(solution)/shard_map/ppermute | solution.py:402
  79.3 4.2 %collective-permute-done.26 = bf16[96,384]{1,0:T(8,128)(2,1)S(1)} collective-permute-done((bf16[96,384]{1,0:T(8,128)(2,1)S(1)}, bf16[96,384]{1,0:T(8,128)(2,1)S(1)}, u32[]{:S(2)}, u32[]{:S(2)}) %collective-permute-start.26) | collective-permute-done | bytes 73760 | tf_op jit(solution)/shard_map/ppermute | solution.py:402
  83.7 0.8 collective-permute-start.28
  84.5 2.6 %collective-permute-start.27 = (bf16[96,384]{1,0:T(8,128)(2,1)S(1)}, bf16[96,384]{1,0:T(8,128)(2,1)S(1)}, u32[]{:S(2)}, u32[]{:S(2)}) collective-permute-start(bf16[96,384]{1,0:T(8,128)(2,1)S(1)} %add_convert_fusion.p0), channel_id=1, source_target_pairs={{0,32},{1,5},{2,34},{3,7},{4,36},{5,1},{6,38},{7,3},{8,40},{9,13},... | collective-permute-start | bytes 221192 | tf_op jit(solution)/shard_map/ppermute | solution.py:402
  87.2 1.2 %decode.1 = bf16[512,384]{1,0:T(8,128)(2,1)} custom-call(bf16[208,384]{1,0:T(8,128)(2,1)S(1)} %get-tuple-element.26.front_rows, bf16[304,384]{1,0:T(8,128)(2,1)S(1)} %get-tuple-element.29.back_rows, bf16[384,384]{1,0:T(8,128)(2,1)S(1)} %copy-done.3), custom_call_target="tpu_custom_call" | custom-call | flops 150994 | bytes 1024 | tf_op jit(solution)/shard_map/decode/pallas_call | solution.py:368
  88.3 0.6 collective-permute-done.29.p3
  89.0 0.8 collective-permute-done.27.p1
  89.7 1.4 %assemble.1 = f32[384,384]{1,0:T(8,128)} custom-call(s32[6]{0:T(128)S(1)} %stack.23.ids, bf16[96,384]{1,0:T(8,128)(2,1)S(1)} %add_convert_fusion.p0, bf16[96,384]{1,0:T(8,128)(2,1)S(1)} %collective-permute-done.27.p1, bf16[96,384]{1,0:T(8,128)(2,1)S(1)} %collective-permute-done.28.p2, bf16[96,384]{1,0:T(8,128)(2,1)S(1)} %collective-permute-done.29.p3), custom_call_target="tpu_custom_call" | custom-call | bytes 1024 | tf_op jit(solution)/shard_map/assemble/pallas_call | solution.py:422
  (39 shorter events, 1.6 us)
Async XLA Ops:
  0.6 16.5 %collective-permute-start.1 = (bf16[512,384]{1,0:T(8,128)(2,1)}, bf16[512,384]{1,0:T(8,128)(2,1)S(1)}, u32[]{:S(2)}, u32[]{:S(2)}) collective-permute-start(bf16[512,384]{1,0:T(8,128)(2,1)} %param.7), channel_id=1, source_target_pairs={{0,1},{1,0},{2,3},{3,2},{4,5},{5,4},{6,7},{7,6},{8,9},{9,8},{10,11... | collective-permute-start | bytes 1179656 | tf_op jit(solution)/shard_map/ppermute | solution.py:260
  1.8 13.9 %collective-permute-start.2 = (bf16[256,384]{1,0:T(8,128)(2,1)S(1)}, bf16[256,384]{1,0:T(8,128)(2,1)S(1)}, u32[]{:S(2)}, u32[]{:S(2)}) collective-permute-start(bf16[256,384]{1,0:T(8,128)(2,1)S(1)} %get-tuple-element.18.own_a), channel_id=1, source_target_pairs={{0,2},{1,3},{2,0},{3,1},{4,6},{5,7},{6,4},{7,5},{8,10},{9,11},{10,... | collective-permute-start | bytes 589832 | tf_op jit(solution)/shard_map/ppermute | solution.py:258
  3.5 12.3 %collective-permute-start.4 = (bf16[256,384]{1,0:T(8,128)(2,1)S(1)}, bf16[256,384]{1,0:T(8,128)(2,1)S(1)}, u32[]{:S(2)}, u32[]{:S(2)}) collective-permute-start(bf16[256,384]{1,0:T(8,128)(2,1)S(1)} %get-tuple-element.19.own_b), channel_id=1, source_target_pairs={{0,130},{1,131},{2,128},{3,129},{128,2},{129,3},{130,0},{131,1},{4... | collective-permute-start | bytes 589832 | tf_op jit(solution)/shard_map/ppermute | solution.py:259
  6.4 8.9 %collective-permute-start = (s32[16,128]{1,0:T(8,128)S(1)}, s32[16,128]{1,0:T(8,128)S(1)}, u32[]{:S(2)}, u32[]{:S(2)}) collective-permute-start(s32[16,128]{1,0:T(8,128)S(1)} %bitcast.15), channel_id=1, source_target_pairs={{0,4},{4,8},{8,12},{12,16},{16,20},{20,24},{24,28},{28,32},{32,36}... | collective-permute-start | bytes 24584 | tf_op jit(solution)/shard_map/ppermute | solution.py:261
  10.2 5.5 %collective-permute-start.3 = (s32[16,128]{1,0:T(8,128)S(1)}, s32[16,128]{1,0:T(8,128)S(1)}, u32[]{:S(2)}, u32[]{:S(2)}) collective-permute-start(s32[16,128]{1,0:T(8,128)S(1)} %bitcast.14), channel_id=1, source_target_pairs={{4,0},{8,4},{12,8},{16,12},{20,16},{24,20},{28,24},{32,28},{36,32}... | collective-permute-start | bytes 24584 | tf_op jit(solution)/shard_map/ppermute | solution.py:279
  12.4 2.6 %copy-start.2 = (s32[1,65536]{1,0:T(1,128)S(1)}, s32[1,65536]{1,0:T(1,128)}, u32[]{:S(2)}) copy-start(s32[1,65536]{1,0:T(1,128)} %param.6) | copy-start | bytes 786436
  12.4 5.1 %copy-start.1 = (f32[3,1536]{1,0:T(4,128)S(1)}, f32[3,1536]{1,0:T(4,128)}, u32[]{:S(2)}) copy-start(f32[3,1536]{1,0:T(4,128)} %refs_8_.3) | copy-start | bytes 55300
  15.7 1.4 %collective-permute-start.6 = (bf16[256,384]{1,0:T(8,128)(2,1)S(1)}, bf16[256,384]{1,0:T(8,128)(2,1)S(1)}, u32[]{:S(2)}, u32[]{:S(2)}) collective-permute-start(bf16[256,384]{1,0:T(8,128)(2,1)S(1)} %collective-permute-done.4.w2b), channel_id=1, source_target_pairs={{0,1},{1,0},{2,3},{3,2},{4,5},{5,4},{6,7},{7,6},{8,9},{9,8},{10,11... | collective-permute-start | bytes 589832 | tf_op jit(solution)/shard_map/ppermute | solution.py:283
  15.7 1.7 %collective-permute-start.5 = (bf16[256,384]{1,0:T(8,128)(2,1)S(1)}, bf16[256,384]{1,0:T(8,128)(2,1)S(1)}, u32[]{:S(2)}, u32[]{:S(2)}) collective-permute-start(bf16[256,384]{1,0:T(8,128)(2,1)S(1)} %collective-permute-done.2.w2a), channel_id=1, source_target_pairs={{0,1},{1,0},{2,3},{3,2},{4,5},{5,4},{6,7},{7,6},{8,9},{9,8},{10,11... | collective-permute-start | bytes 589832 | tf_op jit(solution)/shard_map/ppermute | solution.py:282
  20.6 8.1 %collective-permute-start.8 = (bf16[256,384]{1,0:T(8,128)(2,1)S(1)}, bf16[256,384]{1,0:T(8,128)(2,1)S(1)}, u32[]{:S(2)}, u32[]{:S(2)}) collective-permute-start(bf16[256,384]{1,0:T(8,128)(2,1)S(1)} %zero_front.1.refs_0_), channel_id=1, source_target_pairs={{0,2},{1,3},{2,0},{3,1},{4,6},{5,7},{6,4},{7,5},{8,10},{9,11},{10,... | collective-permute-start | bytes 589832 | tf_op jit(solution)/shard_map/ppermute | solution.py:295
  21.3 7.9 %collective-permute-start.7 = (bf16[256,384]{1,0:T(8,128)(2,1)S(1)}, bf16[256,384]{1,0:T(8,128)(2,1)S(1)}, u32[]{:S(2)}, u32[]{:S(2)}) collective-permute-start(bf16[256,384]{1,0:T(8,128)(2,1)S(1)} %zero_front.1.refs_0_), channel_id=1, source_target_pairs={{0,1},{1,0},{2,3},{3,2},{4,5},{5,4},{6,7},{7,6},{8,9},{9,8},{10,11... | collective-permute-start | bytes 589832 | tf_op jit(solution)/shard_map/ppermute | solution.py:295
  24.6 7.9 %collective-permute-start.13 = (bf16[288,384]{1,0:T(8,128)(2,1)S(1)}, bf16[288,384]{1,0:T(8,128)(2,1)S(1)}, u32[]{:S(2)}, u32[]{:S(2)}) collective-permute-start(bf16[288,384]{1,0:T(8,128)(2,1)S(1)} %zero_back.1.refs_4_), channel_id=1, source_target_pairs={{0,2},{1,3},{2,0},{3,1},{4,6},{5,7},{6,4},{7,5},{8,10},{9,11},{10,... | collective-permute-start | bytes 663560 | tf_op jit(solution)/shard_map/ppermute | solution.py:295
  28.7 1.5 %collective-permute-start.9 = (bf16[256,384]{1,0:T(8,128)(2,1)S(1)}, bf16[256,384]{1,0:T(8,128)(2,1)S(1)}, u32[]{:S(2)}, u32[]{:S(2)}) collective-permute-start(bf16[256,384]{1,0:T(8,128)(2,1)S(1)} %collective-permute-done.8.refs_2_), channel_id=1, source_target_pairs={{0,1},{1,0},{2,3},{3,2},{4,5},{5,4},{6,7},{7,6},{8,9},{9,8},{10,11... | collective-permute-start | bytes 589832 | tf_op jit(solution)/shard_map/ppermute | solution.py:300
  29.0 5.2 %collective-permute-start.12 = (bf16[288,384]{1,0:T(8,128)(2,1)S(1)}, bf16[288,384]{1,0:T(8,128)(2,1)S(1)}, u32[]{:S(2)}, u32[]{:S(2)}) collective-permute-start(bf16[288,384]{1,0:T(8,128)(2,1)S(1)} %zero_back.1.refs_4_), channel_id=1, source_target_pairs={{0,1},{1,0},{2,3},{3,2},{4,5},{5,4},{6,7},{7,6},{8,9},{9,8},{10,11... | collective-permute-start | bytes 663560 | tf_op jit(solution)/shard_map/ppermute | solution.py:295
  32.5 1.6 %collective-permute-start.14 = (bf16[288,384]{1,0:T(8,128)(2,1)S(1)}, bf16[288,384]{1,0:T(8,128)(2,1)S(1)}, u32[]{:S(2)}, u32[]{:S(2)}) collective-permute-start(bf16[288,384]{1,0:T(8,128)(2,1)S(1)} %collective-permute-done.13.refs_6_), channel_id=1, source_target_pairs={{0,1},{1,0},{2,3},{3,2},{4,5},{5,4},{6,7},{7,6},{8,9},{9,8},{10,11... | collective-permute-start | bytes 663560 | tf_op jit(solution)/shard_map/ppermute | solution.py:300
  32.8 7.9 %collective-permute-start.11 = (bf16[240,384]{1,0:T(8,128)(2,1)S(1)}, bf16[240,384]{1,0:T(8,128)(2,1)S(1)}, u32[]{:S(2)}, u32[]{:S(2)}) collective-permute-start(bf16[240,384]{1,0:T(8,128)(2,1)S(1)} %one_front.1.refs_0_), channel_id=1, source_target_pairs={{0,2},{1,3},{2,0},{3,1},{4,6},{5,7},{6,4},{7,5},{8,10},{9,11},{10,... | collective-permute-start | bytes 552968 | tf_op jit(solution)/shard_map/ppermute | solution.py:295
  33.9 7.5 %collective-permute-start.10 = (bf16[240,384]{1,0:T(8,128)(2,1)S(1)}, bf16[240,384]{1,0:T(8,128)(2,1)S(1)}, u32[]{:S(2)}, u32[]{:S(2)}) collective-permute-start(bf16[240,384]{1,0:T(8,128)(2,1)S(1)} %one_front.1.refs_0_), channel_id=1, source_target_pairs={{0,1},{1,0},{2,3},{3,2},{4,5},{5,4},{6,7},{7,6},{8,9},{9,8},{10,11... | collective-permute-start | bytes 552968 | tf_op jit(solution)/shard_map/ppermute | solution.py:295
  36.8 5.5 %copy-start = (bf16[1,512,384]{2,1,0:T(8,128)(2,1)S(1)}, bf16[1,512,384]{2,1,0:T(8,128)(2,1)}, u32[]{:S(2)}) copy-start(bf16[1,512,384]{2,1,0:T(8,128)(2,1)} %param.11) | copy-start | bytes 1179652
  36.9 8.0 %collective-permute-start.17 = (bf16[304,384]{1,0:T(8,128)(2,1)S(1)}, bf16[304,384]{1,0:T(8,128)(2,1)S(1)}, u32[]{:S(2)}, u32[]{:S(2)}) collective-permute-start(bf16[304,384]{1,0:T(8,128)(2,1)S(1)} %one_back.1.refs_4_), channel_id=1, source_target_pairs={{0,2},{1,3},{2,0},{3,1},{4,6},{5,7},{6,4},{7,5},{8,10},{9,11},{10,... | collective-permute-start | bytes 700424 | tf_op jit(solution)/shard_map/ppermute | solution.py:295
  40.8 1.5 %collective-permute-start.15 = (bf16[240,384]{1,0:T(8,128)(2,1)S(1)}, bf16[240,384]{1,0:T(8,128)(2,1)S(1)}, u32[]{:S(2)}, u32[]{:S(2)}) collective-permute-start(bf16[240,384]{1,0:T(8,128)(2,1)S(1)} %collective-permute-done.11.refs_2_), channel_id=1, source_target_pairs={{0,1},{1,0},{2,3},{3,2},{4,5},{5,4},{6,7},{7,6},{8,9},{9,8},{10,11... | collective-permute-start | bytes 552968 | tf_op jit(solution)/shard_map/ppermute | solution.py:300
  40.9 4.1 %collective-permute-start.16 = (bf16[304,384]{1,0:T(8,128)(2,1)S(1)}, bf16[304,384]{1,0:T(8,128)(2,1)S(1)}, u32[]{:S(2)}, u32[]{:S(2)}) collective-permute-start(bf16[304,384]{1,0:T(8,128)(2,1)S(1)} %one_back.1.refs_4_), channel_id=1, source_target_pairs={{0,1},{1,0},{2,3},{3,2},{4,5},{5,4},{6,7},{7,6},{8,9},{9,8},{10,11... | collective-permute-start | bytes 700424 | tf_op jit(solution)/shard_map/ppermute | solution.py:295
  44.8 1.5 %collective-permute-start.18 = (bf16[304,384]{1,0:T(8,128)(2,1)S(1)}, bf16[304,384]{1,0:T(8,128)(2,1)S(1)}, u32[]{:S(2)}, u32[]{:S(2)}) collective-permute-start(bf16[304,384]{1,0:T(8,128)(2,1)S(1)} %collective-permute-done.17.refs_6_), channel_id=1, source_target_pairs={{0,1},{1,0},{2,3},{3,2},{4,5},{5,4},{6,7},{7,6},{8,9},{9,8},{10,11... | collective-permute-start | bytes 700424 | tf_op jit(solution)/shard_map/ppermute | solution.py:300
  46.3 40.9 %copy-start.3 = (bf16[384,384]{1,0:T(8,128)(2,1)S(1)}, bf16[384,384]{1,0:T(8,128)(2,1)}, u32[]{:S(2)}) copy-start(bf16[384,384]{1,0:T(8,128)(2,1)} %weights.1) | copy-start | bytes 884740
  49.5 5.4 %collective-permute-start.19 = (bf16[96,384]{1,0:T(8,128)(2,1)S(1)}, bf16[96,384]{1,0:T(8,128)(2,1)S(1)}, u32[]{:S(2)}, u32[]{:S(2)}) collective-permute-start(bf16[96,384]{1,0:T(8,128)(2,1)S(1)} %get-tuple-element.31), channel_id=1, source_target_pairs={{0,32},{1,5},{2,34},{3,7},{4,36},{5,1},{6,38},{7,3},{8,40},{9,13},... | collective-permute-start | bytes 221192 | tf_op jit(solution)/shard_map/ppermute | solution.py:402
  51.3 6.5 %collective-permute-start.20 = (bf16[96,384]{1,0:T(8,128)(2,1)S(1)}, bf16[96,384]{1,0:T(8,128)(2,1)S(1)}, u32[]{:S(2)}, u32[]{:S(2)}) collective-permute-start(bf16[96,384]{1,0:T(8,128)(2,1)S(1)} %get-tuple-element.32), channel_id=1, source_target_pairs={{0,4},{1,33},{2,6},{3,35},{4,0},{5,37},{6,2},{7,39},{8,12},{9,41},... | collective-permute-start | bytes 221192 | tf_op jit(solution)/shard_map/ppermute | solution.py:402
  54.9 5.3 %collective-permute-start.21 = (bf16[96,384]{1,0:T(8,128)(2,1)S(1)}, bf16[96,384]{1,0:T(8,128)(2,1)S(1)}, u32[]{:S(2)}, u32[]{:S(2)}) collective-permute-start(bf16[96,384]{1,0:T(8,128)(2,1)S(1)} %get-tuple-element.33), channel_id=1, source_target_pairs={{0,36},{1,37},{2,38},{3,39},{4,32},{5,33},{6,34},{7,35},{8,44},{9,... | collective-permute-start | bytes 221192 | tf_op jit(solution)/shard_map/ppermute | solution.py:402
  60.2 6.6 %collective-permute-start.24 = (bf16[96,384]{1,0:T(8,128)(2,1)S(1)}, bf16[96,384]{1,0:T(8,128)(2,1)S(1)}, u32[]{:S(2)}, u32[]{:S(2)}) collective-permute-start(bf16[96,384]{1,0:T(8,128)(2,1)S(1)} %add_convert_fusion.3), channel_id=1, source_target_pairs={{0,124},{1,125},{2,126},{3,127},{4,104},{5,105},{6,106},{7,107},{8... | collective-permute-start | bytes 221192 | tf_op jit(solution)/shard_map/ppermute | solution.py:402
  64.4 4.4 %collective-permute-start.23 = (bf16[96,384]{1,0:T(8,128)(2,1)S(1)}, bf16[96,384]{1,0:T(8,128)(2,1)S(1)}, u32[]{:S(2)}, u32[]{:S(2)}) collective-permute-start(bf16[96,384]{1,0:T(8,128)(2,1)S(1)} %add_convert_fusion.3), channel_id=1, source_target_pairs={{0,28},{1,97},{2,30},{3,99},{4,8},{5,101},{6,10},{7,103},{8,4},{9,... | collective-permute-start | bytes 221192 | tf_op jit(solution)/shard_map/ppermute | solution.py:402
  64.4 5.6 %collective-permute-start.22 = (bf16[96,384]{1,0:T(8,128)(2,1)S(1)}, bf16[96,384]{1,0:T(8,128)(2,1)S(1)}, u32[]{:S(2)}, u32[]{:S(2)}) collective-permute-start(bf16[96,384]{1,0:T(8,128)(2,1)S(1)} %add_convert_fusion.3), channel_id=1, source_target_pairs={{0,96},{1,29},{2,98},{3,31},{4,100},{5,9},{6,102},{7,11},{8,104},{... | collective-permute-start | bytes 221192 | tf_op jit(solution)/shard_map/ppermute | solution.py:402
  70.1 7.5 %collective-permute-start.25 = (bf16[96,384]{1,0:T(8,128)(2,1)S(1)}, bf16[96,384]{1,0:T(8,128)(2,1)S(1)}, u32[]{:S(2)}, u32[]{:S(2)}) collective-permute-start(bf16[96,384]{1,0:T(8,128)(2,1)S(1)} %add_convert_fusion.2), channel_id=1, source_target_pairs={{0,12},{1,129},{2,14},{3,131},{4,24},{5,133},{6,26},{7,135},{8,20}... | collective-permute-start | bytes 221192 | tf_op jit(solution)/shard_map/ppermute | solution.py:402
  77.6 5.9 %collective-permute-start.26 = (bf16[96,384]{1,0:T(8,128)(2,1)S(1)}, bf16[96,384]{1,0:T(8,128)(2,1)S(1)}, u32[]{:S(2)}, u32[]{:S(2)}) collective-permute-start(bf16[96,384]{1,0:T(8,128)(2,1)S(1)} %add_convert_fusion.1), channel_id=1, source_target_pairs={{0,128},{1,13},{2,130},{3,15},{4,132},{5,25},{6,134},{7,27},{8,136... | collective-permute-start | bytes 221192 | tf_op jit(solution)/shard_map/ppermute | solution.py:402
  83.6 5.4 %collective-permute-start.29 = (bf16[96,384]{1,0:T(8,128)(2,1)S(1)}, bf16[96,384]{1,0:T(8,128)(2,1)S(1)}, u32[]{:S(2)}, u32[]{:S(2)}) collective-permute-start(bf16[96,384]{1,0:T(8,128)(2,1)S(1)} %add_convert_fusion.p0), channel_id=1, source_target_pairs={{0,36},{1,37},{2,38},{3,39},{4,32},{5,33},{6,34},{7,35},{8,44},{9,... | collective-permute-start | bytes 221192 | tf_op jit(solution)/shard_map/ppermute | solution.py:402
  83.7 5.3 %collective-permute-start.28 = (bf16[96,384]{1,0:T(8,128)(2,1)S(1)}, bf16[96,384]{1,0:T(8,128)(2,1)S(1)}, u32[]{:S(2)}, u32[]{:S(2)}) collective-permute-start(bf16[96,384]{1,0:T(8,128)(2,1)S(1)} %add_convert_fusion.p0), channel_id=1, source_target_pairs={{0,4},{1,33},{2,6},{3,35},{4,0},{5,37},{6,2},{7,39},{8,12},{9,41},... | collective-permute-start | bytes 221192 | tf_op jit(solution)/shard_map/ppermute | solution.py:402
  84.5 5.2 %collective-permute-start.27 = (bf16[96,384]{1,0:T(8,128)(2,1)S(1)}, bf16[96,384]{1,0:T(8,128)(2,1)S(1)}, u32[]{:S(2)}, u32[]{:S(2)}) collective-permute-start(bf16[96,384]{1,0:T(8,128)(2,1)S(1)} %add_convert_fusion.p0), channel_id=1, source_target_pairs={{0,32},{1,5},{2,34},{3,7},{4,36},{5,1},{6,38},{7,3},{8,40},{9,13},... | collective-permute-start | bytes 221192 | tf_op jit(solution)/shard_map/ppermute | solution.py:402
